TPU v7x, 32 devices: a whole 2x2x4 slice. The times are simulated.
32 devices in a mesh: tm: 32 (over z, y, x, core).
Axes of the slice: x: 2, y: 2, z: 4, core: 2. Of those that a mesh axis runs over, the one named last changes fastest.
Arguments:
- signal: bfloat16 [8192, 512], P('tm'), may hold values from -18 to 18
- conv_weight: bfloat16 [1024, 2048], replicated
- attn_gain: float32 [2048], replicated, may hold values from 0.1 to 1.9
- w_query: bfloat16 [2048, 1024], replicated, may hold values from -0.125 to 0.125
- w_keyval: bfloat16 [2048, 512], replicated, may hold values from -0.125 to 0.125
- w_out: bfloat16 [1024, 2048], replicated, may hold values from -0.1875 to 0.1875
- head_scale: float32 [8], replicated, as said below
- ffn_gain: float32 [2048], replicated, may hold values from 0.1 to 1.9
- router_w: bfloat16 [2048, 64], replicated, may hold values from -0.125 to 0.125
- expert_in: bfloat16 [2, 90112, 2048], P(None, 'tm'), may hold values from -0.125 to 0.125
- expert_out: bfloat16 [90112, 2048], P('tm'), may hold values from -0.15625 to 0.15625
- expert_ids: int32 [8192, 2], P('tm'), may hold values from 0 to 63, as said below
- slot_ids: int32 [8192, 2], P('tm'), may hold values from 0 to 15, as said below
Outputs:
- layer_output: bfloat16 [8192, 2048], P('tm')
Inputs may be any that keep to these rules, and one draw needn't show every extreme that they name: `head_scale`: each head's scale lies between 0.5 and 64. `expert_ids`: the two experts of a token differ. Among the 256 tokens of one device no expert is named more than 16 times, and some expert is named exactly 16 times by the tokens of every device. `slot_ids`: routes of one device's tokens that name the same expert have different slots.
All inputs are finite; a program needn't handle non-finite values.
Results may differ from a plain program's by a relative error of at most 0.019.
Values may be sent and summed in bfloat16 or wider, within the bound.
No kernel may reach another device: no remote copies, remote signals or barrier semaphores. Data moves between devices by JAX's collectives and lax.ppermute only.
A program may use at most 192 MiB of HBM per device.

v0:
```python
import functools
import math

import jax
import jax.numpy as jnp
from jax import lax
from jax.experimental import pallas as pl
from jax.experimental.pallas import tpu as pltpu
from jax.sharding import PartitionSpec as P

HEAD_DIM = 128
WINDOW = 2048
CAP = 16

NORM_EPS = 1e-06
MASKED = -1e30


def from_behind(block, axis, distance):
    devices = range(lax.axis_size(axis))
    route = [(i - distance, i) for i in devices if i - distance in devices]
    return lax.ppermute(block, axis, route)


def rms_scale(values, gain_vec):
    mean_sq = jnp.mean(values * values, axis=-1, keepdims=True)
    return values * lax.rsqrt(mean_sq + NORM_EPS) * gain_vec


def head_norm(values):
    mean_sq = jnp.mean(values * values, axis=-1, keepdims=True)
    return values * lax.rsqrt(mean_sq + NORM_EPS)


def expert_body(steps, rows_ref, w_in_ref, w_out_ref, out_ref, total_ref):
    step = pl.program_id(1)
    width = w_in_ref.shape[1]
    rows = rows_ref[...]
    nt = (((1,), (1,)), ((), ()))
    gate = lax.dot_general(rows, w_in_ref[0], nt, preferred_element_type=jnp.float32)
    up = lax.dot_general(rows, w_in_ref[1], nt, preferred_element_type=jnp.float32)
    hidden = (gate / (1.0 + jnp.exp(-gate)) * up).astype(jnp.bfloat16)
    part = jnp.dot(hidden, w_out_ref[...], preferred_element_type=jnp.float32)

    @pl.when(step == 0)
    def _():
        total_ref[...] = part

    @pl.when(step > 0)
    def _():
        total_ref[...] += part

    @pl.when(step == steps - 1)
    def _():
        out_ref[...] = total_ref[...].astype(out_ref.dtype)


def run_expert(rows, expert_in, expert_out, local, local_count):
    row_total, feat_dim = rows.shape
    units = expert_out.shape[0] // local_count
    width = 352
    steps = units // width
    first = local * steps
    tile = math.gcd(row_total, 512)
    flops = 6 * row_total * units * feat_dim
    return pl.pallas_call(
        functools.partial(expert_body, steps),
        grid=(row_total // tile, steps),
        in_specs=[
            pl.BlockSpec((tile, feat_dim), lambda r, i: (r, 0)),
            pl.BlockSpec((2, width, feat_dim), lambda r, i: (0, first + i, 0)),
            pl.BlockSpec((width, feat_dim), lambda r, i: (first + i, 0)),
        ],
        out_specs=pl.BlockSpec((tile, feat_dim), lambda r, i: (r, 0)),
        out_shape=jax.ShapeDtypeStruct((row_total, feat_dim), jnp.bfloat16),
        scratch_shapes=[pltpu.VMEM((tile, feat_dim), jnp.float32)],
        compiler_params=pltpu.CompilerParams(vmem_limit_bytes=40 << 20),
        cost_estimate=pl.CostEstimate(
            flops=flops,
            bytes_accessed=6 * units * feat_dim + 4 * row_total * feat_dim,
            transcendentals=row_total * units,
        ),
    )(rows, expert_in, expert_out)


def shards(
    signal,
    conv_weight,
    attn_gain,
    w_query,
    w_keyval,
    w_out,
    head_scale,
    ffn_gain,
    router_w,
    expert_in,
    expert_out,
    expert_ids,
    slot_ids,
):
    row_count = signal.shape[0]
    feat_dim = conv_weight.shape[1]
    devices = lax.axis_size("tm")
    dev_index = lax.axis_index("tm")
    experts = router_w.shape[1]
    copies = max(devices // experts, 1)
    local_count = max(experts // devices, 1)
    slots = devices * CAP

    route_key = expert_ids * CAP + slot_ids
    row_id = jnp.arange(slots, dtype=jnp.int32)
    row_dev, row_slot = row_id // CAP, row_id % CAP
    row_keys = [
        (row_dev // copies * local_count + local) * CAP + row_slot for local in range(local_count)
    ]

    def spread(values, local):
        hot = (row_keys[local][:, None] == route_key[None, :, 0]) | (
            row_keys[local][:, None] == route_key[None, :, 1]
        )
        return jnp.dot(
            hot.astype(jnp.bfloat16), values, preferred_element_type=jnp.float32
        ).astype(jnp.bfloat16)

    def exchange(rows):
        return lax.all_to_all(rows, "tm", split_axis=0, concat_axis=0, tiled=True)

    before = from_behind(signal[row_count - 1 :], "tm", 1)
    previous = jnp.concatenate([before, signal[:-1]], axis=0)
    patch_pairs = jnp.concatenate([previous, signal], axis=1)
    pairs_out = jnp.concatenate(
        [spread(patch_pairs, local).reshape(devices, CAP, -1) for local in range(local_count)],
        axis=1,
    )
    pairs_in = exchange(pairs_out)

    embedded = jnp.dot(patch_pairs, conv_weight, preferred_element_type=jnp.float32).astype(
        jnp.bfloat16
    )
    normed = rms_scale(embedded.astype(jnp.float32), attn_gain).astype(jnp.bfloat16)
    head_count = head_scale.shape[0]
    kv_dim = w_keyval.shape[1] // 2
    kv_heads = kv_dim // HEAD_DIM
    group_size = head_count // kv_heads
    keyval = jnp.dot(normed, w_keyval, preferred_element_type=jnp.float32).reshape(
        row_count, 2, kv_heads, HEAD_DIM
    )
    key_unit = head_norm(keyval[:, 0]).astype(jnp.bfloat16)
    value_bf = keyval[:, 1].astype(jnp.bfloat16)
    own_kv = jnp.concatenate(
        [key_unit.reshape(row_count, kv_dim), value_bf.reshape(row_count, kv_dim)], axis=1
    )
    reach_blocks = WINDOW // row_count
    earlier = [from_behind(own_kv, "tm", distance) for distance in range(reach_blocks, 0, -1)]
    queries = jnp.dot(normed, w_query, preferred_element_type=jnp.float32).reshape(
        row_count, kv_heads, group_size, HEAD_DIM
    )
    query_unit = head_norm(queries).astype(jnp.bfloat16)
    window_kv = jnp.concatenate(earlier + [own_kv], axis=0)
    key_len = window_kv.shape[0]
    win_keys = window_kv[:, :kv_dim].reshape(key_len, kv_heads, HEAD_DIM)
    win_values = window_kv[:, kv_dim:].reshape(key_len, kv_heads, HEAD_DIM)
    scores = jnp.einsum("qkgd,lkd->kgql", query_unit, win_keys, preferred_element_type=jnp.float32)
    scores = scores * (head_scale.reshape(kv_heads, group_size, 1, 1) / math.sqrt(HEAD_DIM))
    query_pos = dev_index * row_count + jnp.arange(row_count, dtype=jnp.int32)
    key_pos = (dev_index - reach_blocks) * row_count + jnp.arange(key_len, dtype=jnp.int32)
    visible = (
        (key_pos[None, :] <= query_pos[:, None])
        & (key_pos[None, :] > query_pos[:, None] - WINDOW)
        & (key_pos[None, :] >= 0)
    )
    scores = jnp.where(visible, scores, MASKED)
    row_max = jnp.max(scores, axis=-1, keepdims=True)
    exp_scores = jnp.exp(scores - row_max)
    probs = (exp_scores / jnp.sum(exp_scores, axis=-1, keepdims=True)).astype(jnp.bfloat16)
    context = jnp.einsum("kgql,lkd->qkgd", probs, win_values, preferred_element_type=jnp.float32)
    context = context.astype(jnp.bfloat16).reshape(row_count, head_count * HEAD_DIM)

    context_in = [
        exchange(spread(context, local).reshape(devices, CAP, -1)) for local in range(local_count)
    ]

    def rows_of(pairs, contexts):
        placed = jnp.dot(pairs, conv_weight, preferred_element_type=jnp.float32).astype(
            jnp.bfloat16
        )
        mid = (
            placed.astype(jnp.float32)
            + jnp.dot(contexts, w_out, preferred_element_type=jnp.float32)
        ).astype(jnp.bfloat16)
        return mid, rms_scale(mid.astype(jnp.float32), ffn_gain).astype(jnp.bfloat16)

    returned = []
    for local in range(local_count):
        pairs = pairs_in[:, local * CAP : (local + 1) * CAP].reshape(slots, -1)
        _, rows = rows_of(pairs, context_in[local].reshape(slots, -1))
        result = run_expert(rows, expert_in, expert_out, local, local_count)
        returned.append(exchange(result.reshape(devices, CAP, feat_dim)).reshape(slots, feat_dim))

    stream_mid = (
        embedded.astype(jnp.float32) + jnp.dot(context, w_out, preferred_element_type=jnp.float32)
    ).astype(jnp.bfloat16)
    ffn_input = rms_scale(stream_mid.astype(jnp.float32), ffn_gain).astype(jnp.bfloat16)
    affinity = jax.nn.sigmoid(jnp.dot(ffn_input, router_w, preferred_element_type=jnp.float32))
    chosen_hot = expert_ids[:, :, None] == jnp.arange(experts, dtype=jnp.int32)[None, None, :]
    picked = jnp.sum(jnp.where(chosen_hot, affinity[:, None, :], 0.0), axis=-1)
    route_weight = picked / jnp.sum(picked, axis=1, keepdims=True)

    mixed = stream_mid.astype(jnp.float32)
    for local in range(local_count):
        for route in range(2):
            hot = route_key[:, route][:, None] == row_keys[local][None, :]
            gathered = jnp.dot(
                hot.astype(jnp.bfloat16), returned[local], preferred_element_type=jnp.float32
            ).astype(jnp.bfloat16)
            mixed = mixed + route_weight[:, route : route + 1] * gathered.astype(jnp.float32)
    return mixed.astype(jnp.bfloat16)


def solution(mesh):
    placed = (
        P("tm", None),
        P(),
        P(),
        P(),
        P(),
        P(),
        P(),
        P(),
        P(),
        P(None, "tm", None),
        P("tm", None),
        P("tm", None),
        P("tm", None),
    )
    return jax.shard_map(
        shards, mesh=mesh, in_specs=placed, out_specs=P("tm", None), check_vma=False
    )
```

profile of v0, /device:TPU:0, one launch (start us, length us, event | category | flops | bytes accessed | tf_op | source)
XLA Modules:
  0.0 330.4 jit_solution(14062773345679661061)
XLA Ops:
  4.6 2.4 and_and_fusion
  7.1 3.7 %fusion.27 = (f32[256]{0:T(256)S(1)}, bf16[256,2048]{1,0:T(8,128)(2,1)S(1)}) fusion(bf16[1024,2048]{1,0:T(8,128)(2,1)} %param.14, bf16[256,512]{1,0:T(8,128)(2,1)} %param.13, bf16[255,512]{1,0:T(8,128)(2,1)} %bitcast.103, bf16[1,512]{1,0:T(2,128)(2,1)S(1)} %collective-permute-done), kind=kOutput, calls=%fused_computation.49 | convolution fusion | flops 1077411584 | bytes 5768192 | tf_op jit(solution)/shard_map/dot_general | solution.py:137
  13.8 6.1 %collective-permute-start.1 = (bf16[256,512]{0,1:T(8,128)(2,1)S(1)}, bf16[256,512]{0,1:T(8,128)(2,1)}, u32[]{:S(2)}, u32[]{:S(2)}) collective-permute-start(bf16[256,512]{0,1:T(8,128)(2,1)S(1)} %pad_maximum_fusion.2), channel_id=1, source_target_pairs={{0,8},{1,9},{2,10},{3,11},{4,12},{5,13},{6,14},{7,15},{8,16},{9,17... | collective-permute-start | bytes 786440 | tf_op jit(solution)/shard_map/ppermute | solution.py:22
  19.9 5.1 %collective-permute-start.2 = (bf16[256,512]{0,1:T(8,128)(2,1)S(1)}, bf16[256,512]{0,1:T(8,128)(2,1)}, u32[]{:S(2)}, u32[]{:S(2)}) collective-permute-start(bf16[256,512]{0,1:T(8,128)(2,1)S(1)} %pad_maximum_fusion.2), channel_id=1, source_target_pairs={{0,7},{1,8},{2,9},{3,10},{4,11},{5,12},{6,13},{7,14},{8,15},{9,16}... | collective-permute-start | bytes 786440 | tf_op jit(solution)/shard_map/ppermute | solution.py:22
  25.0 2.8 collective-permute-start.3
  29.1 3.4 %collective-permute-start.5 = (bf16[256,512]{0,1:T(8,128)(2,1)S(1)}, bf16[256,512]{0,1:T(8,128)(2,1)S(1)}, u32[]{:S(2)}, u32[]{:S(2)}) collective-permute-start(bf16[256,512]{0,1:T(8,128)(2,1)S(1)} %pad_maximum_fusion.2), channel_id=1, source_target_pairs={{0,4},{1,5},{2,6},{3,7},{4,8},{5,9},{6,10},{7,11},{8,12},{9,13},{1... | collective-permute-start | bytes 786440 | tf_op jit(solution)/shard_map/ppermute | solution.py:22
  32.5 3.8 %fusion.51 = f32[256,1024]{1,0:T(8,128)S(1)} fusion(bf16[2048,1024]{1,0:T(8,128)(2,1)} %param.16, bf16[256,2048]{1,0:T(8,128)(2,1)} %copy-done.20, f32[2048]{0:T(1024)S(1)} %copy-done.19, f32[256]{0:T(256)S(1)} %add_rsqrt_fusion.5), kind=kOutput, calls=%fused_computation.79 | convolution fusion | flops 1075838976 | bytes 6300672 | tf_op jit(solution)/shard_map/dot_general | solution.py:155
  42.0 2.7 all-to-all-start
  44.8 3.3 %collective-permute-start.6 = (bf16[256,512]{0,1:T(8,128)(2,1)S(1)}, bf16[256,512]{0,1:T(8,128)(2,1)S(1)}, u32[]{:S(2)}, u32[]{:S(2)}) collective-permute-start(bf16[256,512]{0,1:T(8,128)(2,1)S(1)} %pad_maximum_fusion.2), channel_id=1, source_target_pairs={{0,3},{1,4},{2,5},{3,6},{4,7},{5,8},{6,9},{7,10},{8,11},{9,12},{10... | collective-permute-start | bytes 786440 | tf_op jit(solution)/shard_map/ppermute | solution.py:22
  49.1 3.4 %collective-permute-start.7 = (bf16[256,512]{0,1:T(8,128)(2,1)S(1)}, bf16[256,512]{0,1:T(8,128)(2,1)S(1)}, u32[]{:S(2)}, u32[]{:S(2)}) collective-permute-start(bf16[256,512]{0,1:T(8,128)(2,1)S(1)} %pad_maximum_fusion.2), channel_id=1, source_target_pairs={{0,2},{1,3},{2,4},{3,5},{4,6},{5,7},{6,8},{7,9},{8,10},{9,11},{10,... | collective-permute-start | bytes 786440 | tf_op jit(solution)/shard_map/ppermute | solution.py:22
  55.8 13.0 %collective-permute-done.6 = bf16[256,512]{0,1:T(8,128)(2,1)S(1)} collective-permute-done((bf16[256,512]{0,1:T(8,128)(2,1)S(1)}, bf16[256,512]{0,1:T(8,128)(2,1)S(1)}, u32[]{:S(2)}, u32[]{:S(2)}) %collective-permute-start.6) | collective-permute-done | bytes 262176 | tf_op jit(solution)/shard_map/ppermute | solution.py:22
  68.8 7.4 %collective-permute-done.7 = bf16[256,512]{0,1:T(8,128)(2,1)S(1)} collective-permute-done((bf16[256,512]{0,1:T(8,128)(2,1)S(1)}, bf16[256,512]{0,1:T(8,128)(2,1)S(1)}, u32[]{:S(2)}, u32[]{:S(2)}) %collective-permute-start.7) | collective-permute-done | bytes 262176 | tf_op jit(solution)/shard_map/ppermute | solution.py:22
  77.5 11.8 %fusion.94 = (f32[2,4,256]{2,1,0:T(4,128)S(1)}, f32[2,4,256,2304]{2,3,1,0:T(8,128)}) fusion(bf16[2304,2,128,1]{0,2,3,1:T(8,128)(2,1)S(1)} %bitcast.79, f32[2,4]{1,0:T(2,128)S(1)} %div.80, pred[256,2304]{0,1:T(8,128)(4,1)} %and_and_fusion, bf16[256,2,4,128]{3,2,1,0:T(4,128)(2,1)} %multiply_convert_fusion), kind=kOutput, calls=%fused_computation.153 | convolution fusion | flops 1226836224 | bytes 21176352 | tf_op jit(solution)/shard_map/sub | solution.py:174
  89.4 8.1 %fusion.33 = bf16[2,128,4,256]{3,1,2,0:T(8,128)(2,1)S(1)} fusion(bf16[2304,2,128,1]{0,2,3,1:T(8,128)(2,1)} %bitcast.78, f32[2,4,256,2304]{2,3,1,0:T(8,128)} %get-tuple-element.22, f32[2,4,256]{2,1,0:T(4,128)S(1)} %get-tuple-element.21), kind=kOutput, calls=%fused_computation.60 | convolution fusion | flops 1217658880 | bytes 20586496 | tf_op jit(solution)/shard_map/kgql,lkd->qkgd/dot_general | solution.py:176
  99.0 36.6 %all-to-all-start.1 = ((bf16[32,16,1024]{2,1,0:T(8,128)(2,1)}), bf16[32,16,1024]{2,1,0:T(8,128)(2,1)}, u32[]{:S(2)}, u32[]{:S(2)}) async-start(bf16[32,16,1024]{2,1,0:T(8,128)(2,1)} %bitcast.18), calls=%async_computation.1 | async-start | bytes 2097152 | tf_op jit(solution)/shard_map/all_to_all | solution.py:126
  138.7 23.1 %all-to-all-done.1 = bf16[32,16,1024]{2,1,0:T(8,128)(2,1)} async-done(((bf16[32,16,1024]{2,1,0:T(8,128)(2,1)}), bf16[32,16,1024]{2,1,0:T(8,128)(2,1)}, u32[]{:S(2)}, u32[]{:S(2)}) %all-to-all-start.1) | async-done | bytes 1048608 | tf_op jit(solution)/shard_map/all_to_all | solution.py:126
  161.8 3.8 %all-to-all-start.3 = ((bf16[32,16,1024]{2,1,0:T(8,128)(2,1)}), bf16[32,16,1024]{2,1,0:T(8,128)(2,1)S(1)}, u32[]{:S(2)}, u32[]{:S(2)}) async-start(bf16[32,16,1024]{2,1,0:T(8,128)(2,1)} %bitcast.24), calls=%async_computation.3 | async-start | bytes 2097152 | tf_op jit(solution)/shard_map/all_to_all | solution.py:126
  165.6 4.7 %convolution_convert_fusion.1 = bf16[512,2048]{1,0:T(8,128)(2,1)S(1)} fusion(bf16[512,1024]{1,0:T(8,128)(2,1)S(1)} %bitcast.84, bf16[1024,2048]{1,0:T(8,128)(2,1)} %param.14), kind=kOutput, calls=%fused_computation.29 | convolution fusion | flops 2148532224 | bytes 7340032 | tf_op jit(solution)/shard_map/dot_general | solution.py:184
  170.4 5.3 %fusion.8 = (f32[512]{0:T(512)S(1)}, bf16[512,2048]{1,0:T(8,128)(2,1)}) fusion(bf16[512,1024]{1,0:T(8,128)(2,1)} %bitcast.19, bf16[1024,2048]{1,0:T(8,128)(2,1)S(1)} %copy-done.17, bf16[512,2048]{1,0:T(8,128)(2,1)S(1)} %convolution_convert_fusion.1), kind=kOutput, calls=%fused_computation.14 | convolution fusion | flops 2153774592 | bytes 9439232 | tf_op jit(solution)/shard_map/dot_general | solution.py:189
  175.7 3.7 %convolution_convert_fusion = bf16[512,2048]{1,0:T(8,128)(2,1)} fusion(bf16[512,1024]{1,0:T(8,128)(2,1)S(1)} %bitcast.83, bf16[1024,2048]{1,0:T(8,128)(2,1)S(1)} %copy-done.16), kind=kOutput, calls=%fused_computation.28 | convolution fusion | flops 2148532224 | bytes 7340032 | tf_op jit(solution)/shard_map/dot_general | solution.py:184
  179.3 12.3 %all-to-all-done.3 = bf16[32,16,1024]{2,1,0:T(8,128)(2,1)S(1)} async-done(((bf16[32,16,1024]{2,1,0:T(8,128)(2,1)}), bf16[32,16,1024]{2,1,0:T(8,128)(2,1)S(1)}, u32[]{:S(2)}, u32[]{:S(2)}) %all-to-all-start.3) | async-done | bytes 1048608 | tf_op jit(solution)/shard_map/all_to_all | solution.py:126
  191.6 5.5 %fusion.11 = (f32[512]{0:T(512)S(1)}, bf16[512,2048]{1,0:T(8,128)(2,1)S(1)}) fusion(bf16[512,1024]{1,0:T(8,128)(2,1)S(1)} %bitcast.82, bf16[1024,2048]{1,0:T(8,128)(2,1)} %param.18, bf16[512,2048]{1,0:T(8,128)(2,1)} %convolution_convert_fusion), kind=kOutput, calls=%fused_computation.17 | convolution fusion | flops 2153774592 | bytes 9439232 | tf_op jit(solution)/shard_map/dot_general | solution.py:189
  198.3 18.0 %shard_map.128 = bf16[512,2048]{1,0:T(8,128)(2,1)S(1)} custom-call(bf16[512,2048]{1,0:T(8,128)(2,1)S(1)} %get-tuple-element.14.rows_ref, bf16[2,2816,2048]{2,1,0:T(8,128)(2,1)} %w_in_ref.3, bf16[2816,2048]{1,0:T(8,128)(2,1)} %w_out_ref.3), custom_call_target="tpu_custom_call" | custom-call | flops 8858370048 | bytes 21495808 | tf_op jit(solution)/shard_map/pallas_call | solution.py:66
  217.5 3.7 %all-to-all-start.4 = ((bf16[32,16,2048]{2,1,0:T(8,128)(2,1)}), bf16[32,16,2048]{2,1,0:T(8,128)(2,1)}, u32[]{:S(2)}, u32[]{:S(2)}) async-start(bf16[32,16,2048]{2,1,0:T(8,128)(2,1)} %bitcast.72), calls=%async_computation.4 | async-start | bytes 4194304 | tf_op jit(solution)/shard_map/all_to_all | solution.py:126
  221.3 17.7 %shard_map.127 = bf16[512,2048]{1,0:T(8,128)(2,1)S(1)} custom-call(bf16[512,2048]{1,0:T(8,128)(2,1)S(1)} %get-tuple-element.13.rows_ref, bf16[2,2816,2048]{2,1,0:T(8,128)(2,1)} %w_in_ref.3, bf16[2816,2048]{1,0:T(8,128)(2,1)} %w_out_ref.3), custom_call_target="tpu_custom_call" | custom-call | flops 8858370048 | bytes 21495808 | tf_op jit(solution)/shard_map/pallas_call | solution.py:66
  240.4 29.8 %all-to-all-done.4 = bf16[32,16,2048]{2,1,0:T(8,128)(2,1)} async-done(((bf16[32,16,2048]{2,1,0:T(8,128)(2,1)}), bf16[32,16,2048]{2,1,0:T(8,128)(2,1)}, u32[]{:S(2)}, u32[]{:S(2)}) %all-to-all-start.4) | async-done | bytes 2097184 | tf_op jit(solution)/shard_map/all_to_all | solution.py:126
  270.2 4.0 %all-to-all-start.2 = ((bf16[32,16,2048]{2,1,0:T(8,128)(2,1)}), bf16[32,16,2048]{2,1,0:T(8,128)(2,1)S(1)}, u32[]{:S(2)}, u32[]{:S(2)}) async-start(bf16[32,16,2048]{2,1,0:T(8,128)(2,1)} %bitcast.71), calls=%async_computation.2 | async-start | bytes 4194304 | tf_op jit(solution)/shard_map/all_to_all | solution.py:126
  274.2 3.9 %fusion.30 = (f32[256]{0:T(256)S(1)}, bf16[256,2048]{1,0:T(8,128)(2,1)S(1)}) fusion(bf16[256,1024]{0,1:T(8,128)(2,1)S(1)} %bitcast.77, bf16[1024,2048]{1,0:T(8,128)(2,1)} %param.18, bf16[256,2048]{1,0:T(8,128)(2,1)} %copy-done.20), kind=kOutput, calls=%fused_computation.52 | convolution fusion | flops 1076887296 | bytes 6816768 | tf_op jit(solution)/shard_map/dot_general | solution.py:201
  278.9 3.6 %fusion.25 = f32[256,2048]{1,0:T(8,128)} fusion(bf16[512,2048]{1,0:T(8,128)(2,1)} %bitcast.27, f32[256]{0:T(256)S(1)} %bitcast.93, s32[512]{0:T(512)S(1)} %fusion.86, s32[256]{0:T(256)S(1)} %bitcast.91), kind=kOutput, calls=%fused_computation.45 | convolution fusion | flops 538574848 | bytes 4198400 | tf_op jit(solution)/shard_map/dot_general | solution.py:213
  282.6 3.8 %fusion.23 = f32[256,2048]{1,0:T(8,128)} fusion(bf16[512,2048]{1,0:T(8,128)(2,1)} %bitcast.27, f32[256]{0:T(256)S(1)} %bitcast.101, s32[512]{0:T(512)S(1)} %fusion.86, s32[256]{0:T(256)S(1)} %bitcast.99), kind=kOutput, calls=%fused_computation.43 | convolution fusion | flops 538574848 | bytes 4198400 | tf_op jit(solution)/shard_map/dot_general | solution.py:213
  286.3 36.7 %all-to-all-done.2 = bf16[32,16,2048]{2,1,0:T(8,128)(2,1)S(1)} async-done(((bf16[32,16,2048]{2,1,0:T(8,128)(2,1)}), bf16[32,16,2048]{2,1,0:T(8,128)(2,1)S(1)}, u32[]{:S(2)}, u32[]{:S(2)}) %all-to-all-start.2) | async-done | bytes 2097184 | tf_op jit(solution)/shard_map/all_to_all | solution.py:126
  326.6 3.8 %fusion.19 = bf16[256,2048]{1,0:T(8,128)(2,1)} fusion(f32[256,2048]{1,0:T(8,128)S(1)} %copy-done.5, f32[256,2048]{1,0:T(8,128)S(1)} %copy-done.6, f32[256,2048]{1,0:T(8,128)S(1)} %fusion.21, bf16[512,2048]{1,0:T(8,128)(2,1)} %bitcast.74, bf16[256,2048]{1,0:T(8,128)(2,1)S(1)} %copy-done.9, f32[256]{0:T(256)S(1)} %bitcast.102, s32[512]{0:T(512)S(1)} %fusion.83, ...), kind=kOutput, calls=%fused_computation.39 | convolution fusion | flops 541720576 | bytes 10489856 | tf_op jit(solution)/shard_map/dot_general | solution.py:213
  (105 shorter events, 32.6 us)
Async XLA Ops:
  0.0 11.8 %copy-start = (bf16[2048,512]{1,0:T(8,128)(2,1)S(1)}, bf16[2048,512]{1,0:T(8,128)(2,1)}, u32[]{:S(2)}) copy-start(bf16[2048,512]{1,0:T(8,128)(2,1)} %param.17) | copy-start | bytes 6291460
  0.9 6.3 %collective-permute-start = (bf16[1,512]{1,0:T(2,128)(2,1)S(1)}, bf16[1,512]{1,0:T(2,128)(2,1)S(1)}, u32[]{:S(2)}, u32[]{:S(2)}) collective-permute-start(bf16[1,512]{1,0:T(2,128)(2,1)S(1)} %slice.49), channel_id=1, source_target_pairs={{0,1},{1,2},{2,3},{3,4},{4,5},{5,6},{6,7},{7,8},{8,9},{9,10},{10,1... | collective-permute-start | bytes 3080 | tf_op jit(solution)/shard_map/ppermute | solution.py:22
  7.1 4.7 %copy-start.19 = (f32[2048]{0:T(1024)S(1)}, f32[2048]{0:T(1024)}, u32[]{:S(2)}) copy-start(f32[2048]{0:T(1024)} %param.15) | copy-start | bytes 24580
  13.8 31.0 %collective-permute-start.1 = (bf16[256,512]{0,1:T(8,128)(2,1)S(1)}, bf16[256,512]{0,1:T(8,128)(2,1)}, u32[]{:S(2)}, u32[]{:S(2)}) collective-permute-start(bf16[256,512]{0,1:T(8,128)(2,1)S(1)} %pad_maximum_fusion.2), channel_id=1, source_target_pairs={{0,8},{1,9},{2,10},{3,11},{4,12},{5,13},{6,14},{7,15},{8,16},{9,17... | collective-permute-start | bytes 786440 | tf_op jit(solution)/shard_map/ppermute | solution.py:22
  19.9 29.2 %collective-permute-start.2 = (bf16[256,512]{0,1:T(8,128)(2,1)S(1)}, bf16[256,512]{0,1:T(8,128)(2,1)}, u32[]{:S(2)}, u32[]{:S(2)}) collective-permute-start(bf16[256,512]{0,1:T(8,128)(2,1)S(1)} %pad_maximum_fusion.2), channel_id=1, source_target_pairs={{0,7},{1,8},{2,9},{3,10},{4,11},{5,12},{6,13},{7,14},{8,15},{9,16}... | collective-permute-start | bytes 786440 | tf_op jit(solution)/shard_map/ppermute | solution.py:22
  25.0 28.5 %collective-permute-start.3 = (bf16[256,512]{0,1:T(8,128)(2,1)S(1)}, bf16[256,512]{0,1:T(8,128)(2,1)S(1)}, u32[]{:S(2)}, u32[]{:S(2)}) collective-permute-start(bf16[256,512]{0,1:T(8,128)(2,1)S(1)} %pad_maximum_fusion.2), channel_id=1, source_target_pairs={{0,6},{1,7},{2,8},{3,9},{4,10},{5,11},{6,12},{7,13},{8,14},{9,15},... | collective-permute-start | bytes 786440 | tf_op jit(solution)/shard_map/ppermute | solution.py:22
  27.8 27.9 %collective-permute-start.4 = (bf16[256,512]{0,1:T(8,128)(2,1)S(1)}, bf16[256,512]{0,1:T(8,128)(2,1)S(1)}, u32[]{:S(2)}, u32[]{:S(2)}) collective-permute-start(bf16[256,512]{0,1:T(8,128)(2,1)S(1)} %pad_maximum_fusion.2), channel_id=1, source_target_pairs={{0,5},{1,6},{2,7},{3,8},{4,9},{5,10},{6,11},{7,12},{8,13},{9,14},{... | collective-permute-start | bytes 786440 | tf_op jit(solution)/shard_map/ppermute | solution.py:22
  29.1 26.6 %collective-permute-start.5 = (bf16[256,512]{0,1:T(8,128)(2,1)S(1)}, bf16[256,512]{0,1:T(8,128)(2,1)S(1)}, u32[]{:S(2)}, u32[]{:S(2)}) collective-permute-start(bf16[256,512]{0,1:T(8,128)(2,1)S(1)} %pad_maximum_fusion.2), channel_id=1, source_target_pairs={{0,4},{1,5},{2,6},{3,7},{4,8},{5,9},{6,10},{7,11},{8,12},{9,13},{1... | collective-permute-start | bytes 786440 | tf_op jit(solution)/shard_map/ppermute | solution.py:22
  36.8 2.6 copy-start.14
  38.0 1.9 copy-start.15
  42.0 56.9 %all-to-all-start = ((bf16[32,32,1024]{2,1,0:T(8,128)(2,1)}), bf16[32,32,1024]{2,1,0:T(8,128)(2,1)S(1)}, u32[]{:S(2)}, u32[]{:S(2)}) async-start(bf16[32,32,1024]{2,1,0:T(8,128)(2,1)} %pad_maximum_fusion), calls=%async_computation | async-start | bytes 4194304 | tf_op jit(solution)/shard_map/all_to_all | solution.py:126
  44.8 24.0 %collective-permute-start.6 = (bf16[256,512]{0,1:T(8,128)(2,1)S(1)}, bf16[256,512]{0,1:T(8,128)(2,1)S(1)}, u32[]{:S(2)}, u32[]{:S(2)}) collective-permute-start(bf16[256,512]{0,1:T(8,128)(2,1)S(1)} %pad_maximum_fusion.2), channel_id=1, source_target_pairs={{0,3},{1,4},{2,5},{3,6},{4,7},{5,8},{6,9},{7,10},{8,11},{9,12},{10... | collective-permute-start | bytes 786440 | tf_op jit(solution)/shard_map/ppermute | solution.py:22
  49.1 27.1 %collective-permute-start.7 = (bf16[256,512]{0,1:T(8,128)(2,1)S(1)}, bf16[256,512]{0,1:T(8,128)(2,1)S(1)}, u32[]{:S(2)}, u32[]{:S(2)}) collective-permute-start(bf16[256,512]{0,1:T(8,128)(2,1)S(1)} %pad_maximum_fusion.2), channel_id=1, source_target_pairs={{0,2},{1,3},{2,4},{3,5},{4,6},{5,7},{6,8},{7,9},{8,10},{9,11},{10,... | collective-permute-start | bytes 786440 | tf_op jit(solution)/shard_map/ppermute | solution.py:22
  53.5 22.8 %collective-permute-start.8 = (bf16[256,512]{0,1:T(8,128)(2,1)S(1)}, bf16[256,512]{0,1:T(8,128)(2,1)S(1)}, u32[]{:S(2)}, u32[]{:S(2)}) collective-permute-start(bf16[256,512]{0,1:T(8,128)(2,1)S(1)} %pad_maximum_fusion.2), channel_id=1, source_target_pairs={{0,1},{1,2},{2,3},{3,4},{4,5},{5,6},{6,7},{7,8},{8,9},{9,10},{10,1... | collective-permute-start | bytes 786440 | tf_op jit(solution)/shard_map/ppermute | solution.py:22
  99.0 62.8 %all-to-all-start.1 = ((bf16[32,16,1024]{2,1,0:T(8,128)(2,1)}), bf16[32,16,1024]{2,1,0:T(8,128)(2,1)}, u32[]{:S(2)}, u32[]{:S(2)}) async-start(bf16[32,16,1024]{2,1,0:T(8,128)(2,1)} %bitcast.18), calls=%async_computation.1 | async-start | bytes 2097152 | tf_op jit(solution)/shard_map/all_to_all | solution.py:126
  138.7 26.9 %copy-start.11 = (bf16[32,16,1024]{2,1,0:T(8,128)(2,1)S(1)}, bf16[32,16,1024]{2,1,0:T(8,128)(2,1)}, u32[]{:S(2)}) copy-start(bf16[32,16,1024]{2,1,0:T(8,128)(2,1)} %get-tuple-element.9) | copy-start | bytes 3145732
  161.8 29.9 %all-to-all-start.3 = ((bf16[32,16,1024]{2,1,0:T(8,128)(2,1)}), bf16[32,16,1024]{2,1,0:T(8,128)(2,1)S(1)}, u32[]{:S(2)}, u32[]{:S(2)}) async-start(bf16[32,16,1024]{2,1,0:T(8,128)(2,1)} %bitcast.24), calls=%async_computation.3 | async-start | bytes 2097152 | tf_op jit(solution)/shard_map/all_to_all | solution.py:126
  165.6 4.7 %copy-start.17 = (bf16[1024,2048]{1,0:T(8,128)(2,1)S(1)}, bf16[1024,2048]{1,0:T(8,128)(2,1)}, u32[]{:S(2)}) copy-start(bf16[1024,2048]{1,0:T(8,128)(2,1)} %param.18) | copy-start | bytes 12582916
  170.3 5.3 %copy-start.10 = (bf16[32,16,1024]{2,1,0:T(8,128)(2,1)S(1)}, bf16[32,16,1024]{2,1,0:T(8,128)(2,1)}, u32[]{:S(2)}) copy-start(bf16[32,16,1024]{2,1,0:T(8,128)(2,1)} %get-tuple-element.10) | copy-start | bytes 3145732
  170.3 5.3 %copy-start.16 = (bf16[1024,2048]{1,0:T(8,128)(2,1)S(1)}, bf16[1024,2048]{1,0:T(8,128)(2,1)}, u32[]{:S(2)}) copy-start(bf16[1024,2048]{1,0:T(8,128)(2,1)} %param.14) | copy-start | bytes 12582916
  191.6 5.6 %copy-start.7 = (bf16[512,2048]{1,0:T(8,128)(2,1)S(1)}, bf16[512,2048]{1,0:T(8,128)(2,1)}, u32[]{:S(2)}) copy-start(bf16[512,2048]{1,0:T(8,128)(2,1)} %get-tuple-element.26) | copy-start | bytes 6291460
  191.6 5.6 %copy-start.12 = (f32[2048]{0:T(1024)S(1)}, f32[2048]{0:T(1024)}, u32[]{:S(2)}) copy-start(f32[2048]{0:T(1024)} %param.20) | copy-start | bytes 24580
  217.5 52.6 %all-to-all-start.4 = ((bf16[32,16,2048]{2,1,0:T(8,128)(2,1)}), bf16[32,16,2048]{2,1,0:T(8,128)(2,1)}, u32[]{:S(2)}, u32[]{:S(2)}) async-start(bf16[32,16,2048]{2,1,0:T(8,128)(2,1)} %bitcast.72), calls=%async_computation.4 | async-start | bytes 4194304 | tf_op jit(solution)/shard_map/all_to_all | solution.py:126
  239.0 1.4 copy-start.2
  270.2 52.9 %all-to-all-start.2 = ((bf16[32,16,2048]{2,1,0:T(8,128)(2,1)}), bf16[32,16,2048]{2,1,0:T(8,128)(2,1)S(1)}, u32[]{:S(2)}, u32[]{:S(2)}) async-start(bf16[32,16,2048]{2,1,0:T(8,128)(2,1)} %bitcast.71), calls=%async_computation.2 | async-start | bytes 4194304 | tf_op jit(solution)/shard_map/all_to_all | solution.py:126
  274.2 4.0 %copy-start.18 = (bf16[2048,64]{0,1:T(8,128)(2,1)S(1)}, bf16[2048,64]{0,1:T(8,128)(2,1)}, u32[]{:S(2)}) copy-start(bf16[2048,64]{0,1:T(8,128)(2,1)} %param.21) | copy-start | bytes 786436
  278.1 4.4 %copy-start.8 = (bf16[256,2048]{1,0:T(8,128)(2,1)}, bf16[256,2048]{1,0:T(8,128)(2,1)S(1)}, u32[]{:S(2)}) copy-start(bf16[256,2048]{1,0:T(8,128)(2,1)S(1)} %get-tuple-element.24) | copy-start | bytes 3145732
  282.6 42.6 %copy-start.9 = (bf16[256,2048]{1,0:T(8,128)(2,1)S(1)}, bf16[256,2048]{1,0:T(8,128)(2,1)}, u32[]{:S(2)}) copy-start(bf16[256,2048]{1,0:T(8,128)(2,1)} %copy-done.8) | copy-start | bytes 3145732
  323.1 1.3 copy-start.4
  324.4 1.6 copy-start.5
  324.4 2.2 copy-start.6
  326.6 3.8 %copy-start.1 = (bf16[2048,512]{1,0:T(8,128)(2,1)S(1)}, bf16[2048,512]{1,0:T(8,128)(2,1)}, u32[]{:S(2)}) copy-start(bf16[2048,512]{1,0:T(8,128)(2,1)} %param.17) | copy-start | bytes 6291460
  (3 other events, 3.0 us)
where the time goes:
time: 331 us; the launch traced here: 330 us
  waiting for transfers between devices  122 us (37%)
  starting transfers between devices  80.8 us (24%)
  matrix products  67.7 us (20%)
  Pallas kernels  35.7 us (11%)
  local copies, waits for them, and re-layouts  14 us (4%)
  other arithmetic  9.2 us (3%)
    all_to_all x5, waiting for transfers between devices, exchange(): return lax.all_to_all(rows, 'tm', split_axis=0, concat_axis=0, tiled=True)  102 us
    all_to_all x5, starting transfers between devices, exchange(): return lax.all_to_all(rows, 'tm', split_axis=0, concat_axis=0, tiled=True)  50.9 us
    pallas_call x2, Pallas kernels, run_expert(): pl.pallas_call(functools.partial(expert_body, steps), grid=(row_total //...  35.7 us
    ppermute x9, starting transfers between devices, from_behind(): return lax.ppermute(block, axis, route)  29.9 us
    ppermute x9, waiting for transfers between devices, from_behind(): return lax.ppermute(block, axis, route)  20.5 us
    dot_general x4, matrix products, shards(): jnp.dot(hot.astype(jnp.bfloat16), returned[local], preferred_element_type...  12 us
    sub x1, matrix products, shards(): exp_scores = jnp.exp(scores - row_max)  11.8 us
    dot_general x2, matrix products, rows_of(): jnp.dot(contexts, w_out, preferred_element_type=jnp.float32)  10.8 us
  transfers between devices with their start and end apart: 14, of which 6 were waited for; matrix products, arithmetic and copies ran while one was open for 20% of the time, Pallas kernels for 5%

commit v1 on v0

--- a/solution.py
+++ b/solution.py
@@ -32,9 +32,14 @@
     return values * lax.rsqrt(mean_sq + NORM_EPS)
 
 
-def expert_body(steps, rows_ref, w_in_ref, w_out_ref, out_ref, total_ref):
+def expert_body(steps, mid_ref, gain_ref, w_in_ref, w_out_ref, out_ref, rows_ref, total_ref):
     step = pl.program_id(1)
-    width = w_in_ref.shape[1]
+
+    @pl.when(step == 0)
+    def _():
+        mid = mid_ref[...].astype(jnp.float32)
+        rows_ref[...] = rms_scale(mid, gain_ref[...]).astype(jnp.bfloat16)
+
     rows = rows_ref[...]
     nt = (((1,), (1,)), ((), ()))
     gate = lax.dot_general(rows, w_in_ref[0], nt, preferred_element_type=jnp.float32)
@@ -55,8 +60,8 @@
         out_ref[...] = total_ref[...].astype(out_ref.dtype)
 
 
-def run_expert(rows, expert_in, expert_out, local, local_count):
-    row_total, feat_dim = rows.shape
+def run_expert(mid, gain, expert_in, expert_out, local, local_count):
+    row_total, feat_dim = mid.shape
     units = expert_out.shape[0] // local_count
     width = 352
     steps = units // width
@@ -68,19 +73,157 @@
         grid=(row_total // tile, steps),
         in_specs=[
             pl.BlockSpec((tile, feat_dim), lambda r, i: (r, 0)),
+            pl.BlockSpec((1, feat_dim), lambda r, i: (0, 0)),
             pl.BlockSpec((2, width, feat_dim), lambda r, i: (0, first + i, 0)),
             pl.BlockSpec((width, feat_dim), lambda r, i: (first + i, 0)),
         ],
         out_specs=pl.BlockSpec((tile, feat_dim), lambda r, i: (r, 0)),
         out_shape=jax.ShapeDtypeStruct((row_total, feat_dim), jnp.bfloat16),
-        scratch_shapes=[pltpu.VMEM((tile, feat_dim), jnp.float32)],
+        scratch_shapes=[
+            pltpu.VMEM((tile, feat_dim), jnp.bfloat16),
+            pltpu.VMEM((tile, feat_dim), jnp.float32),
+        ],
         compiler_params=pltpu.CompilerParams(vmem_limit_bytes=40 << 20),
         cost_estimate=pl.CostEstimate(
             flops=flops,
             bytes_accessed=6 * units * feat_dim + 4 * row_total * feat_dim,
             transcendentals=row_total * units,
         ),
-    )(rows, expert_in, expert_out)
+    )(mid, gain.reshape(1, -1), expert_in, expert_out)
+
+
+def kv_body(rows_ref, weight_ref, out_ref):
+    both = jnp.dot(rows_ref[...], weight_ref[...], preferred_element_type=jnp.float32)
+    kv_dim = both.shape[1] // 2
+    for start in range(0, kv_dim, HEAD_DIM):
+        head = both[:, start : start + HEAD_DIM]
+        out_ref[:, start : start + HEAD_DIM] = head_norm(head).astype(out_ref.dtype)
+    out_ref[:, kv_dim:] = both[:, kv_dim:].astype(out_ref.dtype)
+
+
+def project_kv(rows, weight):
+    row_count, feat_dim = rows.shape
+    width = weight.shape[1]
+    return pl.pallas_call(
+        kv_body,
+        out_shape=jax.ShapeDtypeStruct((row_count, width), jnp.bfloat16),
+        in_specs=[pl.BlockSpec(memory_space=pltpu.VMEM)] * 2,
+        out_specs=pl.BlockSpec(memory_space=pltpu.VMEM),
+        compiler_params=pltpu.CompilerParams(vmem_limit_bytes=16 << 20),
+        cost_estimate=pl.CostEstimate(
+            flops=2 * row_count * feat_dim * width,
+            bytes_accessed=2 * (row_count * feat_dim + feat_dim * width),
+            transcendentals=row_count,
+        ),
+    )(rows, weight)
+
+
+def attend_body(
+    kv_heads, valid_ref, scale_ref, query_ref, *refs
+):
+    *kv_refs, out_ref, unit_ref, key_ref, value_ref, score_ref = refs
+    blocks = [ref.at[part] for ref in kv_refs for part in range(ref.shape[0])]
+    rows = query_ref.shape[0]
+    heads = query_ref.shape[1] // HEAD_DIM
+    group = heads // kv_heads
+    kv_dim = kv_heads * HEAD_DIM
+    for head in range(heads):
+        unit_ref[head] = head_norm(
+            query_ref[:, head * HEAD_DIM : (head + 1) * HEAD_DIM]
+        ).astype(jnp.bfloat16)
+    for pos, block in enumerate(blocks):
+        for kv in range(kv_heads):
+            low = kv * HEAD_DIM
+            key_ref[kv, pos] = block[:, low : low + HEAD_DIM]
+            value_ref[kv, pos, :, :HEAD_DIM] = block[:, kv_dim + low : kv_dim + low + HEAD_DIM]
+            value_ref[kv, pos, :, HEAD_DIM:] = jnp.ones((rows, HEAD_DIM), jnp.bfloat16)
+    query_at = lax.broadcasted_iota(jnp.int32, (rows, rows), 0)
+    key_at = lax.broadcasted_iota(jnp.int32, (rows, rows), 1)
+
+    @pl.loop(0, heads)
+    def _(head):
+        kv = head // group
+        unit = unit_ref[head]
+        top = jnp.full((rows, HEAD_DIM), MASKED, jnp.float32)
+        for pos in range(len(blocks)):
+            score = lax.dot_general(
+                unit,
+                key_ref[kv, pos],
+                (((1,), (1,)), ((), ())),
+                preferred_element_type=jnp.float32,
+            )
+            if pos == 0:
+                score = jnp.where(key_at <= query_at, score, MASKED)
+            else:
+                seen = valid_ref[pos] > 0
+                if pos == 1:
+                    score = jnp.where((key_at > query_at) & seen, score, MASKED)
+                else:
+                    score = jnp.where(seen, score, MASKED)
+            score_ref[pos] = score
+            for low in range(0, rows, HEAD_DIM):
+                top = jnp.maximum(top, score[:, low : low + HEAD_DIM])
+        top = jnp.max(top, axis=1, keepdims=True)
+        factor = scale_ref[head] * (math.log2(math.e) / math.sqrt(HEAD_DIM))
+        total = jnp.zeros((rows, 2 * HEAD_DIM), jnp.float32)
+        for pos in range(len(blocks)):
+            weight = jnp.exp2((score_ref[pos] - top) * factor).astype(jnp.bfloat16)
+            total += jnp.dot(weight, value_ref[kv, pos], preferred_element_type=jnp.float32)
+        place = pl.ds(pl.multiple_of(head * HEAD_DIM, HEAD_DIM), HEAD_DIM)
+        out_ref[:, place] = (total[:, :HEAD_DIM] / total[:, HEAD_DIM:]).astype(out_ref.dtype)
+
+
+def attend(valid, head_scale, queries, kv_parts, kv_heads):
+    rows, width = queries.shape
+    heads = width // HEAD_DIM
+    count = sum(part.shape[0] for part in kv_parts)
+    smem = pl.BlockSpec(memory_space=pltpu.SMEM)
+    vmem = pl.BlockSpec(memory_space=pltpu.VMEM)
+    return pl.pallas_call(
+        functools.partial(attend_body, kv_heads),
+        out_shape=jax.ShapeDtypeStruct((rows, width), jnp.bfloat16),
+        in_specs=[smem, smem, vmem] + [vmem] * len(kv_parts),
+        out_specs=vmem,
+        scratch_shapes=[
+            pltpu.VMEM((heads, rows, HEAD_DIM), jnp.bfloat16),
+            pltpu.VMEM((kv_heads, count, rows, HEAD_DIM), jnp.bfloat16),
+            pltpu.VMEM((kv_heads, count, rows, 2 * HEAD_DIM), jnp.bfloat16),
+            pltpu.VMEM((count, rows, rows), jnp.float32),
+        ],
+        compiler_params=pltpu.CompilerParams(vmem_limit_bytes=32 << 20),
+        cost_estimate=pl.CostEstimate(
+            flops=6 * heads * count * rows * rows * HEAD_DIM,
+            bytes_accessed=rows * width * 6 + count * rows * kv_heads * HEAD_DIM * 4,
+            transcendentals=heads * count * rows * rows,
+        ),
+    )(valid, head_scale, queries, *kv_parts)
+
+
+def window_parts(own_kv, group):
+    devices = lax.axis_size("tm")
+    me = lax.axis_index("tm")
+    core, chip, base = me % 2, me % group // 2, me // group * group
+    prior = from_behind(own_kv, "tm", group)
+    parts = [(own_kv, me), (prior, me - group)]
+    fetched = []
+    for step in range(1, group // 2):
+        route = []
+        for dev in range(devices):
+            target = dev ^ (2 * step)
+            target += 0 if dev < target else group
+            if target < devices:
+                route.append((dev, target))
+        other = chip ^ step
+        start = base - jnp.where(other > chip, group, 0) + 2 * other
+        fetched.append((lax.ppermute(own_kv, "tm", route), start))
+    shared = jnp.stack([block for block, _ in fetched] + [jnp.where(core == 0, own_kv, prior)])
+    shared = lax.ppermute(shared, "tm", [(dev, dev ^ 1) for dev in range(devices)])
+    numbers = [start + core for _, start in fetched]
+    numbers += [start + 1 - core for _, start in fetched]
+    numbers.append(jnp.where(core == 0, me + 1 - group, me - 1))
+    blocks = [own_kv[None], prior[None]] + [block[None] for block, _ in fetched] + [shared]
+    numbers = jnp.stack([me, me - group] + numbers)
+    return blocks, numbers
 
 
 def shards(
@@ -125,76 +268,82 @@
     def exchange(rows):
         return lax.all_to_all(rows, "tm", split_axis=0, concat_axis=0, tiled=True)
 
+    reach_blocks = WINDOW // row_count
+    group = reach_blocks
+    lines = devices // group
     before = from_behind(signal[row_count - 1 :], "tm", 1)
     previous = jnp.concatenate([before, signal[:-1]], axis=0)
     patch_pairs = jnp.concatenate([previous, signal], axis=1)
-    pairs_out = jnp.concatenate(
-        [spread(patch_pairs, local).reshape(devices, CAP, -1) for local in range(local_count)],
-        axis=1,
-    )
-    pairs_in = exchange(pairs_out)
+
+    ahead = jnp.concatenate(
+        [
+            signal,
+            before,
+            expert_ids.astype(jnp.bfloat16).T.reshape(-1, signal.shape[1]),
+            slot_ids.astype(jnp.bfloat16).T.reshape(-1, signal.shape[1]),
+        ],
+        axis=0,
+    )
+    used = ahead.shape[0]
+    ahead = jnp.pad(ahead, ((0, -used % 16), (0, 0)))
+    line_groups = [[row * group + place for row in range(lines)] for place in range(group)]
+    gathered = lax.all_gather(ahead, "tm", axis_index_groups=line_groups)
 
     embedded = jnp.dot(patch_pairs, conv_weight, preferred_element_type=jnp.float32).astype(
         jnp.bfloat16
     )
     normed = rms_scale(embedded.astype(jnp.float32), attn_gain).astype(jnp.bfloat16)
-    head_count = head_scale.shape[0]
-    kv_dim = w_keyval.shape[1] // 2
-    kv_heads = kv_dim // HEAD_DIM
-    group_size = head_count // kv_heads
-    keyval = jnp.dot(normed, w_keyval, preferred_element_type=jnp.float32).reshape(
-        row_count, 2, kv_heads, HEAD_DIM
-    )
-    key_unit = head_norm(keyval[:, 0]).astype(jnp.bfloat16)
-    value_bf = keyval[:, 1].astype(jnp.bfloat16)
-    own_kv = jnp.concatenate(
-        [key_unit.reshape(row_count, kv_dim), value_bf.reshape(row_count, kv_dim)], axis=1
-    )
-    reach_blocks = WINDOW // row_count
-    earlier = [from_behind(own_kv, "tm", distance) for distance in range(reach_blocks, 0, -1)]
-    queries = jnp.dot(normed, w_query, preferred_element_type=jnp.float32).reshape(
-        row_count, kv_heads, group_size, HEAD_DIM
-    )
-    query_unit = head_norm(queries).astype(jnp.bfloat16)
-    window_kv = jnp.concatenate(earlier + [own_kv], axis=0)
-    key_len = window_kv.shape[0]
-    win_keys = window_kv[:, :kv_dim].reshape(key_len, kv_heads, HEAD_DIM)
-    win_values = window_kv[:, kv_dim:].reshape(key_len, kv_heads, HEAD_DIM)
-    scores = jnp.einsum("qkgd,lkd->kgql", query_unit, win_keys, preferred_element_type=jnp.float32)
-    scores = scores * (head_scale.reshape(kv_heads, group_size, 1, 1) / math.sqrt(HEAD_DIM))
-    query_pos = dev_index * row_count + jnp.arange(row_count, dtype=jnp.int32)
-    key_pos = (dev_index - reach_blocks) * row_count + jnp.arange(key_len, dtype=jnp.int32)
-    visible = (
-        (key_pos[None, :] <= query_pos[:, None])
-        & (key_pos[None, :] > query_pos[:, None] - WINDOW)
-        & (key_pos[None, :] >= 0)
-    )
-    scores = jnp.where(visible, scores, MASKED)
-    row_max = jnp.max(scores, axis=-1, keepdims=True)
-    exp_scores = jnp.exp(scores - row_max)
-    probs = (exp_scores / jnp.sum(exp_scores, axis=-1, keepdims=True)).astype(jnp.bfloat16)
-    context = jnp.einsum("kgql,lkd->qkgd", probs, win_values, preferred_element_type=jnp.float32)
-    context = context.astype(jnp.bfloat16).reshape(row_count, head_count * HEAD_DIM)
+    kv_heads = w_keyval.shape[1] // 2 // HEAD_DIM
+    own_kv = project_kv(normed, w_keyval)
+    kv_parts, numbers = window_parts(own_kv, group)
+    queries = jnp.dot(normed, w_query, preferred_element_type=jnp.float32)
+    context = attend((numbers >= 0).astype(jnp.int32), head_scale, queries, kv_parts, kv_heads)
+
+    line_signal = gathered[:, :row_count]
+    line_before = gathered[:, row_count : row_count + 1]
+    line_previous = jnp.concatenate([line_before, line_signal[:, :-1]], axis=1)
+    line_pairs = jnp.concatenate([line_previous, line_signal], axis=2)
+    id_rows = (used - row_count - 1) // 2
+    line_ids = gathered[:, row_count + 1 : row_count + 1 + id_rows].astype(jnp.int32)
+    line_slots = gathered[:, row_count + 1 + id_rows : used].astype(jnp.int32)
+    line_keys = (line_ids * CAP + line_slots).reshape(lines, 2, 1, row_count)
+    near_dev = dev_index // group * group + jnp.arange(group, dtype=jnp.int32)
+    near_expert = (near_dev // copies * local_count)[:, None] + jnp.arange(
+        local_count, dtype=jnp.int32
+    )
+    near_keys = near_expert[:, :, None] * CAP + jnp.arange(CAP, dtype=jnp.int32)
+    near_keys = near_keys.reshape(1, -1, 1)
+    line_hot = (near_keys == line_keys[:, 0]) | (near_keys == line_keys[:, 1])
+    pairs_out = jnp.einsum(
+        "lrt,ltf->rlf", line_hot.astype(jnp.bfloat16), line_pairs,
+        preferred_element_type=jnp.float32,
+    ).astype(jnp.bfloat16)
+    pairs_out = pairs_out.reshape(group, local_count * CAP, lines, -1)
+    near_groups = [[row * group + place for place in range(group)] for row in range(lines)]
+    pairs_in = lax.all_to_all(
+        pairs_out, "tm", split_axis=0, concat_axis=0, axis_index_groups=near_groups, tiled=True
+    )
+    pairs_in = pairs_in.transpose(2, 0, 1, 3).reshape(devices, local_count * CAP, -1)
 
     context_in = [
         exchange(spread(context, local).reshape(devices, CAP, -1)) for local in range(local_count)
     ]
 
-    def rows_of(pairs, contexts):
+    def mid_of(pairs, contexts):
         placed = jnp.dot(pairs, conv_weight, preferred_element_type=jnp.float32).astype(
             jnp.bfloat16
         )
-        mid = (
+        return (
             placed.astype(jnp.float32)
             + jnp.dot(contexts, w_out, preferred_element_type=jnp.float32)
         ).astype(jnp.bfloat16)
-        return mid, rms_scale(mid.astype(jnp.float32), ffn_gain).astype(jnp.bfloat16)
 
     returned = []
     for local in range(local_count):
         pairs = pairs_in[:, local * CAP : (local + 1) * CAP].reshape(slots, -1)
-        _, rows = rows_of(pairs, context_in[local].reshape(slots, -1))
-        result = run_expert(rows, expert_in, expert_out, local, local_count)
+        contexts = context_in[local].reshape(slots, -1)
+        mid = mid_of(pairs, contexts)
+        result = run_expert(mid, ffn_gain, expert_in, expert_out, local, local_count)
         returned.append(exchange(result.reshape(devices, CAP, feat_dim)).reshape(slots, feat_dim))
 
     stream_mid = (

time: 331 us -> 282 us (0.85)
  matrix products: 67.7 us -> 42.3 us
  starting transfers between devices: 80.8 us -> 55.4 us
  waiting for transfers between devices: 122 us -> 97.4 us
  Pallas kernels: 35.7 us -> 55.4 us
  between operations: 0.58 us -> 13.9 us
  other arithmetic: 9.2 us -> 4.18 us
    all_to_all x5 -> x4, starting transfers between devices: 50.9 us -> 17.1 us  [exchange(): return lax.all_to_all(rows, 'tm', split_axis=0, concat_axis=0, tiled=True)]
    ppermute x9 -> x2, waiting for transfers between devices: 20.5 us -> 0.01 us  [from_behind(): return lax.ppermute(block, axis, route)]
    all_to_all x5 -> x4, waiting for transfers between devices: 102 us -> 82.5 us  [exchange(): return lax.all_to_all(rows, 'tm', split_axis=0, concat_axis=0, tiled=True)]
    ppermute x9 -> x2, starting transfers between devices: 29.9 us -> 10.8 us  [from_behind(): return lax.ppermute(block, axis, route)]
    pallas_call x0 -> x2, Pallas kernels: none -> 15.8 us  [the longest x1 15 us: attend(): pl.pallas_call(functools.partial(attend_body, kv_heads), out_shape=jax.Sh...]
    all_to_all x0 -> x1, starting transfers between devices: none -> 15.7 us  [shards(): lax.all_to_all(pairs_out, 'tm', split_axis=0, concat_axis=0, axis_index_g...]
    sub x1 -> x0, matrix products: 11.8 us -> none  [shards(): exp_scores = jnp.exp(scores - row_max)]
    ppermute x0 -> x4, starting transfers between devices: none -> 11.7 us  [the longest x3 11.2 us: window_parts(): fetched.append((lax.ppermute(own_kv, 'tm', route), start))]
  transfers between devices with their start and end apart: 14 -> 12, of which waited for: 6 -> 5; matrix products, arithmetic and copies ran while one was open for 20% -> 17% of each run, Pallas kernels for 5% -> 20%
where the time goes in v1:
time: 282 us; the launch traced here: 281 us
  waiting for transfers between devices  97.4 us (35%)
  starting transfers between devices  55.4 us (20%)
  Pallas kernels  55.4 us (20%)
  matrix products  42.3 us (15%)
  between operations  13.9 us (5%)
  local copies, waits for them, and re-layouts  12.7 us (5%)
  other arithmetic  4.18 us (1%)
    all_to_all x4, waiting for transfers between devices, exchange(): return lax.all_to_all(rows, 'tm', split_axis=0, concat_axis=0, tiled=True)  82.5 us
    pallas_call x2, Pallas kernels, run_expert(): pl.pallas_call(functools.partial(expert_body, steps), grid=(row_total //...  39.7 us
    all_to_all x4, starting transfers between devices, exchange(): return lax.all_to_all(rows, 'tm', split_axis=0, concat_axis=0, tiled=True)  17.1 us
    all_to_all x1, starting transfers between devices, shards(): lax.all_to_all(pairs_out, 'tm', split_axis=0, concat_axis=0, axis_index_g...  15.7 us
    pallas_call x1, Pallas kernels, attend(): pl.pallas_call(functools.partial(attend_body, kv_heads), out_shape=jax.Sh...  15 us
    ppermute x3, starting transfers between devices, window_parts(): fetched.append((lax.ppermute(own_kv, 'tm', route), start))  11.2 us
    ppermute x2, starting transfers between devices, from_behind(): return lax.ppermute(block, axis, route)  10.8 us
    dot_general x4, matrix products, shards(): jnp.dot(hot.astype(jnp.bfloat16), returned[local], preferred_element_type...  10.7 us
  transfers between devices with their start and end apart: 12, of which 5 were waited for; matrix products, arithmetic and copies ran while one was open for 17% of the time, Pallas kernels for 20%

profile of v1, /device:TPU:0, one launch (start us, length us, event | category | flops | bytes accessed | tf_op | source)
XLA Modules:
  0.0 281.2 jit_solution(7333486814710045765)
XLA Ops:
  7.3 2.3 collective-permute-start
  10.5 1.7 fusion.61
  12.4 3.7 %fusion.13 = (f32[256]{0:T(256)S(1)}, bf16[256,2048]{1,0:T(8,128)(2,1)S(1)}) fusion(bf16[1024,2048]{1,0:T(8,128)(2,1)} %param.14, bf16[256,512]{1,0:T(8,128)(2,1)} %param.13, bf16[255,512]{1,0:T(8,128)(2,1)} %bitcast.95, bf16[1,512]{1,0:T(2,128)(2,1)S(1)} %collective-permute-done), kind=kOutput, calls=%fused_computation.28 | convolution fusion | flops 1077411584 | bytes 5768192 | tf_op jit(solution)/shard_map/dot_general | solution.py:292
  19.0 8.5 %collective-permute-start.1 = (bf16[256,512]{1,0:T(8,128)(2,1)S(1)}, bf16[256,512]{1,0:T(8,128)(2,1)S(1)}, u32[]{:S(2)}, u32[]{:S(2)}) collective-permute-start(bf16[256,512]{1,0:T(8,128)(2,1)S(1)} %shard_map.127), channel_id=1, source_target_pairs={{0,8},{1,9},{2,10},{3,11},{4,12},{5,13},{6,14},{7,15},{8,16},{9,17... | collective-permute-start | bytes 786440 | tf_op jit(solution)/shard_map/ppermute | solution.py:22
  29.0 3.4 %collective-permute-start.3 = (bf16[256,512]{1,0:T(8,128)(2,1)S(1)}, bf16[256,512]{1,0:T(8,128)(2,1)S(1)}, u32[]{:S(2)}, u32[]{:S(2)}) collective-permute-start(bf16[256,512]{1,0:T(8,128)(2,1)S(1)} %shard_map.127), channel_id=1, source_target_pairs={{0,4},{1,5},{2,6},{3,7},{4,8},{5,9},{6,10},{7,11},{8,12},{9,13},{1... | collective-permute-start | bytes 786440 | tf_op jit(solution)/shard_map/ppermute | solution.py:218
  32.5 6.2 %collective-permute-start.4 = (bf16[256,512]{1,0:T(8,128)(2,1)S(1)}, bf16[256,512]{1,0:T(8,128)(2,1)S(1)}, u32[]{:S(2)}, u32[]{:S(2)}) collective-permute-start(bf16[256,512]{1,0:T(8,128)(2,1)S(1)} %shard_map.127), channel_id=1, source_target_pairs={{0,6},{1,7},{2,4},{3,5},{4,10},{5,11},{6,8},{7,9},{8,14},{9,15},{1... | collective-permute-start | bytes 786440 | tf_op jit(solution)/shard_map/ppermute | solution.py:218
  38.7 9.7 %all-gather.3.cloned.1.call-done = bf16[1088,512]{1,0:T(8,128)(2,1)} async-done(((bf16[272,512]{1,0:T(8,128)(2,1)}), bf16[1088,512]{1,0:T(8,128)(2,1)}) %all-gather.3.cloned.1.call-update) | async-done | bytes 1114128 | tf_op jit(solution)/shard_map/all_gather | solution.py:290
  48.4 2.4 slice.73
  52.0 2.3 fusion.25
  55.9 15.7 %all-to-all-start = ((bf16[8,32,4,1024]{3,1,2,0:T(8,128)(2,1)}), bf16[8,32,4,1024]{3,1,2,0:T(8,128)(2,1)}, u32[]{:S(2)}, u32[]{:S(2)}) async-start(bf16[8,32,4,1024]{3,1,2,0:T(8,128)(2,1)} %copy.25), calls=%async_computation | async-start | bytes 4194304 | tf_op jit(solution)/shard_map/all_to_all | solution.py:323
  73.4 3.4 %fusion.98.query_ref = f32[256,1024]{1,0:T(8,128)S(1)} fusion(bf16[256,2048]{1,0:T(8,128)(2,1)S(1)} %fusion.15.rows_ref, bf16[2048,1024]{1,0:T(8,128)(2,1)} %param.16), kind=kOutput, calls=%fused_computation.137 | convolution fusion | flops 1073741824 | bytes 6291456 | tf_op jit(solution)/shard_map/dot_general | solution.py:299
  76.9 15.0 %shard_map.128 = bf16[256,1024]{1,0:T(8,128)(2,1)S(1)} custom-call(s32[9]{0:T(128)S(1)} %compare_convert_fusion.valid_ref, f32[8]{0:T(128)S(1)} %copy-done.3, f32[256,1024]{1,0:T(8,128)S(1)} %fusion.98.query_ref, bf16[1,256,512]{2,1,0:T(8,128)(2,1)S(1)} %bitcast.73, bf16[1,256,512]{2,1,0:T(8,128)(2,1)S(1)} %bitcast.74, bf16[1,256,512]{2,1,0:T(8,128)(2,1)S(1)} %bitcast.76, ...), custom_call_target="tpu_custom_call" | custom-call | flops 3623878656 | bytes 3932160 | tf_op jit(solution)/shard_map/pallas_call | solution.py:182
  93.3 5.1 %all-to-all-done = bf16[8,32,4,1024]{3,1,2,0:T(8,128)(2,1)} async-done(((bf16[8,32,4,1024]{3,1,2,0:T(8,128)(2,1)}), bf16[8,32,4,1024]{3,1,2,0:T(8,128)(2,1)}, u32[]{:S(2)}, u32[]{:S(2)}) %all-to-all-start) | async-done | bytes 2097184 | tf_op jit(solution)/shard_map/all_to_all | solution.py:323
  98.4 3.1 %all-to-all-start.3 = ((bf16[32,16,1024]{2,1,0:T(8,128)(2,1)}), bf16[32,16,1024]{2,1,0:T(8,128)(2,1)S(1)}, u32[]{:S(2)}, u32[]{:S(2)}) async-start(bf16[32,16,1024]{2,1,0:T(8,128)(2,1)} %bitcast.34), calls=%async_computation.3 | async-start | bytes 2097152 | tf_op jit(solution)/shard_map/all_to_all | solution.py:269
  103.0 1.8 copy.26
  106.2 21.5 %all-to-all-done.3 = bf16[32,16,1024]{2,1,0:T(8,128)(2,1)S(1)} async-done(((bf16[32,16,1024]{2,1,0:T(8,128)(2,1)}), bf16[32,16,1024]{2,1,0:T(8,128)(2,1)S(1)}, u32[]{:S(2)}, u32[]{:S(2)}) %all-to-all-start.3) | async-done | bytes 1048608 | tf_op jit(solution)/shard_map/all_to_all | solution.py:269
  127.8 3.8 %all-to-all-start.1 = ((bf16[32,16,1024]{2,1,0:T(8,128)(2,1)}), bf16[32,16,1024]{2,1,0:T(8,128)(2,1)S(1)}, u32[]{:S(2)}, u32[]{:S(2)}) async-start(bf16[32,16,1024]{2,1,0:T(8,128)(2,1)} %bitcast.26), calls=%async_computation.1 | async-start | bytes 2097152 | tf_op jit(solution)/shard_map/all_to_all | solution.py:269
  131.6 5.0 %convolution_convert_fusion = bf16[512,2048]{1,0:T(8,128)(2,1)S(1)} fusion(bf16[512,1024]{1,0:T(8,128)(2,1)} %bitcast.94, bf16[1024,2048]{1,0:T(8,128)(2,1)} %param.14), kind=kOutput, calls=%fused_computation.8 | convolution fusion | flops 2148532224 | bytes 7340032 | tf_op jit(solution)/shard_map/dot_general | solution.py:333
  136.6 2.4 add_convert_fusion.mid_ref
  139.0 19.9 %shard_map.130 = bf16[512,2048]{1,0:T(8,128)(2,1)} custom-call(bf16[512,2048]{1,0:T(8,128)(2,1)S(1)} %add_convert_fusion.mid_ref, f32[1,2048]{1,0:T(1,128)S(1)} %bitcast.81, bf16[2,2816,2048]{2,1,0:T(8,128)(2,1)} %w_in_ref.3, bf16[2816,2048]{1,0:T(8,128)(2,1)} %w_out_ref.3), custom_call_target="tpu_custom_call" | custom-call | flops 8858370048 | bytes 21495808 | tf_op jit(solution)/shard_map/pallas_call | solution.py:71
  159.9 5.9 %all-to-all-start.4 = ((bf16[32,16,2048]{2,1,0:T(8,128)(2,1)}), bf16[32,16,2048]{2,1,0:T(8,128)(2,1)S(1)}, u32[]{:S(2)}, u32[]{:S(2)}) async-start(bf16[32,16,2048]{2,1,0:T(8,128)(2,1)} %bitcast.36), calls=%async_computation.4 | async-start | bytes 4194304 | tf_op jit(solution)/shard_map/all_to_all | solution.py:269
  165.8 5.0 %convolution_convert_fusion.1 = bf16[512,2048]{1,0:T(8,128)(2,1)S(1)} fusion(bf16[512,1024]{1,0:T(8,128)(2,1)} %bitcast.93, bf16[1024,2048]{1,0:T(8,128)(2,1)} %param.14), kind=kOutput, calls=%fused_computation.9 | convolution fusion | flops 2148532224 | bytes 7340032 | tf_op jit(solution)/shard_map/dot_general | solution.py:333
  170.8 2.4 add_convert_fusion.1.mid_ref
  173.2 19.8 %shard_map.129 = bf16[512,2048]{1,0:T(8,128)(2,1)} custom-call(bf16[512,2048]{1,0:T(8,128)(2,1)S(1)} %add_convert_fusion.1.mid_ref, f32[1,2048]{1,0:T(1,128)S(1)} %bitcast.82, bf16[2,2816,2048]{2,1,0:T(8,128)(2,1)} %w_in_ref.3, bf16[2816,2048]{1,0:T(8,128)(2,1)} %w_out_ref.3), custom_call_target="tpu_custom_call" | custom-call | flops 8858370048 | bytes 21495808 | tf_op jit(solution)/shard_map/pallas_call | solution.py:71
  193.0 21.5 %all-to-all-done.4 = bf16[32,16,2048]{2,1,0:T(8,128)(2,1)S(1)} async-done(((bf16[32,16,2048]{2,1,0:T(8,128)(2,1)}), bf16[32,16,2048]{2,1,0:T(8,128)(2,1)S(1)}, u32[]{:S(2)}, u32[]{:S(2)}) %all-to-all-start.4) | async-done | bytes 2097184 | tf_op jit(solution)/shard_map/all_to_all | solution.py:269
  214.5 4.3 %all-to-all-start.2 = ((bf16[32,16,2048]{2,1,0:T(8,128)(2,1)}), bf16[32,16,2048]{2,1,0:T(8,128)(2,1)}, u32[]{:S(2)}, u32[]{:S(2)}) async-start(bf16[32,16,2048]{2,1,0:T(8,128)(2,1)} %bitcast.29), calls=%async_computation.2 | async-start | bytes 4194304 | tf_op jit(solution)/shard_map/all_to_all | solution.py:269
  218.8 3.9 %fusion.16 = (f32[256]{0:T(256)S(1)}, bf16[256,2048]{1,0:T(8,128)(2,1)S(1)}) fusion(bf16[256,1024]{1,0:T(8,128)(2,1)S(1)} %shard_map.128, bf16[1024,2048]{1,0:T(8,128)(2,1)} %param.18, bf16[256,2048]{1,0:T(8,128)(2,1)} %copy-done.10), kind=kOutput, calls=%fused_computation.31 | convolution fusion | flops 1076887296 | bytes 6816768 | tf_op jit(solution)/shard_map/dot_general | solution.py:350
  223.8 2.1 fusion.11
  225.9 2.2 fusion.9
  228.1 39.5 %all-to-all-done.2 = bf16[32,16,2048]{2,1,0:T(8,128)(2,1)} async-done(((bf16[32,16,2048]{2,1,0:T(8,128)(2,1)}), bf16[32,16,2048]{2,1,0:T(8,128)(2,1)}, u32[]{:S(2)}, u32[]{:S(2)}) %all-to-all-start.2) | async-done | bytes 2097184 | tf_op jit(solution)/shard_map/all_to_all | solution.py:269
  267.6 2.5 fusion.7
  270.4 3.9 %fusion.5 = bf16[256,2048]{1,0:T(8,128)(2,1)} fusion(f32[256,2048]{1,0:T(8,128)S(1)} %copy-done.4, f32[256,2048]{1,0:T(8,128)S(1)} %copy-done.5, f32[256,2048]{1,0:T(8,128)S(1)} %fusion.7, bf16[512,2048]{1,0:T(8,128)(2,1)} %bitcast.30, bf16[256,2048]{1,0:T(8,128)(2,1)} %copy-done.7, f32[256]{0:T(256)S(1)} %bitcast.107, s32[512]{0:T(512)S(1)} %fusion.86, ...), kind=kOutput, calls=%fused_computation.19 | convolution fusion | flops 541720576 | bytes 10489856 | tf_op jit(solution)/shard_map/dot_general | solution.py:362
  (74 shorter events, 17.5 us)
Async XLA Ops:
  6.5 216.2 %copy-start = (bf16[2048,64]{0,1:T(8,128)(2,1)S(1)}, bf16[2048,64]{0,1:T(8,128)(2,1)}, u32[]{:S(2)}) copy-start(bf16[2048,64]{0,1:T(8,128)(2,1)} %param.21) | copy-start | bytes 786436
  6.5 41.9 %all-gather.3.cloned.1.call-start = ((), (), s32[]{:S(2)}) async-start(), calls=%async_computation.5 | async-start | bytes 1392640 | tf_op jit(solution)/shard_map/all_gather | solution.py:290
  7.3 3.2 %collective-permute-start = (bf16[1,512]{1,0:T(2,128)(2,1)S(1)}, bf16[1,512]{1,0:T(2,128)(2,1)S(1)}, u32[]{:S(2)}, u32[]{:S(2)}) collective-permute-start(bf16[1,512]{1,0:T(2,128)(2,1)S(1)} %slice.54), channel_id=1, source_target_pairs={{0,1},{1,2},{2,3},{3,4},{4,5},{5,6},{6,7},{7,8},{8,9},{9,10},{10,1... | collective-permute-start | bytes 3080 | tf_op jit(solution)/shard_map/ppermute | solution.py:22
  12.4 3.8 %copy-start.11 = (f32[2048]{0:T(1024)S(1)}, f32[2048]{0:T(1024)}, u32[]{:S(2)}) copy-start(f32[2048]{0:T(1024)} %param.15) | copy-start | bytes 24580
  16.1 2.8 copy-start.10
  16.2 2.0 copy-start.1
  19.0 52.7 %collective-permute-start.1 = (bf16[256,512]{1,0:T(8,128)(2,1)S(1)}, bf16[256,512]{1,0:T(8,128)(2,1)S(1)}, u32[]{:S(2)}, u32[]{:S(2)}) collective-permute-start(bf16[256,512]{1,0:T(8,128)(2,1)S(1)} %shard_map.127), channel_id=1, source_target_pairs={{0,8},{1,9},{2,10},{3,11},{4,12},{5,13},{6,14},{7,15},{8,16},{9,17... | collective-permute-start | bytes 786440 | tf_op jit(solution)/shard_map/ppermute | solution.py:22
  27.4 44.3 %collective-permute-start.2 = (bf16[256,512]{1,0:T(8,128)(2,1)S(1)}, bf16[256,512]{1,0:T(8,128)(2,1)S(1)}, u32[]{:S(2)}, u32[]{:S(2)}) collective-permute-start(bf16[256,512]{1,0:T(8,128)(2,1)S(1)} %shard_map.127), channel_id=1, source_target_pairs={{0,2},{1,3},{2,8},{3,9},{4,6},{5,7},{6,12},{7,13},{8,10},{9,11},{1... | collective-permute-start | bytes 786440 | tf_op jit(solution)/shard_map/ppermute | solution.py:218
  29.0 42.6 %collective-permute-start.3 = (bf16[256,512]{1,0:T(8,128)(2,1)S(1)}, bf16[256,512]{1,0:T(8,128)(2,1)S(1)}, u32[]{:S(2)}, u32[]{:S(2)}) collective-permute-start(bf16[256,512]{1,0:T(8,128)(2,1)S(1)} %shard_map.127), channel_id=1, source_target_pairs={{0,4},{1,5},{2,6},{3,7},{4,8},{5,9},{6,10},{7,11},{8,12},{9,13},{1... | collective-permute-start | bytes 786440 | tf_op jit(solution)/shard_map/ppermute | solution.py:218
  32.5 39.2 %collective-permute-start.4 = (bf16[256,512]{1,0:T(8,128)(2,1)S(1)}, bf16[256,512]{1,0:T(8,128)(2,1)S(1)}, u32[]{:S(2)}, u32[]{:S(2)}) collective-permute-start(bf16[256,512]{1,0:T(8,128)(2,1)S(1)} %shard_map.127), channel_id=1, source_target_pairs={{0,6},{1,7},{2,4},{3,5},{4,10},{5,11},{6,8},{7,9},{8,14},{9,15},{1... | collective-permute-start | bytes 786440 | tf_op jit(solution)/shard_map/ppermute | solution.py:218
  48.4 2.4 copy-start.6
  55.9 42.4 %all-to-all-start = ((bf16[8,32,4,1024]{3,1,2,0:T(8,128)(2,1)}), bf16[8,32,4,1024]{3,1,2,0:T(8,128)(2,1)}, u32[]{:S(2)}, u32[]{:S(2)}) async-start(bf16[8,32,4,1024]{3,1,2,0:T(8,128)(2,1)} %copy.25), calls=%async_computation | async-start | bytes 4194304 | tf_op jit(solution)/shard_map/all_to_all | solution.py:323
  72.8 4.1 %collective-permute-start.5 = (bf16[4,256,512]{2,1,0:T(8,128)(2,1)}, bf16[4,256,512]{2,1,0:T(8,128)(2,1)}, u32[]{:S(2)}, u32[]{:S(2)}) collective-permute-start(bf16[4,256,512]{2,1,0:T(8,128)(2,1)} %pad_maximum_fusion), channel_id=1, source_target_pairs={{0,1},{1,0},{2,3},{3,2},{4,5},{5,4},{6,7},{7,6},{8,9},{9,8},{10,11... | collective-permute-start | bytes 3145736 | tf_op jit(solution)/shard_map/ppermute | solution.py:220
  73.4 3.5 %copy-start.3 = (f32[8]{0:T(128)S(1)}, f32[8]{0:T(128)}, u32[]{:S(2)}) copy-start(f32[8]{0:T(128)} %scale_ref.1) | copy-start | bytes 100
  98.4 29.4 %all-to-all-start.3 = ((bf16[32,16,1024]{2,1,0:T(8,128)(2,1)}), bf16[32,16,1024]{2,1,0:T(8,128)(2,1)S(1)}, u32[]{:S(2)}, u32[]{:S(2)}) async-start(bf16[32,16,1024]{2,1,0:T(8,128)(2,1)} %bitcast.34), calls=%async_computation.3 | async-start | bytes 2097152 | tf_op jit(solution)/shard_map/all_to_all | solution.py:269
  127.8 31.1 %all-to-all-start.1 = ((bf16[32,16,1024]{2,1,0:T(8,128)(2,1)}), bf16[32,16,1024]{2,1,0:T(8,128)(2,1)S(1)}, u32[]{:S(2)}, u32[]{:S(2)}) async-start(bf16[32,16,1024]{2,1,0:T(8,128)(2,1)} %bitcast.26), calls=%async_computation.1 | async-start | bytes 2097152 | tf_op jit(solution)/shard_map/all_to_all | solution.py:269
  131.6 5.0 %copy-start.13 = (bf16[1024,2048]{1,0:T(8,128)(2,1)S(1)}, bf16[1024,2048]{1,0:T(8,128)(2,1)}, u32[]{:S(2)}) copy-start(bf16[1024,2048]{1,0:T(8,128)(2,1)} %param.18) | copy-start | bytes 12582916
  136.6 2.4 copy-start.2
  158.9 1.0 copy-start.8
  159.9 54.6 %all-to-all-start.4 = ((bf16[32,16,2048]{2,1,0:T(8,128)(2,1)}), bf16[32,16,2048]{2,1,0:T(8,128)(2,1)S(1)}, u32[]{:S(2)}, u32[]{:S(2)}) async-start(bf16[32,16,2048]{2,1,0:T(8,128)(2,1)} %bitcast.36), calls=%async_computation.4 | async-start | bytes 4194304 | tf_op jit(solution)/shard_map/all_to_all | solution.py:269
  165.7 5.0 %copy-start.9 = (bf16[32,16,1024]{2,1,0:T(8,128)(2,1)S(1)}, bf16[32,16,1024]{2,1,0:T(8,128)(2,1)}, u32[]{:S(2)}) copy-start(bf16[32,16,1024]{2,1,0:T(8,128)(2,1)} %copy-done.8) | copy-start | bytes 3145732
  165.8 5.0 %copy-start.14 = (bf16[1024,2048]{1,0:T(8,128)(2,1)S(1)}, bf16[1024,2048]{1,0:T(8,128)(2,1)}, u32[]{:S(2)}) copy-start(bf16[1024,2048]{1,0:T(8,128)(2,1)} %param.18) | copy-start | bytes 12582916
  214.5 53.1 %all-to-all-start.2 = ((bf16[32,16,2048]{2,1,0:T(8,128)(2,1)}), bf16[32,16,2048]{2,1,0:T(8,128)(2,1)}, u32[]{:S(2)}, u32[]{:S(2)}) async-start(bf16[32,16,2048]{2,1,0:T(8,128)(2,1)} %bitcast.29), calls=%async_computation.2 | async-start | bytes 4194304 | tf_op jit(solution)/shard_map/all_to_all | solution.py:269
  222.7 1.0 copy-start.7
  222.7 1.0 copy-start.12
  267.6 2.5 copy-start.4
  267.6 2.9 %copy-start.5 = (f32[256,2048]{1,0:T(8,128)S(1)}, f32[256,2048]{1,0:T(8,128)}, u32[]{:S(2)}) copy-start(f32[256,2048]{1,0:T(8,128)} %fusion.9) | copy-start | bytes 6291460
Sparse Core Ops, SparseCore 0:
  12.3 36.0 all-gather.2

commit v2 on v1

--- a/solution.py
+++ b/solution.py
@@ -270,7 +270,6 @@
 
     reach_blocks = WINDOW // row_count
     group = reach_blocks
-    lines = devices // group
     before = from_behind(signal[row_count - 1 :], "tm", 1)
     previous = jnp.concatenate([before, signal[:-1]], axis=0)
     patch_pairs = jnp.concatenate([previous, signal], axis=1)
@@ -286,8 +285,8 @@
     )
     used = ahead.shape[0]
     ahead = jnp.pad(ahead, ((0, -used % 16), (0, 0)))
-    line_groups = [[row * group + place for row in range(lines)] for place in range(group)]
-    gathered = lax.all_gather(ahead, "tm", axis_index_groups=line_groups)
+    half = devices // 2
+    far = lax.ppermute(ahead, "tm", [(dev, (dev + half) % devices) for dev in range(devices)])
 
     embedded = jnp.dot(patch_pairs, conv_weight, preferred_element_type=jnp.float32).astype(
         jnp.bfloat16
@@ -299,31 +298,42 @@
     queries = jnp.dot(normed, w_query, preferred_element_type=jnp.float32)
     context = attend((numbers >= 0).astype(jnp.int32), head_scale, queries, kv_parts, kv_heads)
 
-    line_signal = gathered[:, :row_count]
-    line_before = gathered[:, row_count : row_count + 1]
-    line_previous = jnp.concatenate([line_before, line_signal[:, :-1]], axis=1)
-    line_pairs = jnp.concatenate([line_previous, line_signal], axis=2)
+    far, _ = lax.optimization_barrier((far, own_kv))
+    in_first = dev_index < half
+    both = jnp.stack([jnp.where(in_first, ahead, far), jnp.where(in_first, far, ahead)])
+    both_signal = both[:, :row_count]
+    both_before = both[:, row_count : row_count + 1]
+    both_previous = jnp.concatenate([both_before, both_signal[:, :-1]], axis=1)
+    both_pairs = jnp.concatenate([both_previous, both_signal], axis=2)
+    both_pairs = both_pairs.reshape(2 * row_count, -1)
     id_rows = (used - row_count - 1) // 2
-    line_ids = gathered[:, row_count + 1 : row_count + 1 + id_rows].astype(jnp.int32)
-    line_slots = gathered[:, row_count + 1 + id_rows : used].astype(jnp.int32)
-    line_keys = (line_ids * CAP + line_slots).reshape(lines, 2, 1, row_count)
-    near_dev = dev_index // group * group + jnp.arange(group, dtype=jnp.int32)
-    near_expert = (near_dev // copies * local_count)[:, None] + jnp.arange(
-        local_count, dtype=jnp.int32
-    )
-    near_keys = near_expert[:, :, None] * CAP + jnp.arange(CAP, dtype=jnp.int32)
-    near_keys = near_keys.reshape(1, -1, 1)
-    line_hot = (near_keys == line_keys[:, 0]) | (near_keys == line_keys[:, 1])
-    pairs_out = jnp.einsum(
-        "lrt,ltf->rlf", line_hot.astype(jnp.bfloat16), line_pairs,
-        preferred_element_type=jnp.float32,
+    both_ids = both[:, row_count + 1 : row_count + 1 + id_rows].astype(jnp.int32)
+    both_slots = both[:, row_count + 1 + id_rows : used].astype(jnp.int32)
+    both_keys = (both_ids * CAP + both_slots).reshape(2, 2, row_count)
+    span = experts * CAP
+    both_keys = both_keys + span * jnp.arange(2, dtype=jnp.int32)[:, None, None]
+    both_keys = both_keys.transpose(1, 0, 2).reshape(2, 1, 2 * row_count)
+    place = jnp.arange(half * 2 * local_count * CAP, dtype=jnp.int32)
+    place_slot = place % CAP
+    place_local = place // CAP % local_count
+    place_block = place // (CAP * local_count) % 2
+    place_dev = place // (CAP * local_count * 2) + jnp.where(in_first, 0, half)
+    place_key = (place_dev // copies * local_count + place_local) * CAP + place_slot
+    place_key = (place_key + span * place_block)[:, None]
+    both_hot = (place_key == both_keys[0]) | (place_key == both_keys[1])
+    pairs_out = jnp.dot(
+        both_hot.astype(jnp.bfloat16), both_pairs, preferred_element_type=jnp.float32
     ).astype(jnp.bfloat16)
-    pairs_out = pairs_out.reshape(group, local_count * CAP, lines, -1)
-    near_groups = [[row * group + place for place in range(group)] for row in range(lines)]
+    pairs_out, _ = lax.optimization_barrier((pairs_out, kv_parts[1:-1]))
     pairs_in = lax.all_to_all(
-        pairs_out, "tm", split_axis=0, concat_axis=0, axis_index_groups=near_groups, tiled=True
-    )
-    pairs_in = pairs_in.transpose(2, 0, 1, 3).reshape(devices, local_count * CAP, -1)
+        pairs_out.reshape(half, 2 * local_count * CAP, -1),
+        "tm",
+        split_axis=0,
+        concat_axis=0,
+        axis_index_groups=[list(range(half)), list(range(half, devices))],
+        tiled=True,
+    )
+    pairs_in = pairs_in.reshape(half, 2, local_count, CAP, -1)
 
     context_in = [
         exchange(spread(context, local).reshape(devices, CAP, -1)) for local in range(local_count)
@@ -340,7 +350,7 @@
 
     returned = []
     for local in range(local_count):
-        pairs = pairs_in[:, local * CAP : (local + 1) * CAP].reshape(slots, -1)
+        pairs = pairs_in[:, :, local].transpose(1, 0, 2, 3).reshape(slots, -1)
         contexts = context_in[local].reshape(slots, -1)
         mid = mid_of(pairs, contexts)
         result = run_expert(mid, ffn_gain, expert_in, expert_out, local, local_count)

time: 282 us -> 262 us (0.929)
  between operations: 13.9 us -> 0.47 us
  waiting for transfers between devices: 97.4 us -> 89.1 us
  local copies, waits for them, and re-layouts: 12.7 us -> 9.36 us
  starting transfers between devices: 55.4 us -> 58.5 us
    all_gather x1 -> x0, waiting for transfers between devices: 9.74 us -> none  [shards(): gathered = lax.all_gather(ahead, 'tm', axis_index_groups=line_groups)]
    ppermute x0 -> x1, starting transfers between devices: none -> 7.6 us  [shards(): lax.ppermute(ahead, 'tm', [(dev, (dev + half) % devices) for dev in range...]
    transpose x0 -> x3, local copies, waits for them, and re-layouts: none -> 5.08 us  [shards(): pairs = pairs_in[:, :, local].transpose(1, 0, 2, 3).reshape(slots, -1)]
    ppermute x2, starting transfers between devices: 10.8 us -> 5.85 us  [from_behind(): return lax.ppermute(block, axis, route)]
    slice x5 -> x1, local copies, waits for them, and re-layouts: 4.96 us -> 0.01 us  [shards(): both_hot = (place_key == both_keys[0]) | (place_key == both_keys[1])]
    all_to_all x4, starting transfers between devices: 17.1 us -> 21.9 us  [exchange(): return lax.all_to_all(rows, 'tm', split_axis=0, concat_axis=0, tiled=True)]
  transfers between devices with their start and end apart: 12 -> 12, of which waited for: 5 -> 5; matrix products, arithmetic and copies ran while one was open for 17% -> 18% of each run, Pallas kernels for 20% -> 21%
where the time goes in v2:
time: 262 us; the launch traced here: 261 us
  waiting for transfers between devices  89.1 us (34%)
  starting transfers between devices  58.5 us (22%)
  Pallas kernels  55.4 us (21%)
  matrix products  43.5 us (17%)
  local copies, waits for them, and re-layouts  9.36 us (4%)
  other arithmetic  4.69 us (2%)
    all_to_all x4, waiting for transfers between devices, exchange(): return lax.all_to_all(rows, 'tm', split_axis=0, concat_axis=0, tiled=True)  81 us
    pallas_call x2, Pallas kernels, run_expert(): pl.pallas_call(functools.partial(expert_body, steps), grid=(row_total //...  39.6 us
    all_to_all x4, starting transfers between devices, exchange(): return lax.all_to_all(rows, 'tm', split_axis=0, concat_axis=0, tiled=True)  21.9 us
    pallas_call x1, Pallas kernels, attend(): pl.pallas_call(functools.partial(attend_body, kv_heads), out_shape=jax.Sh...  15 us
    all_to_all x1, starting transfers between devices, shards(): lax.all_to_all(pairs_out.reshape(half, 2 * local_count * CAP, -1), 'tm',...  13.8 us
    dot_general x4, matrix products, shards(): jnp.dot(hot.astype(jnp.bfloat16), returned[local], preferred_element_type...  10.7 us
    dot_general x2, matrix products, mid_of(): jnp.dot(pairs, conv_weight, preferred_element_type=jnp.float32)  9.68 us
    ppermute x3, starting transfers between devices, window_parts(): fetched.append((lax.ppermute(own_kv, 'tm', route), start))  8.98 us
  transfers between devices with their start and end apart: 12, of which 5 were waited for; matrix products, arithmetic and copies ran while one was open for 18% of the time, Pallas kernels for 21%

profile of v2, /device:TPU:0, one launch (start us, length us, event | category | flops | bytes accessed | tf_op | source)
XLA Modules:
  0.0 261.0 jit_solution(16295053385009894530)
XLA Ops:
  0.7 2.3 collective-permute-start
  4.9 7.6 %collective-permute-start.6 = (bf16[272,512]{1,0:T(8,128)(2,1)S(1)}, bf16[272,512]{1,0:T(8,128)(2,1)S(1)}, u32[]{:S(2)}, u32[]{:S(2)}) collective-permute-start(bf16[272,512]{1,0:T(8,128)(2,1)S(1)} %fusion.65), channel_id=1, source_target_pairs={{0,16},{1,17},{2,18},{3,19},{4,20},{5,21},{6,22},{7,23},{8,24},{9,... | collective-permute-start | bytes 835592 | tf_op jit(solution)/shard_map/ppermute | solution.py:289
  12.5 3.7 %fusion.13 = (f32[256]{0:T(256)S(1)}, bf16[256,2048]{1,0:T(8,128)(2,1)S(1)}) fusion(bf16[1024,2048]{1,0:T(8,128)(2,1)} %param.14, bf16[256,512]{1,0:T(8,128)(2,1)} %param.13, bf16[255,512]{1,0:T(8,128)(2,1)} %bitcast.95, bf16[1,512]{1,0:T(2,128)(2,1)S(1)} %collective-permute-done), kind=kOutput, calls=%fused_computation.28 | convolution fusion | flops 1077411584 | bytes 5768192 | tf_op jit(solution)/shard_map/dot_general | solution.py:291
  16.6 1.6 copy-done.1
  19.0 3.5 %collective-permute-start.1 = (bf16[256,512]{1,0:T(8,128)(2,1)S(1)}, bf16[256,512]{1,0:T(8,128)(2,1)S(1)}, u32[]{:S(2)}, u32[]{:S(2)}) collective-permute-start(bf16[256,512]{1,0:T(8,128)(2,1)S(1)} %shard_map.127), channel_id=1, source_target_pairs={{0,8},{1,9},{2,10},{3,11},{4,12},{5,13},{6,14},{7,15},{8,16},{9,17... | collective-permute-start | bytes 786440 | tf_op jit(solution)/shard_map/ppermute | solution.py:22
  22.6 1.6 collective-permute-start.2
  24.2 3.4 %collective-permute-start.3 = (bf16[256,512]{1,0:T(8,128)(2,1)S(1)}, bf16[256,512]{1,0:T(8,128)(2,1)S(1)}, u32[]{:S(2)}, u32[]{:S(2)}) collective-permute-start(bf16[256,512]{1,0:T(8,128)(2,1)S(1)} %shard_map.127), channel_id=1, source_target_pairs={{0,4},{1,5},{2,6},{3,7},{4,8},{5,9},{6,10},{7,11},{8,12},{9,13},{1... | collective-permute-start | bytes 786440 | tf_op jit(solution)/shard_map/ppermute | solution.py:218
  27.6 3.9 %collective-permute-start.4 = (bf16[256,512]{1,0:T(8,128)(2,1)S(1)}, bf16[256,512]{1,0:T(8,128)(2,1)S(1)}, u32[]{:S(2)}, u32[]{:S(2)}) collective-permute-start(bf16[256,512]{1,0:T(8,128)(2,1)S(1)} %shard_map.127), channel_id=1, source_target_pairs={{0,6},{1,7},{2,4},{3,5},{4,10},{5,11},{6,8},{7,9},{8,14},{9,15},{1... | collective-permute-start | bytes 786440 | tf_op jit(solution)/shard_map/ppermute | solution.py:218
  33.0 3.8 %fusion.26 = bf16[1024,1024]{1,0:T(8,128)(2,1)} fusion(bf16[512,1024]{1,0:T(8,128)(2,1)} %bitcast.98, s32[512]{0:T(512)S(1)} %bitcast.118, s32[512]{0:T(512)S(1)} %bitcast.117, s32[1024]{0:T(1024)S(1)} %fusion.89), kind=kOutput, calls=%fused_computation.43 | convolution fusion | flops 1076363264 | bytes 3153920 | tf_op jit(solution)/shard_map/dot_general | solution.py:324
  37.1 13.8 %all-to-all-start = ((bf16[16,64,1024]{2,1,0:T(8,128)(2,1)}), bf16[16,64,1024]{2,1,0:T(8,128)(2,1)}, u32[]{:S(2)}, u32[]{:S(2)}) async-start(bf16[16,64,1024]{2,1,0:T(8,128)(2,1)} %bitcast.94), calls=%async_computation | async-start | bytes 4194304 | tf_op jit(solution)/shard_map/all_to_all | solution.py:328
  52.5 3.4 %fusion.118.query_ref = f32[256,1024]{1,0:T(8,128)S(1)} fusion(bf16[256,2048]{1,0:T(8,128)(2,1)S(1)} %fusion.15.rows_ref, bf16[2048,1024]{1,0:T(8,128)(2,1)} %param.16), kind=kOutput, calls=%fused_computation.180 | convolution fusion | flops 1073741824 | bytes 6291456 | tf_op jit(solution)/shard_map/dot_general | solution.py:298
  56.0 15.0 %shard_map.128 = bf16[256,1024]{1,0:T(8,128)(2,1)S(1)} custom-call(s32[9]{0:T(128)S(1)} %compare_convert_fusion.valid_ref, f32[8]{0:T(128)S(1)} %copy-done.3, f32[256,1024]{1,0:T(8,128)S(1)} %fusion.118.query_ref, bf16[1,256,512]{2,1,0:T(8,128)(2,1)S(1)} %bitcast.82, bf16[1,256,512]{2,1,0:T(8,128)(2,1)S(1)} %bitcast.83, bf16[1,256,512]{2,1,0:T(8,128)(2,1)S(1)} %bitcast.85, ...), custom_call_target="tpu_custom_call" | custom-call | flops 3623878656 | bytes 3932160 | tf_op jit(solution)/shard_map/pallas_call | solution.py:182
  72.4 7.9 %all-to-all-done = bf16[16,64,1024]{2,1,0:T(8,128)(2,1)} async-done(((bf16[16,64,1024]{2,1,0:T(8,128)(2,1)}), bf16[16,64,1024]{2,1,0:T(8,128)(2,1)}, u32[]{:S(2)}, u32[]{:S(2)}) %all-to-all-start) | async-done | bytes 2097184 | tf_op jit(solution)/shard_map/all_to_all | solution.py:328
  80.3 7.9 %all-to-all-start.3 = ((bf16[32,16,1024]{2,1,0:T(8,128)(2,1)}), bf16[32,16,1024]{2,1,0:T(8,128)(2,1)S(1)}, u32[]{:S(2)}, u32[]{:S(2)}) async-start(bf16[32,16,1024]{2,1,0:T(8,128)(2,1)} %bitcast.40), calls=%async_computation.3 | async-start | bytes 2097152 | tf_op jit(solution)/shard_map/all_to_all | solution.py:269
  89.7 2.7 %slice_bitcast_fusion.1 = (bf16[2,16,16,1024]{3,2,0,1:T(8,128)(2,1)}, bf16[2,16,16,1024]{3,2,0,1:T(8,128)(2,1)S(1)}) fusion(bf16[16,2,2,16,1024]{4,3,2,1,0:T(8,128)(2,1)} %bitcast.26), kind=kLoop, calls=%fused_computation.56 | loop fusion | bytes 4194304 | tf_op jit(solution)/shard_map/transpose | solution.py:353
  93.5 21.0 %all-to-all-done.3 = bf16[32,16,1024]{2,1,0:T(8,128)(2,1)S(1)} async-done(((bf16[32,16,1024]{2,1,0:T(8,128)(2,1)}), bf16[32,16,1024]{2,1,0:T(8,128)(2,1)S(1)}, u32[]{:S(2)}, u32[]{:S(2)}) %all-to-all-start.3) | async-done | bytes 1048608 | tf_op jit(solution)/shard_map/all_to_all | solution.py:269
  114.5 3.8 %all-to-all-start.1 = ((bf16[32,16,1024]{2,1,0:T(8,128)(2,1)}), bf16[32,16,1024]{2,1,0:T(8,128)(2,1)S(1)}, u32[]{:S(2)}, u32[]{:S(2)}) async-start(bf16[32,16,1024]{2,1,0:T(8,128)(2,1)} %bitcast.31), calls=%async_computation.1 | async-start | bytes 2097152 | tf_op jit(solution)/shard_map/all_to_all | solution.py:269
  118.3 5.0 %convolution_convert_fusion = bf16[512,2048]{1,0:T(8,128)(2,1)S(1)} fusion(bf16[512,1024]{1,0:T(8,128)(2,1)} %bitcast.99, bf16[1024,2048]{1,0:T(8,128)(2,1)} %param.14), kind=kOutput, calls=%fused_computation.8 | convolution fusion | flops 2148532224 | bytes 7340032 | tf_op jit(solution)/shard_map/dot_general | solution.py:343
  123.3 2.4 add_convert_fusion.mid_ref
  125.7 19.8 %shard_map.130 = bf16[512,2048]{1,0:T(8,128)(2,1)} custom-call(bf16[512,2048]{1,0:T(8,128)(2,1)S(1)} %add_convert_fusion.mid_ref, f32[1,2048]{1,0:T(1,128)S(1)} %bitcast.90, bf16[2,2816,2048]{2,1,0:T(8,128)(2,1)} %w_in_ref.3, bf16[2816,2048]{1,0:T(8,128)(2,1)} %w_out_ref.3), custom_call_target="tpu_custom_call" | custom-call | flops 8858370048 | bytes 21495808 | tf_op jit(solution)/shard_map/pallas_call | solution.py:71
  146.5 5.9 %all-to-all-start.4 = ((bf16[32,16,2048]{2,1,0:T(8,128)(2,1)}), bf16[32,16,2048]{2,1,0:T(8,128)(2,1)S(1)}, u32[]{:S(2)}, u32[]{:S(2)}) async-start(bf16[32,16,2048]{2,1,0:T(8,128)(2,1)} %bitcast.42), calls=%async_computation.4 | async-start | bytes 4194304 | tf_op jit(solution)/shard_map/all_to_all | solution.py:269
  153.7 4.7 %convolution_convert_fusion.1 = bf16[512,2048]{1,0:T(8,128)(2,1)S(1)} fusion(bf16[512,1024]{1,0:T(8,128)(2,1)S(1)} %bitcast.100, bf16[1024,2048]{1,0:T(8,128)(2,1)} %param.14), kind=kOutput, calls=%fused_computation.9 | convolution fusion | flops 2148532224 | bytes 7340032 | tf_op jit(solution)/shard_map/dot_general | solution.py:343
  158.5 2.4 add_convert_fusion.1.mid_ref
  160.8 19.8 %shard_map.129 = bf16[512,2048]{1,0:T(8,128)(2,1)} custom-call(bf16[512,2048]{1,0:T(8,128)(2,1)S(1)} %add_convert_fusion.1.mid_ref, f32[1,2048]{1,0:T(1,128)S(1)} %bitcast.91, bf16[2,2816,2048]{2,1,0:T(8,128)(2,1)} %w_in_ref.3, bf16[2816,2048]{1,0:T(8,128)(2,1)} %w_out_ref.3), custom_call_target="tpu_custom_call" | custom-call | flops 8858370048 | bytes 21495808 | tf_op jit(solution)/shard_map/pallas_call | solution.py:71
  180.6 20.5 %all-to-all-done.4 = bf16[32,16,2048]{2,1,0:T(8,128)(2,1)S(1)} async-done(((bf16[32,16,2048]{2,1,0:T(8,128)(2,1)}), bf16[32,16,2048]{2,1,0:T(8,128)(2,1)S(1)}, u32[]{:S(2)}, u32[]{:S(2)}) %all-to-all-start.4) | async-done | bytes 2097184 | tf_op jit(solution)/shard_map/all_to_all | solution.py:269
  201.2 4.3 %all-to-all-start.2 = ((bf16[32,16,2048]{2,1,0:T(8,128)(2,1)}), bf16[32,16,2048]{2,1,0:T(8,128)(2,1)}, u32[]{:S(2)}, u32[]{:S(2)}) async-start(bf16[32,16,2048]{2,1,0:T(8,128)(2,1)} %bitcast.34), calls=%async_computation.2 | async-start | bytes 4194304 | tf_op jit(solution)/shard_map/all_to_all | solution.py:269
  205.5 3.9 %fusion.16 = (f32[256]{0:T(256)S(1)}, bf16[256,2048]{1,0:T(8,128)(2,1)S(1)}) fusion(bf16[256,1024]{1,0:T(8,128)(2,1)S(1)} %shard_map.128, bf16[1024,2048]{1,0:T(8,128)(2,1)} %param.18, bf16[256,2048]{1,0:T(8,128)(2,1)} %copy-done.10), kind=kOutput, calls=%fused_computation.31 | convolution fusion | flops 1076887296 | bytes 6816768 | tf_op jit(solution)/shard_map/dot_general | solution.py:360
  210.4 2.2 fusion.11
  212.6 2.2 fusion.9
  214.8 39.5 %all-to-all-done.2 = bf16[32,16,2048]{2,1,0:T(8,128)(2,1)} async-done(((bf16[32,16,2048]{2,1,0:T(8,128)(2,1)}), bf16[32,16,2048]{2,1,0:T(8,128)(2,1)}, u32[]{:S(2)}, u32[]{:S(2)}) %all-to-all-start.2) | async-done | bytes 2097184 | tf_op jit(solution)/shard_map/all_to_all | solution.py:269
  254.2 2.5 fusion.7
  257.1 3.9 %fusion.5 = bf16[256,2048]{1,0:T(8,128)(2,1)} fusion(f32[256,2048]{1,0:T(8,128)S(1)} %copy-done.4, f32[256,2048]{1,0:T(8,128)S(1)} %copy-done.5, f32[256,2048]{1,0:T(8,128)S(1)} %fusion.7, bf16[512,2048]{1,0:T(8,128)(2,1)} %bitcast.35, bf16[256,2048]{1,0:T(8,128)(2,1)} %copy-done.7, f32[256]{0:T(256)S(1)} %bitcast.112, s32[512]{0:T(512)S(1)} %fusion.108, ...), kind=kOutput, calls=%fused_computation.19 | convolution fusion | flops 541720576 | bytes 10489856 | tf_op jit(solution)/shard_map/dot_general | solution.py:372
  (71 shorter events, 14.5 us)
Async XLA Ops:
  0.0 209.4 %copy-start = (bf16[2048,64]{0,1:T(8,128)(2,1)S(1)}, bf16[2048,64]{0,1:T(8,128)(2,1)}, u32[]{:S(2)}) copy-start(bf16[2048,64]{0,1:T(8,128)(2,1)} %param.21) | copy-start | bytes 786436
  0.7 3.2 %collective-permute-start = (bf16[1,512]{1,0:T(2,128)(2,1)S(1)}, bf16[1,512]{1,0:T(2,128)(2,1)S(1)}, u32[]{:S(2)}, u32[]{:S(2)}) collective-permute-start(bf16[1,512]{1,0:T(2,128)(2,1)S(1)} %slice.56), channel_id=1, source_target_pairs={{0,1},{1,2},{2,3},{3,4},{4,5},{5,6},{6,7},{7,8},{8,9},{9,10},{10,1... | collective-permute-start | bytes 3080 | tf_op jit(solution)/shard_map/ppermute | solution.py:22
  4.9 26.6 %collective-permute-start.6 = (bf16[272,512]{1,0:T(8,128)(2,1)S(1)}, bf16[272,512]{1,0:T(8,128)(2,1)S(1)}, u32[]{:S(2)}, u32[]{:S(2)}) collective-permute-start(bf16[272,512]{1,0:T(8,128)(2,1)S(1)} %fusion.65), channel_id=1, source_target_pairs={{0,16},{1,17},{2,18},{3,19},{4,20},{5,21},{6,22},{7,23},{8,24},{9,... | collective-permute-start | bytes 835592 | tf_op jit(solution)/shard_map/ppermute | solution.py:289
  12.5 3.7 %copy-start.11 = (f32[2048]{0:T(1024)S(1)}, f32[2048]{0:T(1024)}, u32[]{:S(2)}) copy-start(f32[2048]{0:T(1024)} %param.15) | copy-start | bytes 24580
  16.2 2.8 %copy-start.10 = (bf16[256,2048]{1,0:T(8,128)(2,1)}, bf16[256,2048]{1,0:T(8,128)(2,1)S(1)}, u32[]{:S(2)}) copy-start(bf16[256,2048]{1,0:T(8,128)(2,1)S(1)} %get-tuple-element.25) | copy-start | bytes 3145732
  16.2 2.0 copy-start.1
  18.2 13.4 %copy-start.6 = (bf16[256,512]{1,0:T(8,128)(2,1)S(1)}, bf16[256,512]{1,0:T(8,128)(2,1)}, u32[]{:S(2)}) copy-start(bf16[256,512]{1,0:T(8,128)(2,1)} %param.13) | copy-start | bytes 786436
  19.0 17.8 %collective-permute-start.1 = (bf16[256,512]{1,0:T(8,128)(2,1)S(1)}, bf16[256,512]{1,0:T(8,128)(2,1)S(1)}, u32[]{:S(2)}, u32[]{:S(2)}) collective-permute-start(bf16[256,512]{1,0:T(8,128)(2,1)S(1)} %shard_map.127), channel_id=1, source_target_pairs={{0,8},{1,9},{2,10},{3,11},{4,12},{5,13},{6,14},{7,15},{8,16},{9,17... | collective-permute-start | bytes 786440 | tf_op jit(solution)/shard_map/ppermute | solution.py:22
  22.6 14.3 %collective-permute-start.2 = (bf16[256,512]{1,0:T(8,128)(2,1)S(1)}, bf16[256,512]{1,0:T(8,128)(2,1)S(1)}, u32[]{:S(2)}, u32[]{:S(2)}) collective-permute-start(bf16[256,512]{1,0:T(8,128)(2,1)S(1)} %shard_map.127), channel_id=1, source_target_pairs={{0,2},{1,3},{2,8},{3,9},{4,6},{5,7},{6,12},{7,13},{8,10},{9,11},{1... | collective-permute-start | bytes 786440 | tf_op jit(solution)/shard_map/ppermute | solution.py:218
  24.2 12.9 %collective-permute-start.3 = (bf16[256,512]{1,0:T(8,128)(2,1)S(1)}, bf16[256,512]{1,0:T(8,128)(2,1)S(1)}, u32[]{:S(2)}, u32[]{:S(2)}) collective-permute-start(bf16[256,512]{1,0:T(8,128)(2,1)S(1)} %shard_map.127), channel_id=1, source_target_pairs={{0,4},{1,5},{2,6},{3,7},{4,8},{5,9},{6,10},{7,11},{8,12},{9,13},{1... | collective-permute-start | bytes 786440 | tf_op jit(solution)/shard_map/ppermute | solution.py:218
  27.6 9.5 %collective-permute-start.4 = (bf16[256,512]{1,0:T(8,128)(2,1)S(1)}, bf16[256,512]{1,0:T(8,128)(2,1)S(1)}, u32[]{:S(2)}, u32[]{:S(2)}) collective-permute-start(bf16[256,512]{1,0:T(8,128)(2,1)S(1)} %shard_map.127), channel_id=1, source_target_pairs={{0,6},{1,7},{2,4},{3,5},{4,10},{5,11},{6,8},{7,9},{8,14},{9,15},{1... | collective-permute-start | bytes 786440 | tf_op jit(solution)/shard_map/ppermute | solution.py:218
  37.1 43.2 %all-to-all-start = ((bf16[16,64,1024]{2,1,0:T(8,128)(2,1)}), bf16[16,64,1024]{2,1,0:T(8,128)(2,1)}, u32[]{:S(2)}, u32[]{:S(2)}) async-start(bf16[16,64,1024]{2,1,0:T(8,128)(2,1)} %bitcast.94), calls=%async_computation | async-start | bytes 4194304 | tf_op jit(solution)/shard_map/all_to_all | solution.py:328
  52.0 3.9 %collective-permute-start.5 = (bf16[4,256,512]{2,1,0:T(8,128)(2,1)}, bf16[4,256,512]{2,1,0:T(8,128)(2,1)}, u32[]{:S(2)}, u32[]{:S(2)}) collective-permute-start(bf16[4,256,512]{2,1,0:T(8,128)(2,1)} %pad_maximum_fusion.1), channel_id=1, source_target_pairs={{0,1},{1,0},{2,3},{3,2},{4,5},{5,4},{6,7},{7,6},{8,9},{9,8},{10,11... | collective-permute-start | bytes 3145736 | tf_op jit(solution)/shard_map/ppermute | solution.py:220
  52.5 3.5 %copy-start.3 = (f32[8]{0:T(128)S(1)}, f32[8]{0:T(128)}, u32[]{:S(2)}) copy-start(f32[8]{0:T(128)} %scale_ref.1) | copy-start | bytes 100
  80.3 34.2 %all-to-all-start.3 = ((bf16[32,16,1024]{2,1,0:T(8,128)(2,1)}), bf16[32,16,1024]{2,1,0:T(8,128)(2,1)S(1)}, u32[]{:S(2)}, u32[]{:S(2)}) async-start(bf16[32,16,1024]{2,1,0:T(8,128)(2,1)} %bitcast.40), calls=%async_computation.3 | async-start | bytes 2097152 | tf_op jit(solution)/shard_map/all_to_all | solution.py:269
  114.5 31.1 %all-to-all-start.1 = ((bf16[32,16,1024]{2,1,0:T(8,128)(2,1)}), bf16[32,16,1024]{2,1,0:T(8,128)(2,1)S(1)}, u32[]{:S(2)}, u32[]{:S(2)}) async-start(bf16[32,16,1024]{2,1,0:T(8,128)(2,1)} %bitcast.31), calls=%async_computation.1 | async-start | bytes 2097152 | tf_op jit(solution)/shard_map/all_to_all | solution.py:269
  118.3 5.0 %copy-start.13 = (bf16[1024,2048]{1,0:T(8,128)(2,1)S(1)}, bf16[1024,2048]{1,0:T(8,128)(2,1)}, u32[]{:S(2)}) copy-start(bf16[1024,2048]{1,0:T(8,128)(2,1)} %param.18) | copy-start | bytes 12582916
  123.3 2.4 copy-start.2
  145.5 1.0 copy-start.8
  146.5 54.6 %all-to-all-start.4 = ((bf16[32,16,2048]{2,1,0:T(8,128)(2,1)}), bf16[32,16,2048]{2,1,0:T(8,128)(2,1)S(1)}, u32[]{:S(2)}, u32[]{:S(2)}) async-start(bf16[32,16,2048]{2,1,0:T(8,128)(2,1)} %bitcast.42), calls=%async_computation.4 | async-start | bytes 4194304 | tf_op jit(solution)/shard_map/all_to_all | solution.py:269
  153.7 4.7 %copy-start.9 = (bf16[32,16,1024]{2,1,0:T(8,128)(2,1)S(1)}, bf16[32,16,1024]{2,1,0:T(8,128)(2,1)}, u32[]{:S(2)}) copy-start(bf16[32,16,1024]{2,1,0:T(8,128)(2,1)} %copy-done.8) | copy-start | bytes 3145732
  153.7 4.7 %copy-start.14 = (bf16[1024,2048]{1,0:T(8,128)(2,1)S(1)}, bf16[1024,2048]{1,0:T(8,128)(2,1)}, u32[]{:S(2)}) copy-start(bf16[1024,2048]{1,0:T(8,128)(2,1)} %param.18) | copy-start | bytes 12582916
  201.2 53.1 %all-to-all-start.2 = ((bf16[32,16,2048]{2,1,0:T(8,128)(2,1)}), bf16[32,16,2048]{2,1,0:T(8,128)(2,1)}, u32[]{:S(2)}, u32[]{:S(2)}) async-start(bf16[32,16,2048]{2,1,0:T(8,128)(2,1)} %bitcast.34), calls=%async_computation.2 | async-start | bytes 4194304 | tf_op jit(solution)/shard_map/all_to_all | solution.py:269
  209.4 1.0 copy-start.7
  209.4 1.0 copy-start.12
  254.2 2.5 copy-start.4
  254.2 2.9 %copy-start.5 = (f32[256,2048]{1,0:T(8,128)S(1)}, f32[256,2048]{1,0:T(8,128)}, u32[]{:S(2)}) copy-start(f32[256,2048]{1,0:T(8,128)} %fusion.9) | copy-start | bytes 6291460

commit v3 on v2

--- a/solution.py
+++ b/solution.py
@@ -90,6 +90,41 @@
             transcendentals=row_total * units,
         ),
     )(mid, gain.reshape(1, -1), expert_in, expert_out)
+
+
+def combine_body(base_ref, weight_ref, key_ref, row_ref, rows_ref, out_ref):
+    total = base_ref[...]
+    for route in range(2):
+        hot = (key_ref[:, route : route + 1] == row_ref[...]).astype(jnp.bfloat16)
+        rows = jnp.dot(hot, rows_ref[...], preferred_element_type=jnp.float32)
+        rows = rows.astype(jnp.bfloat16).astype(jnp.float32)
+        total = total + weight_ref[:, route : route + 1] * rows
+    out_ref[...] = total.astype(out_ref.dtype)
+
+
+def combine(base, weight, key, row_key, rows, kind):
+    row_count, feat_dim = base.shape
+    slots = rows.shape[0]
+    width = math.gcd(feat_dim, 512)
+    return pl.pallas_call(
+        combine_body,
+        grid=(feat_dim // width,),
+        in_specs=[
+            pl.BlockSpec((row_count, width), lambda i: (0, i)),
+            pl.BlockSpec((row_count, 2), lambda i: (0, 0)),
+            pl.BlockSpec((row_count, 2), lambda i: (0, 0)),
+            pl.BlockSpec((1, slots), lambda i: (0, 0)),
+            pl.BlockSpec((slots, width), lambda i: (0, i)),
+        ],
+        out_specs=pl.BlockSpec((row_count, width), lambda i: (0, i)),
+        out_shape=jax.ShapeDtypeStruct((row_count, feat_dim), kind),
+        compiler_params=pltpu.CompilerParams(vmem_limit_bytes=24 << 20),
+        cost_estimate=pl.CostEstimate(
+            flops=4 * row_count * slots * feat_dim,
+            bytes_accessed=2 * slots * feat_dim + 8 * row_count * feat_dim,
+            transcendentals=0,
+        ),
+    )(base, weight, key, row_key.reshape(1, -1), rows)
 
 
 def kv_body(rows_ref, weight_ref, out_ref):
@@ -274,19 +309,19 @@
     previous = jnp.concatenate([before, signal[:-1]], axis=0)
     patch_pairs = jnp.concatenate([previous, signal], axis=1)
 
-    ahead = jnp.concatenate(
-        [
-            signal,
-            before,
-            expert_ids.astype(jnp.bfloat16).T.reshape(-1, signal.shape[1]),
-            slot_ids.astype(jnp.bfloat16).T.reshape(-1, signal.shape[1]),
-        ],
-        axis=0,
-    )
-    used = ahead.shape[0]
+    half = devices // 2
+    routes = [
+        table.astype(jnp.bfloat16).T.reshape(-1, signal.shape[1]) for table in (expert_ids, slot_ids)
+    ]
+    used = row_count + 2 * routes[0].shape[0]
+    ahead = jnp.concatenate([signal] + routes, axis=0)
     ahead = jnp.pad(ahead, ((0, -used % 16), (0, 0)))
-    half = devices // 2
     far = lax.ppermute(ahead, "tm", [(dev, (dev + half) % devices) for dev in range(devices)])
+    far_before = lax.ppermute(
+        signal[row_count - 1 :],
+        "tm",
+        [(dev, (dev + 1 + half) % devices) for dev in range(devices - 1)],
+    )
 
     embedded = jnp.dot(patch_pairs, conv_weight, preferred_element_type=jnp.float32).astype(
         jnp.bfloat16
@@ -300,16 +335,18 @@
 
     far, _ = lax.optimization_barrier((far, own_kv))
     in_first = dev_index < half
-    both = jnp.stack([jnp.where(in_first, ahead, far), jnp.where(in_first, far, ahead)])
-    both_signal = both[:, :row_count]
-    both_before = both[:, row_count : row_count + 1]
-    both_previous = jnp.concatenate([both_before, both_signal[:, :-1]], axis=1)
-    both_pairs = jnp.concatenate([both_previous, both_signal], axis=2)
-    both_pairs = both_pairs.reshape(2 * row_count, -1)
-    id_rows = (used - row_count - 1) // 2
-    both_ids = both[:, row_count + 1 : row_count + 1 + id_rows].astype(jnp.int32)
-    both_slots = both[:, row_count + 1 + id_rows : used].astype(jnp.int32)
-    both_keys = (both_ids * CAP + both_slots).reshape(2, 2, row_count)
+    far_signal = far[:row_count]
+    far_previous = jnp.concatenate([far_before, far_signal[:-1]], axis=0)
+    far_pairs = jnp.concatenate([far_previous, far_signal], axis=1)
+    both_pairs = jnp.concatenate(
+        [jnp.where(in_first, patch_pairs, far_pairs), jnp.where(in_first, far_pairs, patch_pairs)]
+    )
+    far_tables = far[row_count:used].astype(jnp.int32).reshape(2, 2, row_count)
+    far_key = far_tables[0] * CAP + far_tables[1]
+    own_key = route_key.T
+    both_keys = jnp.stack(
+        [jnp.where(in_first, own_key, far_key), jnp.where(in_first, far_key, own_key)]
+    )
     span = experts * CAP
     both_keys = both_keys + span * jnp.arange(2, dtype=jnp.int32)[:, None, None]
     both_keys = both_keys.transpose(1, 0, 2).reshape(2, 1, 2 * row_count)
@@ -335,24 +372,27 @@
     )
     pairs_in = pairs_in.reshape(half, 2, local_count, CAP, -1)
 
-    context_in = [
-        exchange(spread(context, local).reshape(devices, CAP, -1)) for local in range(local_count)
+    placed = [
+        jnp.dot(
+            pairs_in[:, :, local].transpose(1, 0, 2, 3).reshape(slots, -1),
+            conv_weight,
+            preferred_element_type=jnp.float32,
+        ).astype(jnp.bfloat16)
+        for local in range(local_count)
     ]
-
-    def mid_of(pairs, contexts):
-        placed = jnp.dot(pairs, conv_weight, preferred_element_type=jnp.float32).astype(
-            jnp.bfloat16
-        )
-        return (
-            placed.astype(jnp.float32)
-            + jnp.dot(contexts, w_out, preferred_element_type=jnp.float32)
-        ).astype(jnp.bfloat16)
+    context_in = []
+    for local in range(local_count):
+        outgoing = spread(context, local)
+        if local:
+            outgoing, placed = lax.optimization_barrier((outgoing, placed))
+        context_in.append(exchange(outgoing.reshape(devices, CAP, -1)).reshape(slots, -1))
 
     returned = []
     for local in range(local_count):
-        pairs = pairs_in[:, :, local].transpose(1, 0, 2, 3).reshape(slots, -1)
-        contexts = context_in[local].reshape(slots, -1)
-        mid = mid_of(pairs, contexts)
+        mid = (
+            placed[local].astype(jnp.float32)
+            + jnp.dot(context_in[local], w_out, preferred_element_type=jnp.float32)
+        ).astype(jnp.bfloat16)
         result = run_expert(mid, ffn_gain, expert_in, expert_out, local, local_count)
         returned.append(exchange(result.reshape(devices, CAP, feat_dim)).reshape(slots, feat_dim))
 
@@ -367,13 +407,9 @@
 
     mixed = stream_mid.astype(jnp.float32)
     for local in range(local_count):
-        for route in range(2):
-            hot = route_key[:, route][:, None] == row_keys[local][None, :]
-            gathered = jnp.dot(
-                hot.astype(jnp.bfloat16), returned[local], preferred_element_type=jnp.float32
-            ).astype(jnp.bfloat16)
-            mixed = mixed + route_weight[:, route : route + 1] * gathered.astype(jnp.float32)
-    return mixed.astype(jnp.bfloat16)
+        kind = jnp.bfloat16 if local == local_count - 1 else jnp.float32
+        mixed = combine(mixed, route_weight, route_key, row_keys[local], returned[local], kind)
+    return mixed
 
 
 def solution(mesh):

time: 262 us -> 263 us (level)
  local copies, waits for them, and re-layouts: 9.36 us -> 21.5 us
  waiting for transfers between devices: 89.1 us -> 81.3 us
  matrix products: 43.5 us -> 35.9 us
  other arithmetic: 4.69 us -> 9.14 us
  starting transfers between devices: 58.5 us -> 54.9 us
  Pallas kernels: 55.4 us -> 58.4 us
    unnamed x32 -> x39, local copies, waits for them, and re-layouts: 3.42 us -> 15.8 us
    all_to_all x4, waiting for transfers between devices: 81 us -> 73.6 us  [exchange(): return lax.all_to_all(rows, 'tm', split_axis=0, concat_axis=0, tiled=True)]
    dot_general x8 -> x4, matrix products: 25.2 us -> 18.1 us  [the longest x2 10.7 us: shards(): jnp.dot(context_in[local], w_out, preferred_element_type=jnp.float32)]
    ppermute x1, starting transfers between devices: 7.6 us -> 0.89 us  [shards(): lax.ppermute(ahead, 'tm', [(dev, (dev + half) % devices) for dev in range...]
    ppermute x0 -> x1, starting transfers between devices: none -> 6.71 us  [shards(): lax.ppermute(signal[row_count - 1:], 'tm', [(dev, (dev + 1 + half) % devi...]
    pallas_call x0 -> x2, Pallas kernels: none -> 5.57 us  [combine(): pl.pallas_call(combine_body, grid=(feat_dim // width,), in_specs=[pl.Bloc...]
    all_to_all x1, starting transfers between devices: 13.8 us -> 9.67 us  [shards(): lax.all_to_all(pairs_out.reshape(half, 2 * local_count * CAP, -1), 'tm',...]
    transpose x3, local copies, waits for them, and re-layouts: 5.08 us -> 1.89 us  [shards(): pairs_in[:, :, local].transpose(1, 0, 2, 3).reshape(slots, -1)]
  transfers between devices with their start and end apart: 12 -> 13, of which waited for: 5 -> 5; matrix products, arithmetic and copies ran while one was open for 18% -> 19% of each run, Pallas kernels for 21% -> 21%
where the time goes in v3:
time: 263 us; the launch traced here: 262 us
  waiting for transfers between devices  81.3 us (31%)
  Pallas kernels  58.4 us (22%)
  starting transfers between devices  54.9 us (21%)
  matrix products  35.9 us (14%)
  local copies, waits for them, and re-layouts  21.5 us (8%)
  other arithmetic  9.14 us (3%)
    all_to_all x4, waiting for transfers between devices, exchange(): return lax.all_to_all(rows, 'tm', split_axis=0, concat_axis=0, tiled=True)  73.6 us
    pallas_call x2, Pallas kernels, run_expert(): pl.pallas_call(functools.partial(expert_body, steps), grid=(row_total //...  37 us
    all_to_all x4, starting transfers between devices, exchange(): return lax.all_to_all(rows, 'tm', split_axis=0, concat_axis=0, tiled=True)  20.6 us
    unnamed x39, local copies, waits for them, and re-layouts  15.8 us
    pallas_call x1, Pallas kernels, attend(): pl.pallas_call(functools.partial(attend_body, kv_heads), out_shape=jax.Sh...  14.9 us
    ppermute x3, starting transfers between devices, window_parts(): fetched.append((lax.ppermute(own_kv, 'tm', route), start))  11.2 us
    dot_general x2, matrix products, shards(): jnp.dot(context_in[local], w_out, preferred_element_type=jnp.float32)  10.7 us
    all_to_all x1, starting transfers between devices, shards(): lax.all_to_all(pairs_out.reshape(half, 2 * local_count * CAP, -1), 'tm',...  9.67 us
  transfers between devices with their start and end apart: 13, of which 5 were waited for; matrix products, arithmetic and copies ran while one was open for 19% of the time, Pallas kernels for 21%

profile of v3, /device:TPU:0, one launch (start us, length us, event | category | flops | bytes accessed | tf_op | source)
XLA Modules:
  0.0 261.6 jit_solution(14436853907798158931)
XLA Ops:
  1.3 2.3 collective-permute-start
  3.7 6.7 %collective-permute-start.7 = (bf16[1,512]{1,0:T(2,128)(2,1)}, bf16[1,512]{1,0:T(2,128)(2,1)}, u32[]{:S(2)}, u32[]{:S(2)}) collective-permute-start(bf16[1,512]{1,0:T(2,128)(2,1)} %slice.47), channel_id=1, source_target_pairs={{0,17},{1,18},{2,19},{3,20},{4,21},{5,22},{6,23},{7,24},{8,25},{9,... | collective-permute-start | bytes 3080 | tf_op jit(solution)/shard_map/ppermute | solution.py:320
  11.9 1.7 fusion.33
  17.1 3.7 %fusion.2 = (f32[256]{0:T(256)S(1)}, bf16[256,2048]{1,0:T(8,128)(2,1)S(1)}) fusion(bf16[1024,2048]{1,0:T(8,128)(2,1)} %param.14, bf16[256,512]{1,0:T(8,128)(2,1)} %param.13, bf16[255,512]{1,0:T(8,128)(2,1)} %bitcast.93, bf16[1,512]{1,0:T(2,128)(2,1)S(1)} %collective-permute-done), kind=kOutput, calls=%fused_computation.10 | convolution fusion | flops 1077411584 | bytes 5768192 | tf_op jit(solution)/shard_map/dot_general | solution.py:326
  21.2 1.6 copy-done.9
  23.7 3.1 %collective-permute-start.1 = (bf16[256,512]{1,0:T(8,128)(2,1)S(1)}, bf16[256,512]{1,0:T(8,128)(2,1)S(1)}, u32[]{:S(2)}, u32[]{:S(2)}) collective-permute-start(bf16[256,512]{1,0:T(8,128)(2,1)S(1)} %shard_map.127), channel_id=1, source_target_pairs={{0,8},{1,9},{2,10},{3,11},{4,12},{5,13},{6,14},{7,15},{8,16},{9,17... | collective-permute-start | bytes 786440 | tf_op jit(solution)/shard_map/ppermute | solution.py:22
  26.8 3.4 %collective-permute-start.2 = (bf16[256,512]{1,0:T(8,128)(2,1)S(1)}, bf16[256,512]{1,0:T(8,128)(2,1)S(1)}, u32[]{:S(2)}, u32[]{:S(2)}) collective-permute-start(bf16[256,512]{1,0:T(8,128)(2,1)S(1)} %shard_map.127), channel_id=1, source_target_pairs={{0,2},{1,3},{2,8},{3,9},{4,6},{5,7},{6,12},{7,13},{8,10},{9,11},{1... | collective-permute-start | bytes 786440 | tf_op jit(solution)/shard_map/ppermute | solution.py:253
  30.2 3.4 %collective-permute-start.3 = (bf16[256,512]{1,0:T(8,128)(2,1)S(1)}, bf16[256,512]{1,0:T(8,128)(2,1)S(1)}, u32[]{:S(2)}, u32[]{:S(2)}) collective-permute-start(bf16[256,512]{1,0:T(8,128)(2,1)S(1)} %shard_map.127), channel_id=1, source_target_pairs={{0,4},{1,5},{2,6},{3,7},{4,8},{5,9},{6,10},{7,11},{8,12},{9,13},{1... | collective-permute-start | bytes 786440 | tf_op jit(solution)/shard_map/ppermute | solution.py:253
  33.6 4.4 %collective-permute-start.4 = (bf16[256,512]{1,0:T(8,128)(2,1)S(1)}, bf16[256,512]{1,0:T(8,128)(2,1)S(1)}, u32[]{:S(2)}, u32[]{:S(2)}) collective-permute-start(bf16[256,512]{1,0:T(8,128)(2,1)S(1)} %shard_map.127), channel_id=1, source_target_pairs={{0,6},{1,7},{2,4},{3,5},{4,10},{5,11},{6,8},{7,9},{8,14},{9,15},{1... | collective-permute-start | bytes 786440 | tf_op jit(solution)/shard_map/ppermute | solution.py:253
  42.6 3.3 %fusion.9 = bf16[1024,1024]{1,0:T(8,128)(2,1)} fusion(bf16[256,1024]{1,0:T(8,128)(2,1)S(1)} %get-tuple-element.24, bf16[256,1024]{1,0:T(8,128)(2,1)S(1)} %get-tuple-element.23, s32[512]{0:T(512)S(1)} %bitcast.102, s32[512]{0:T(512)S(1)} %bitcast.101, s32[1024]{0:T(1024)} %fusion.51), kind=kOutput, calls=%fused_computation.19 | convolution fusion | flops 1078460416 | bytes 3153920 | tf_op jit(solution)/shard_map/dot_general | solution.py:361
  45.9 9.7 %all-to-all-start = ((bf16[16,64,1024]{2,1,0:T(8,128)(2,1)}), bf16[16,64,1024]{2,1,0:T(8,128)(2,1)}, u32[]{:S(2)}, u32[]{:S(2)}) async-start(bf16[16,64,1024]{2,1,0:T(8,128)(2,1)} %bitcast.95), calls=%async_computation | async-start | bytes 4194304 | tf_op jit(solution)/shard_map/all_to_all | solution.py:365
  57.2 3.4 %fusion.77.query_ref = f32[256,1024]{1,0:T(8,128)S(1)} fusion(bf16[256,2048]{1,0:T(8,128)(2,1)S(1)} %fusion.4.rows_ref, bf16[2048,1024]{1,0:T(8,128)(2,1)} %param.16), kind=kOutput, calls=%fused_computation.144 | convolution fusion | flops 1073741824 | bytes 6291456 | tf_op jit(solution)/shard_map/dot_general | solution.py:333
  60.9 14.9 %shard_map.128 = bf16[256,1024]{1,0:T(8,128)(2,1)S(1)} custom-call(s32[9]{0:T(128)S(1)} %compare_convert_fusion.valid_ref, f32[8]{0:T(128)S(1)} %copy-done.11, f32[256,1024]{1,0:T(8,128)S(1)} %fusion.77.query_ref, bf16[1,256,512]{2,1,0:T(8,128)(2,1)S(1)} %bitcast.83, bf16[1,256,512]{2,1,0:T(8,128)(2,1)S(1)} %bitcast.84, bf16[1,256,512]{2,1,0:T(8,128)(2,1)S(1)} %bitcast.86, ...), custom_call_target="tpu_custom_call" | custom-call | flops 3623878656 | bytes 3932160 | tf_op jit(solution)/shard_map/pallas_call | solution.py:217
  77.3 7.7 %all-to-all-done = bf16[16,64,1024]{2,1,0:T(8,128)(2,1)} async-done(((bf16[16,64,1024]{2,1,0:T(8,128)(2,1)}), bf16[16,64,1024]{2,1,0:T(8,128)(2,1)}, u32[]{:S(2)}, u32[]{:S(2)}) %all-to-all-start) | async-done | bytes 2097184 | tf_op jit(solution)/shard_map/all_to_all | solution.py:365
  85.0 8.1 %all-to-all-start.1 = ((bf16[32,16,1024]{2,1,0:T(8,128)(2,1)}), bf16[32,16,1024]{2,1,0:T(8,128)(2,1)S(1)}, u32[]{:S(2)}, u32[]{:S(2)}) async-start(bf16[32,16,1024]{2,1,0:T(8,128)(2,1)} %bitcast.31), calls=%async_computation.1 | async-start | bytes 2097152 | tf_op jit(solution)/shard_map/all_to_all | solution.py:304
  94.6 1.7 slice_bitcast_fusion
  96.5 2.0 copy-done.17
  98.5 3.7 %convolution_convert_fusion = bf16[512,2048]{1,0:T(8,128)(2,1)} fusion(bf16[512,1024]{1,0:T(8,128)(2,1)S(1)} %bitcast.97, bf16[1024,2048]{1,0:T(8,128)(2,1)S(1)} %copy-done.17), kind=kOutput, calls=%fused_computation.5 | convolution fusion | flops 2148532224 | bytes 7340032 | tf_op jit(solution)/shard_map/dot_general | solution.py:376
  102.2 3.7 %convolution_convert_fusion.1 = bf16[512,2048]{1,0:T(8,128)(2,1)} fusion(bf16[512,1024]{1,0:T(8,128)(2,1)S(1)} %bitcast.98, bf16[1024,2048]{1,0:T(8,128)(2,1)S(1)} %copy-done.17), kind=kOutput, calls=%fused_computation.6 | convolution fusion | flops 2148532224 | bytes 7340032 | tf_op jit(solution)/shard_map/dot_general | solution.py:376
  105.9 13.3 %all-to-all-done.1 = bf16[32,16,1024]{2,1,0:T(8,128)(2,1)S(1)} async-done(((bf16[32,16,1024]{2,1,0:T(8,128)(2,1)}), bf16[32,16,1024]{2,1,0:T(8,128)(2,1)S(1)}, u32[]{:S(2)}, u32[]{:S(2)}) %all-to-all-start.1) | async-done | bytes 1048608 | tf_op jit(solution)/shard_map/all_to_all | solution.py:304
  119.2 3.7 %all-to-all-start.3 = ((bf16[32,16,1024]{2,1,0:T(8,128)(2,1)}), bf16[32,16,1024]{2,1,0:T(8,128)(2,1)}, u32[]{:S(2)}, u32[]{:S(2)}) async-start(bf16[32,16,1024]{2,1,0:T(8,128)(2,1)} %bitcast.36), calls=%async_computation.3 | async-start | bytes 2097152 | tf_op jit(solution)/shard_map/all_to_all | solution.py:304
  123.0 5.2 %add_convert_fusion.1.mid_ref = bf16[512,2048]{1,0:T(8,128)(2,1)S(1)} fusion(bf16[512,2048]{1,0:T(8,128)(2,1)} %convolution_convert_fusion.1, bf16[512,1024]{1,0:T(8,128)(2,1)S(1)} %bitcast.96, bf16[1024,2048]{1,0:T(8,128)(2,1)} %param.18), kind=kOutput, calls=%fused_computation.1 | convolution fusion | flops 2150629376 | bytes 9437184 | tf_op jit(solution)/shard_map/dot_general | solution.py:394
  128.2 18.5 %shard_map.129 = bf16[512,2048]{1,0:T(8,128)(2,1)S(1)} custom-call(bf16[512,2048]{1,0:T(8,128)(2,1)S(1)} %add_convert_fusion.1.mid_ref, f32[1,2048]{1,0:T(1,128)S(1)} %bitcast.91, bf16[2,2816,2048]{2,1,0:T(8,128)(2,1)} %w_in_ref.3, bf16[2816,2048]{1,0:T(8,128)(2,1)} %w_out_ref.3), custom_call_target="tpu_custom_call" | custom-call | flops 8858370048 | bytes 21495808 | tf_op jit(solution)/shard_map/pallas_call | solution.py:71
  149.2 4.8 %all-to-all-start.2 = ((bf16[32,16,2048]{2,1,0:T(8,128)(2,1)}), bf16[32,16,2048]{2,1,0:T(8,128)(2,1)S(1)}, u32[]{:S(2)}, u32[]{:S(2)}) async-start(bf16[32,16,2048]{2,1,0:T(8,128)(2,1)} %bitcast.82), calls=%async_computation.2 | async-start | bytes 4194304 | tf_op jit(solution)/shard_map/all_to_all | solution.py:304
  154.0 5.5 %add_convert_fusion.mid_ref = bf16[512,2048]{1,0:T(8,128)(2,1)S(1)} fusion(bf16[512,2048]{1,0:T(8,128)(2,1)} %convolution_convert_fusion, bf16[512,1024]{1,0:T(8,128)(2,1)} %bitcast.37, bf16[1024,2048]{1,0:T(8,128)(2,1)} %param.18), kind=kOutput, calls=%fused_computation | convolution fusion | flops 2150629376 | bytes 9437184 | tf_op jit(solution)/shard_map/dot_general | solution.py:394
  159.5 18.5 %shard_map.131 = bf16[512,2048]{1,0:T(8,128)(2,1)S(1)} custom-call(bf16[512,2048]{1,0:T(8,128)(2,1)S(1)} %add_convert_fusion.mid_ref, f32[1,2048]{1,0:T(1,128)S(1)} %bitcast.92, bf16[2,2816,2048]{2,1,0:T(8,128)(2,1)} %w_in_ref.3, bf16[2816,2048]{1,0:T(8,128)(2,1)} %w_out_ref.3), custom_call_target="tpu_custom_call" | custom-call | flops 8858370048 | bytes 21495808 | tf_op jit(solution)/shard_map/pallas_call | solution.py:71
  179.4 23.4 %all-to-all-done.2 = bf16[32,16,2048]{2,1,0:T(8,128)(2,1)S(1)} async-done(((bf16[32,16,2048]{2,1,0:T(8,128)(2,1)}), bf16[32,16,2048]{2,1,0:T(8,128)(2,1)S(1)}, u32[]{:S(2)}, u32[]{:S(2)}) %all-to-all-start.2) | async-done | bytes 2097184 | tf_op jit(solution)/shard_map/all_to_all | solution.py:304
  204.1 3.9 %all-to-all-start.4 = ((bf16[32,16,2048]{2,1,0:T(8,128)(2,1)}), bf16[32,16,2048]{2,1,0:T(8,128)(2,1)S(1)}, u32[]{:S(2)}, u32[]{:S(2)}) async-start(bf16[32,16,2048]{2,1,0:T(8,128)(2,1)} %bitcast.81), calls=%async_computation.4 | async-start | bytes 4194304 | tf_op jit(solution)/shard_map/all_to_all | solution.py:304
  208.1 3.9 %multiply_reduce_fusion = (f32[256]{0:T(256)S(1)}, f32[256,2048]{1,0:T(8,128)S(1)}) fusion(bf16[256,1024]{1,0:T(8,128)(2,1)S(1)} %shard_map.128, bf16[1024,2048]{1,0:T(8,128)(2,1)} %param.18, bf16[256,2048]{1,0:T(8,128)(2,1)} %copy-done.13), kind=kOutput, calls=%fused_computation.14 | convolution fusion | flops 1076887296 | bytes 7865344 | tf_op jit(solution)/shard_map/dot_general | solution.py:400
  217.3 2.4 shard_map.130.base_ref
  221.1 35.8 %all-to-all-done.4 = bf16[32,16,2048]{2,1,0:T(8,128)(2,1)S(1)} async-done(((bf16[32,16,2048]{2,1,0:T(8,128)(2,1)}), bf16[32,16,2048]{2,1,0:T(8,128)(2,1)S(1)}, u32[]{:S(2)}, u32[]{:S(2)}) %all-to-all-start.4) | async-done | bytes 2097184 | tf_op jit(solution)/shard_map/all_to_all | solution.py:304
  258.5 3.1 %shard_map.132 = bf16[256,2048]{1,0:T(8,128)(2,1)} custom-call(f32[256,2048]{1,0:T(8,128)S(1)} %copy-done.2, f32[256,2]{1,0:T(8,128)S(1)} %broadcast_divide_fusion.weight_ref, s32[256,2]{1,0:T(8,128)S(1)} %get-tuple-element.20.key_ref, s32[1,512]{1,0:T(1,128)S(1)} %multiply_add_fusion.row_ref, bf16[512,2048]{1,0:T(8,128)(2,1)S(1)} %bitcast.79), custom_call_target="tpu_custom_call" | custom-call | flops 1073741824 | bytes 6291456 | tf_op jit(solution)/shard_map/pallas_call | solution.py:109
  (88 shorter events, 30.3 us)
Async XLA Ops:
  0.0 212.0 %copy-start = (bf16[2048,64]{0,1:T(8,128)(2,1)S(1)}, bf16[2048,64]{0,1:T(8,128)(2,1)}, u32[]{:S(2)}) copy-start(bf16[2048,64]{0,1:T(8,128)(2,1)} %param.21) | copy-start | bytes 786436
  1.3 15.8 %collective-permute-start = (bf16[1,512]{1,0:T(2,128)(2,1)}, bf16[1,512]{1,0:T(2,128)(2,1)S(1)}, u32[]{:S(2)}, u32[]{:S(2)}) collective-permute-start(bf16[1,512]{1,0:T(2,128)(2,1)} %slice.47), channel_id=1, source_target_pairs={{0,1},{1,2},{2,3},{3,4},{4,5},{5,6},{6,7},{7,8},{8,9},{9,10},{10,1... | collective-permute-start | bytes 3080 | tf_op jit(solution)/shard_map/ppermute | solution.py:22
  3.7 38.0 %collective-permute-start.7 = (bf16[1,512]{1,0:T(2,128)(2,1)}, bf16[1,512]{1,0:T(2,128)(2,1)}, u32[]{:S(2)}, u32[]{:S(2)}) collective-permute-start(bf16[1,512]{1,0:T(2,128)(2,1)} %slice.47), channel_id=1, source_target_pairs={{0,17},{1,18},{2,19},{3,20},{4,21},{5,22},{6,23},{7,24},{8,25},{9,... | collective-permute-start | bytes 3080 | tf_op jit(solution)/shard_map/ppermute | solution.py:320
  13.5 20.1 %collective-permute-start.6 = (bf16[272,512]{1,0:T(8,128)(2,1)}, bf16[272,512]{1,0:T(8,128)(2,1)S(1)}, u32[]{:S(2)}, u32[]{:S(2)}) collective-permute-start(bf16[272,512]{1,0:T(8,128)(2,1)} %fusion.33), channel_id=1, source_target_pairs={{0,16},{1,17},{2,18},{3,19},{4,20},{5,21},{6,22},{7,23},{8,24},{9,... | collective-permute-start | bytes 835592 | tf_op jit(solution)/shard_map/ppermute | solution.py:319
  17.1 3.7 %copy-start.16 = (bf16[1,512]{1,0:T(2,128)(2,1)}, bf16[1,512]{1,0:T(2,128)(2,1)S(1)}, u32[]{:S(2)}) copy-start(bf16[1,512]{1,0:T(2,128)(2,1)S(1)} %collective-permute-done) | copy-start | bytes 3076
  17.1 3.8 %copy-start.14 = (f32[2048]{0:T(1024)S(1)}, f32[2048]{0:T(1024)}, u32[]{:S(2)}) copy-start(f32[2048]{0:T(1024)} %param.15) | copy-start | bytes 24580
  20.9 2.8 %copy-start.13 = (bf16[256,2048]{1,0:T(8,128)(2,1)}, bf16[256,2048]{1,0:T(8,128)(2,1)S(1)}, u32[]{:S(2)}) copy-start(bf16[256,2048]{1,0:T(8,128)(2,1)S(1)} %get-tuple-element.30) | copy-start | bytes 3145732
  20.9 2.0 copy-start.9
  23.7 18.0 %copy-start.12 = (bf16[256,512]{1,0:T(8,128)(2,1)S(1)}, bf16[256,512]{1,0:T(8,128)(2,1)}, u32[]{:S(2)}) copy-start(bf16[256,512]{1,0:T(8,128)(2,1)} %param.13) | copy-start | bytes 786436
  23.7 22.2 %collective-permute-start.1 = (bf16[256,512]{1,0:T(8,128)(2,1)S(1)}, bf16[256,512]{1,0:T(8,128)(2,1)S(1)}, u32[]{:S(2)}, u32[]{:S(2)}) collective-permute-start(bf16[256,512]{1,0:T(8,128)(2,1)S(1)} %shard_map.127), channel_id=1, source_target_pairs={{0,8},{1,9},{2,10},{3,11},{4,12},{5,13},{6,14},{7,15},{8,16},{9,17... | collective-permute-start | bytes 786440 | tf_op jit(solution)/shard_map/ppermute | solution.py:22
  26.8 19.2 %collective-permute-start.2 = (bf16[256,512]{1,0:T(8,128)(2,1)S(1)}, bf16[256,512]{1,0:T(8,128)(2,1)S(1)}, u32[]{:S(2)}, u32[]{:S(2)}) collective-permute-start(bf16[256,512]{1,0:T(8,128)(2,1)S(1)} %shard_map.127), channel_id=1, source_target_pairs={{0,2},{1,3},{2,8},{3,9},{4,6},{5,7},{6,12},{7,13},{8,10},{9,11},{1... | collective-permute-start | bytes 786440 | tf_op jit(solution)/shard_map/ppermute | solution.py:253
  30.2 15.8 %collective-permute-start.3 = (bf16[256,512]{1,0:T(8,128)(2,1)S(1)}, bf16[256,512]{1,0:T(8,128)(2,1)S(1)}, u32[]{:S(2)}, u32[]{:S(2)}) collective-permute-start(bf16[256,512]{1,0:T(8,128)(2,1)S(1)} %shard_map.127), channel_id=1, source_target_pairs={{0,4},{1,5},{2,6},{3,7},{4,8},{5,9},{6,10},{7,11},{8,12},{9,13},{1... | collective-permute-start | bytes 786440 | tf_op jit(solution)/shard_map/ppermute | solution.py:253
  33.6 12.3 %collective-permute-start.4 = (bf16[256,512]{1,0:T(8,128)(2,1)S(1)}, bf16[256,512]{1,0:T(8,128)(2,1)S(1)}, u32[]{:S(2)}, u32[]{:S(2)}) collective-permute-start(bf16[256,512]{1,0:T(8,128)(2,1)S(1)} %shard_map.127), channel_id=1, source_target_pairs={{0,6},{1,7},{2,4},{3,5},{4,10},{5,11},{6,8},{7,9},{8,14},{9,15},{1... | collective-permute-start | bytes 786440 | tf_op jit(solution)/shard_map/ppermute | solution.py:253
  45.9 39.1 %all-to-all-start = ((bf16[16,64,1024]{2,1,0:T(8,128)(2,1)}), bf16[16,64,1024]{2,1,0:T(8,128)(2,1)}, u32[]{:S(2)}, u32[]{:S(2)}) async-start(bf16[16,64,1024]{2,1,0:T(8,128)(2,1)} %bitcast.95), calls=%async_computation | async-start | bytes 4194304 | tf_op jit(solution)/shard_map/all_to_all | solution.py:365
  56.8 4.1 %collective-permute-start.5 = (bf16[4,256,512]{2,1,0:T(8,128)(2,1)}, bf16[4,256,512]{2,1,0:T(8,128)(2,1)}, u32[]{:S(2)}, u32[]{:S(2)}) collective-permute-start(bf16[4,256,512]{2,1,0:T(8,128)(2,1)} %pad_maximum_fusion), channel_id=1, source_target_pairs={{0,1},{1,0},{2,3},{3,2},{4,5},{5,4},{6,7},{7,6},{8,9},{9,8},{10,11... | collective-permute-start | bytes 3145736 | tf_op jit(solution)/shard_map/ppermute | solution.py:255
  57.2 3.7 %copy-start.11 = (f32[8]{0:T(128)S(1)}, f32[8]{0:T(128)}, u32[]{:S(2)}) copy-start(f32[8]{0:T(128)} %scale_ref.1) | copy-start | bytes 100
  85.0 34.2 %all-to-all-start.1 = ((bf16[32,16,1024]{2,1,0:T(8,128)(2,1)}), bf16[32,16,1024]{2,1,0:T(8,128)(2,1)S(1)}, u32[]{:S(2)}, u32[]{:S(2)}) async-start(bf16[32,16,1024]{2,1,0:T(8,128)(2,1)} %bitcast.31), calls=%async_computation.1 | async-start | bytes 2097152 | tf_op jit(solution)/shard_map/all_to_all | solution.py:304
  96.3 2.2 copy-start.17
  119.2 30.0 %all-to-all-start.3 = ((bf16[32,16,1024]{2,1,0:T(8,128)(2,1)}), bf16[32,16,1024]{2,1,0:T(8,128)(2,1)}, u32[]{:S(2)}, u32[]{:S(2)}) async-start(bf16[32,16,1024]{2,1,0:T(8,128)(2,1)} %bitcast.36), calls=%async_computation.3 | async-start | bytes 2097152 | tf_op jit(solution)/shard_map/all_to_all | solution.py:304
  123.0 5.2 %copy-start.10 = (f32[2048]{0:T(1024)S(1)}, f32[2048]{0:T(1024)}, u32[]{:S(2)}) copy-start(f32[2048]{0:T(1024)} %param.20) | copy-start | bytes 24580
  146.7 1.3 copy-start.8
  149.2 53.6 %all-to-all-start.2 = ((bf16[32,16,2048]{2,1,0:T(8,128)(2,1)}), bf16[32,16,2048]{2,1,0:T(8,128)(2,1)S(1)}, u32[]{:S(2)}, u32[]{:S(2)}) async-start(bf16[32,16,2048]{2,1,0:T(8,128)(2,1)} %bitcast.82), calls=%async_computation.2 | async-start | bytes 4194304 | tf_op jit(solution)/shard_map/all_to_all | solution.py:304
  178.1 1.3 copy-start.7
  202.8 1.3 copy-start.3
  204.1 52.8 %all-to-all-start.4 = ((bf16[32,16,2048]{2,1,0:T(8,128)(2,1)}), bf16[32,16,2048]{2,1,0:T(8,128)(2,1)S(1)}, u32[]{:S(2)}, u32[]{:S(2)}) async-start(bf16[32,16,2048]{2,1,0:T(8,128)(2,1)} %bitcast.81), calls=%async_computation.4 | async-start | bytes 4194304 | tf_op jit(solution)/shard_map/all_to_all | solution.py:304
  211.9 1.9 copy-start.15
  212.5 1.3 copy-start.5
  214.1 1.6 copy-start.4
  215.7 1.6 copy-start.6
  219.8 1.3 copy-start.1
  256.9 1.6 copy-start.2

commit v4 on v3

--- a/solution.py
+++ b/solution.py
@@ -92,6 +92,76 @@
     )(mid, gain.reshape(1, -1), expert_in, expert_out)
 
 
+def spread_body(
+    shape, info_ref, signal_ref, before_ref, key_ref, far_ref, out_ref
+):
+    half, copies, local_count, count = shape
+    rows = out_ref.shape[0]
+    tokens, width = signal_ref.shape
+    first_dev, own_block = info_ref[0], info_ref[1]
+    row = pl.program_id(0) * rows + lax.broadcasted_iota(jnp.int32, (rows, 1), 0)
+    slot = lax.rem(row, CAP)
+    local = lax.rem(lax.div(row, CAP), local_count)
+    block = lax.rem(lax.div(row, CAP * local_count), 2)
+    dev = first_dev + lax.div(row, CAP * local_count * 2)
+    want = ((lax.div(dev, copies) * local_count + local) * CAP + slot).astype(jnp.float32)
+    lane = lax.broadcasted_iota(jnp.int32, (8, tokens), 1)
+
+    own_keys = [key_ref[route : route + 1].astype(jnp.float32) for route in range(2)]
+    far_rows = [far_ref[tokens + 1 + at : tokens + 2 + at].astype(jnp.float32) for at in range(2)]
+    far_all = far_rows[0] * CAP + far_rows[1]
+    far_keys = [far_all[:, route * tokens : (route + 1) * tokens] for route in range(2)]
+    far_before = far_ref[tokens : tokens + 1]
+    now = jnp.zeros((rows, width), jnp.float32)
+    past = jnp.zeros((rows, width), jnp.float32)
+    for mine, keys, samples, before in (
+        (True, own_keys, signal_ref[...], before_ref[...]),
+        (False, far_keys, far_ref[:tokens], far_before),
+    ):
+        here = (block == own_block) if mine else (block != own_block)
+        sought = jnp.where(here, want, -1.0)
+        hot, hot_next, hot_first = False, False, False
+        for key in keys:
+            wide = jnp.broadcast_to(key, (8, tokens))
+            after = jnp.where(lane == tokens - 1, -2.0, pltpu.roll(wide, tokens - 1, 1))[:1]
+            hot = (sought == key) | hot
+            hot_next = (sought == after) | hot_next
+            hot_first = (sought == key[:, :1]) | hot_first
+        now += jnp.dot(hot.astype(jnp.bfloat16), samples, preferred_element_type=jnp.float32)
+        past += jnp.dot(
+            hot_next.astype(jnp.bfloat16), samples, preferred_element_type=jnp.float32
+        )
+        past += jnp.where(hot_first, before.astype(jnp.float32), 0.0)
+    out_ref[:, :width] = past.astype(out_ref.dtype)
+    out_ref[:, width:] = now.astype(out_ref.dtype)
+
+
+def spread_pairs(info, signal, before, keys, far, half, copies, local_count):
+    tokens, width = signal.shape
+    rows = half * 2 * local_count * CAP
+    tile = math.gcd(rows, 256)
+    whole = lambda shape: pl.BlockSpec(shape, lambda i: (0, 0))
+    return pl.pallas_call(
+        functools.partial(spread_body, (half, copies, local_count, tokens)),
+        grid=(rows // tile,),
+        in_specs=[
+            pl.BlockSpec(memory_space=pltpu.SMEM),
+            whole(signal.shape),
+            whole(before.shape),
+            whole(keys.shape),
+            whole(far.shape),
+        ],
+        out_specs=pl.BlockSpec((tile, 2 * width), lambda i: (i, 0)),
+        out_shape=jax.ShapeDtypeStruct((rows, 2 * width), jnp.bfloat16),
+        compiler_params=pltpu.CompilerParams(vmem_limit_bytes=16 << 20),
+        cost_estimate=pl.CostEstimate(
+            flops=8 * rows * tokens * width,
+            bytes_accessed=4 * rows * width + 4 * tokens * width,
+            transcendentals=0,
+        ),
+    )(info, signal, before, keys, far)
+
+
 def combine_body(base_ref, weight_ref, key_ref, row_ref, rows_ref, out_ref):
     total = base_ref[...]
     for route in range(2):
@@ -153,25 +223,26 @@
     )(rows, weight)
 
 
-def attend_body(
-    kv_heads, valid_ref, scale_ref, query_ref, *refs
-):
+def attend_body(kv_heads, flag_ref, scale_ref, query_ref, *refs):
     *kv_refs, out_ref, unit_ref, key_ref, value_ref, score_ref = refs
     blocks = [ref.at[part] for ref in kv_refs for part in range(ref.shape[0])]
     rows = query_ref.shape[0]
     heads = query_ref.shape[1] // HEAD_DIM
     group = heads // kv_heads
     kv_dim = kv_heads * HEAD_DIM
-    for head in range(heads):
-        unit_ref[head] = head_norm(
-            query_ref[:, head * HEAD_DIM : (head + 1) * HEAD_DIM]
-        ).astype(jnp.bfloat16)
+    count = len(blocks)
     for pos, block in enumerate(blocks):
         for kv in range(kv_heads):
             low = kv * HEAD_DIM
             key_ref[kv, pos] = block[:, low : low + HEAD_DIM]
             value_ref[kv, pos, :, :HEAD_DIM] = block[:, kv_dim + low : kv_dim + low + HEAD_DIM]
+    for kv in range(kv_heads):
+        for pos in range(count):
             value_ref[kv, pos, :, HEAD_DIM:] = jnp.ones((rows, HEAD_DIM), jnp.bfloat16)
+    for head in range(heads):
+        unit_ref[head] = head_norm(
+            query_ref[:, head * HEAD_DIM : (head + 1) * HEAD_DIM]
+        ).astype(jnp.bfloat16)
     query_at = lax.broadcasted_iota(jnp.int32, (rows, rows), 0)
     key_at = lax.broadcasted_iota(jnp.int32, (rows, rows), 1)
 
@@ -180,7 +251,7 @@
         kv = head // group
         unit = unit_ref[head]
         top = jnp.full((rows, HEAD_DIM), MASKED, jnp.float32)
-        for pos in range(len(blocks)):
+        for pos in range(count):
             score = lax.dot_general(
                 unit,
                 key_ref[kv, pos],
@@ -189,29 +260,30 @@
             )
             if pos == 0:
                 score = jnp.where(key_at <= query_at, score, MASKED)
-            else:
-                seen = valid_ref[pos] > 0
-                if pos == 1:
-                    score = jnp.where((key_at > query_at) & seen, score, MASKED)
-                else:
-                    score = jnp.where(seen, score, MASKED)
+            if pos == 1:
+                score = jnp.where(key_at > query_at, score, MASKED)
             score_ref[pos] = score
-            for low in range(0, rows, HEAD_DIM):
-                top = jnp.maximum(top, score[:, low : low + HEAD_DIM])
+            high = score[:, :HEAD_DIM]
+            for low in range(HEAD_DIM, rows, HEAD_DIM):
+                high = jnp.maximum(high, score[:, low : low + HEAD_DIM])
+            if pos:
+                high = jnp.where(flag_ref[pos] > 0, high, MASKED)
+            top = jnp.maximum(top, high)
+        factor = scale_ref[head] * (math.log2(math.e) / math.sqrt(HEAD_DIM))
         top = jnp.max(top, axis=1, keepdims=True)
-        factor = scale_ref[head] * (math.log2(math.e) / math.sqrt(HEAD_DIM))
         total = jnp.zeros((rows, 2 * HEAD_DIM), jnp.float32)
-        for pos in range(len(blocks)):
-            weight = jnp.exp2((score_ref[pos] - top) * factor).astype(jnp.bfloat16)
+        for pos in range(count):
+            base = jnp.where(flag_ref[pos] > 0, top, -MASKED) if pos else top
+            weight = jnp.exp2((score_ref[pos] - base) * factor).astype(jnp.bfloat16)
             total += jnp.dot(weight, value_ref[kv, pos], preferred_element_type=jnp.float32)
-        place = pl.ds(pl.multiple_of(head * HEAD_DIM, HEAD_DIM), HEAD_DIM)
-        out_ref[:, place] = (total[:, :HEAD_DIM] / total[:, HEAD_DIM:]).astype(out_ref.dtype)
-
-
-def attend(valid, head_scale, queries, kv_parts, kv_heads):
+        place_at = pl.ds(pl.multiple_of(head * HEAD_DIM, HEAD_DIM), HEAD_DIM)
+        out_ref[:, place_at] = (total[:, :HEAD_DIM] / total[:, HEAD_DIM:]).astype(out_ref.dtype)
+
+
+def attend(flags, head_scale, queries, kv_parts, kv_heads):
     rows, width = queries.shape
     heads = width // HEAD_DIM
-    count = sum(part.shape[0] for part in kv_parts)
+    count = flags.shape[0]
     smem = pl.BlockSpec(memory_space=pltpu.SMEM)
     vmem = pl.BlockSpec(memory_space=pltpu.VMEM)
     return pl.pallas_call(
@@ -231,34 +303,27 @@
             bytes_accessed=rows * width * 6 + count * rows * kv_heads * HEAD_DIM * 4,
             transcendentals=heads * count * rows * rows,
         ),
-    )(valid, head_scale, queries, *kv_parts)
-
-
-def window_parts(own_kv, group):
+    )(flags, head_scale, queries, *kv_parts)
+
+
+def window_parts(own_kv, prior_kv, group):
     devices = lax.axis_size("tm")
     me = lax.axis_index("tm")
     core, chip, base = me % 2, me % group // 2, me // group * group
-    prior = from_behind(own_kv, "tm", group)
-    parts = [(own_kv, me), (prior, me - group)]
-    fetched = []
+    fetched, flags, sent = [], [], []
     for step in range(1, group // 2):
-        route = []
-        for dev in range(devices):
-            target = dev ^ (2 * step)
-            target += 0 if dev < target else group
-            if target < devices:
-                route.append((dev, target))
         other = chip ^ step
-        start = base - jnp.where(other > chip, group, 0) + 2 * other
-        fetched.append((lax.ppermute(own_kv, "tm", route), start))
-    shared = jnp.stack([block for block, _ in fetched] + [jnp.where(core == 0, own_kv, prior)])
+        block = jnp.where(other > chip, own_kv, prior_kv)
+        sent.append(block)
+        fetched.append(
+            lax.ppermute(block, "tm", [(dev, dev ^ (2 * step)) for dev in range(devices)])
+        )
+        flags.append((other < chip) | (base > 0))
+    shared = jnp.stack(fetched + [jnp.where(core == 0, own_kv, prior_kv)])
     shared = lax.ppermute(shared, "tm", [(dev, dev ^ 1) for dev in range(devices)])
-    numbers = [start + core for _, start in fetched]
-    numbers += [start + 1 - core for _, start in fetched]
-    numbers.append(jnp.where(core == 0, me + 1 - group, me - 1))
-    blocks = [own_kv[None], prior[None]] + [block[None] for block, _ in fetched] + [shared]
-    numbers = jnp.stack([me, me - group] + numbers)
-    return blocks, numbers
+    flags = [me >= 0, base > 0] + flags + flags + [(core > 0) | (base > 0)]
+    parts = [block[None] for block in [own_kv, prior_kv] + fetched] + [shared]
+    return parts, jnp.stack(flags).astype(jnp.int32), sent
 
 
 def shards(
@@ -306,62 +371,43 @@
     reach_blocks = WINDOW // row_count
     group = reach_blocks
     before = from_behind(signal[row_count - 1 :], "tm", 1)
-    previous = jnp.concatenate([before, signal[:-1]], axis=0)
-    patch_pairs = jnp.concatenate([previous, signal], axis=1)
-
     half = devices // 2
     routes = [
         table.astype(jnp.bfloat16).T.reshape(-1, signal.shape[1]) for table in (expert_ids, slot_ids)
     ]
-    used = row_count + 2 * routes[0].shape[0]
-    ahead = jnp.concatenate([signal] + routes, axis=0)
+    ahead = jnp.concatenate([signal, before] + routes, axis=0)
+    used = ahead.shape[0]
     ahead = jnp.pad(ahead, ((0, -used % 16), (0, 0)))
+    prior = from_behind(ahead, "tm", group)
+    ahead, prior = lax.optimization_barrier((ahead, prior))
     far = lax.ppermute(ahead, "tm", [(dev, (dev + half) % devices) for dev in range(devices)])
-    far_before = lax.ppermute(
-        signal[row_count - 1 :],
-        "tm",
-        [(dev, (dev + 1 + half) % devices) for dev in range(devices - 1)],
-    )
-
-    embedded = jnp.dot(patch_pairs, conv_weight, preferred_element_type=jnp.float32).astype(
-        jnp.bfloat16
-    )
-    normed = rms_scale(embedded.astype(jnp.float32), attn_gain).astype(jnp.bfloat16)
+
+    def pairs_of(block, first):
+        return jnp.concatenate([jnp.concatenate([first, block[:-1]], axis=0), block], axis=1)
+
+    def embed(pairs):
+        rows = jnp.dot(pairs, conv_weight, preferred_element_type=jnp.float32)
+        return rows.astype(jnp.bfloat16)
+
+    def norm_rows(rows):
+        return rms_scale(rows.astype(jnp.float32), attn_gain).astype(jnp.bfloat16)
+
+    patch_pairs = pairs_of(signal, before)
+    embedded = embed(patch_pairs)
+    normed = norm_rows(embedded)
     kv_heads = w_keyval.shape[1] // 2 // HEAD_DIM
     own_kv = project_kv(normed, w_keyval)
-    kv_parts, numbers = window_parts(own_kv, group)
+    prior_pairs = pairs_of(prior[:row_count], prior[row_count : row_count + 1])
+    prior_kv = project_kv(norm_rows(embed(prior_pairs)), w_keyval)
+    kv_parts, flags, sent = window_parts(own_kv, prior_kv, group)
     queries = jnp.dot(normed, w_query, preferred_element_type=jnp.float32)
-    context = attend((numbers >= 0).astype(jnp.int32), head_scale, queries, kv_parts, kv_heads)
-
-    far, _ = lax.optimization_barrier((far, own_kv))
+    context = attend(flags, head_scale, queries, kv_parts, kv_heads)
+
+    far, _ = lax.optimization_barrier((far, sent))
     in_first = dev_index < half
-    far_signal = far[:row_count]
-    far_previous = jnp.concatenate([far_before, far_signal[:-1]], axis=0)
-    far_pairs = jnp.concatenate([far_previous, far_signal], axis=1)
-    both_pairs = jnp.concatenate(
-        [jnp.where(in_first, patch_pairs, far_pairs), jnp.where(in_first, far_pairs, patch_pairs)]
-    )
-    far_tables = far[row_count:used].astype(jnp.int32).reshape(2, 2, row_count)
-    far_key = far_tables[0] * CAP + far_tables[1]
-    own_key = route_key.T
-    both_keys = jnp.stack(
-        [jnp.where(in_first, own_key, far_key), jnp.where(in_first, far_key, own_key)]
-    )
-    span = experts * CAP
-    both_keys = both_keys + span * jnp.arange(2, dtype=jnp.int32)[:, None, None]
-    both_keys = both_keys.transpose(1, 0, 2).reshape(2, 1, 2 * row_count)
-    place = jnp.arange(half * 2 * local_count * CAP, dtype=jnp.int32)
-    place_slot = place % CAP
-    place_local = place // CAP % local_count
-    place_block = place // (CAP * local_count) % 2
-    place_dev = place // (CAP * local_count * 2) + jnp.where(in_first, 0, half)
-    place_key = (place_dev // copies * local_count + place_local) * CAP + place_slot
-    place_key = (place_key + span * place_block)[:, None]
-    both_hot = (place_key == both_keys[0]) | (place_key == both_keys[1])
-    pairs_out = jnp.dot(
-        both_hot.astype(jnp.bfloat16), both_pairs, preferred_element_type=jnp.float32
-    ).astype(jnp.bfloat16)
-    pairs_out, _ = lax.optimization_barrier((pairs_out, kv_parts[1:-1]))
+    info = jnp.stack([jnp.where(in_first, 0, half), jnp.where(in_first, 0, 1)]).astype(jnp.int32)
+    pairs_out = spread_pairs(info, signal, before, route_key.T, far, half, copies, local_count)
+    pairs_out, _ = lax.optimization_barrier((pairs_out, kv_parts[2:-1]))
     pairs_in = lax.all_to_all(
         pairs_out.reshape(half, 2 * local_count * CAP, -1),
         "tm",
@@ -373,11 +419,7 @@
     pairs_in = pairs_in.reshape(half, 2, local_count, CAP, -1)
 
     placed = [
-        jnp.dot(
-            pairs_in[:, :, local].transpose(1, 0, 2, 3).reshape(slots, -1),
-            conv_weight,
-            preferred_element_type=jnp.float32,
-        ).astype(jnp.bfloat16)
+        embed(pairs_in[:, :, local].transpose(1, 0, 2, 3).reshape(slots, -1))
         for local in range(local_count)
     ]
     context_in = []
@@ -396,6 +438,8 @@
         result = run_expert(mid, ffn_gain, expert_in, expert_out, local, local_count)
         returned.append(exchange(result.reshape(devices, CAP, feat_dim)).reshape(slots, feat_dim))
 
+    expert_ids, slot_ids, _ = lax.optimization_barrier((expert_ids, slot_ids, context))
+    route_key = expert_ids * CAP + slot_ids
     stream_mid = (
         embedded.astype(jnp.float32) + jnp.dot(context, w_out, preferred_element_type=jnp.float32)
     ).astype(jnp.bfloat16)

time: 263 us -> 251 us (0.954)
  starting transfers between devices: 54.9 us -> 41.4 us
  waiting for transfers between devices: 81.3 us -> 88 us
  Pallas kernels: 58.4 us -> 62.4 us
  other arithmetic: 9.14 us -> 5.35 us
  local copies, waits for them, and re-layouts: 21.5 us -> 18.5 us
    ppermute x4 -> x3, starting transfers between devices: 18 us -> 3.49 us  [window_parts(): lax.ppermute(block, 'tm', [(dev, dev ^ 2 * step) for dev in range(devices)])]
    ppermute x2, starting transfers between devices: 5.42 us -> 10.8 us  [from_behind(): return lax.ppermute(block, axis, route)]
    ppermute x1, waiting for transfers between devices: 0.01 us -> 4.98 us  [shards(): lax.ppermute(ahead, 'tm', [(dev, (dev + half) % devices) for dev in range...]
    all_to_all x1, starting transfers between devices: 9.67 us -> 4.84 us  [shards(): lax.all_to_all(pairs_out.reshape(half, 2 * local_count * CAP, -1), 'tm',...]
    pallas_call x0 -> x1, Pallas kernels: none -> 3.86 us  [spread_pairs(): pl.pallas_call(functools.partial(spread_body, (half, copies, local_count,...]
    unnamed x39 -> x42, local copies, waits for them, and re-layouts: 15.8 us -> 15.5 us
  transfers between devices with their start and end apart: 13 -> 12, of which waited for: 5 -> 8; matrix products, arithmetic and copies ran while one was open for 19% -> 15% of each run, Pallas kernels for 21% -> 23%
where the time goes in v4:
time: 251 us; the launch traced here: 250 us
  waiting for transfers between devices  88 us (35%)
  Pallas kernels  62.4 us (25%)
  starting transfers between devices  41.4 us (16%)
  matrix products  34.1 us (14%)
  local copies, waits for them, and re-layouts  18.5 us (7%)
  other arithmetic  5.35 us (2%)
    all_to_all x4, waiting for transfers between devices, exchange(): return lax.all_to_all(rows, 'tm', split_axis=0, concat_axis=0, tiled=True)  73.3 us
    pallas_call x2, Pallas kernels, run_expert(): pl.pallas_call(functools.partial(expert_body, steps), grid=(row_total //...  37 us
    all_to_all x4, starting transfers between devices, exchange(): return lax.all_to_all(rows, 'tm', split_axis=0, concat_axis=0, tiled=True)  18.5 us
    unnamed x42, local copies, waits for them, and re-layouts  15.5 us
    pallas_call x1, Pallas kernels, attend(): pl.pallas_call(functools.partial(attend_body, kv_heads), out_shape=jax.Sh...  14.4 us
    dot_general x4, matrix products, embed(): rows = jnp.dot(pairs, conv_weight, preferred_element_type=jnp.float32)  12.6 us
    ppermute x2, starting transfers between devices, from_behind(): return lax.ppermute(block, axis, route)  10.8 us
    dot_general x2, matrix products, shards(): jnp.dot(context_in[local], w_out, preferred_element_type=jnp.float32)  10.7 us
  transfers between devices with their start and end apart: 12, of which 8 were waited for; matrix products, arithmetic and copies ran while one was open for 15% of the time, Pallas kernels for 23%

profile of v4, /device:TPU:0, one launch (start us, length us, event | category | flops | bytes accessed | tf_op | source)
XLA Modules:
  0.0 250.4 jit_solution(9741274726815509195)
XLA Ops:
  0.7 2.3 collective-permute-start
  3.9 1.7 fusion.35
  5.6 8.4 %collective-permute-start.1 = (bf16[272,512]{1,0:T(8,128)(2,1)}, bf16[272,512]{1,0:T(8,128)(2,1)S(1)}, u32[]{:S(2)}, u32[]{:S(2)}) collective-permute-start(bf16[272,512]{1,0:T(8,128)(2,1)} %fusion.35), channel_id=1, source_target_pairs={{0,8},{1,9},{2,10},{3,11},{4,12},{5,13},{6,14},{7,15},{8,16},{9,17... | collective-permute-start | bytes 835592 | tf_op jit(solution)/shard_map/ppermute | solution.py:22
  14.1 3.8 %fusion.5 = (f32[256]{0:T(256)S(1)}, bf16[256,2048]{1,0:T(8,128)(2,1)S(1)}) fusion(bf16[1024,2048]{1,0:T(8,128)(2,1)} %param.14, bf16[256,512]{1,0:T(8,128)(2,1)} %signal_ref.1, bf16[255,512]{1,0:T(8,128)(2,1)} %bitcast.73, bf16[1,512]{1,0:T(2,128)(2,1)S(1)} %collective-permute-done.before_ref), kind=kOutput, calls=%fused_computation.16 | convolution fusion | flops 1077411584 | bytes 5768192 | tf_op jit(solution)/shard_map/dot_general | solution.py:389
  23.1 3.5 %collective-permute-start.6 = (bf16[272,512]{1,0:T(8,128)(2,1)}, bf16[272,512]{1,0:T(8,128)(2,1)S(1)}, u32[]{:S(2)}, u32[]{:S(2)}) collective-permute-start(bf16[272,512]{1,0:T(8,128)(2,1)} %fusion.35), channel_id=1, source_target_pairs={{0,16},{1,17},{2,18},{3,19},{4,20},{5,21},{6,22},{7,23},{8,24},{9,... | collective-permute-start | bytes 835592 | tf_op jit(solution)/shard_map/ppermute | solution.py:383
  31.1 5.0 %collective-permute-done.6.far_ref = bf16[272,512]{1,0:T(8,128)(2,1)S(1)} collective-permute-done((bf16[272,512]{1,0:T(8,128)(2,1)}, bf16[272,512]{1,0:T(8,128)(2,1)S(1)}, u32[]{:S(2)}, u32[]{:S(2)}) %collective-permute-start.6) | collective-permute-done | bytes 278560 | tf_op jit(solution)/shard_map/ppermute | solution.py:383
  36.0 3.9 %shard_map.130 = bf16[1024,1024]{1,0:T(8,128)(2,1)} custom-call(s32[2]{0:T(128)S(1)} %pad_add_fusion.info_ref, bf16[256,512]{1,0:T(8,128)(2,1)S(1)} %copy-done.10, bf16[1,512]{1,0:T(2,128)(2,1)S(1)} %collective-permute-done.before_ref, s32[2,256]{1,0:T(2,128)S(1)} %bitcast.82, bf16[272,512]{1,0:T(8,128)(2,1)S(1)} %collective-permute-done.6.far_ref), custom_call_target="tpu_custom_call" | custom-call | flops 1073741824 | bytes 2621440 | tf_op jit(solution)/shard_map/pallas_call | solution.py:144
  40.7 4.8 %all-to-all-start = ((bf16[16,64,1024]{2,1,0:T(8,128)(2,1)}), bf16[16,64,1024]{2,1,0:T(8,128)(2,1)}, u32[]{:S(2)}, u32[]{:S(2)}) async-start(bf16[16,64,1024]{2,1,0:T(8,128)(2,1)} %bitcast.19), calls=%async_computation | async-start | bytes 4194304 | tf_op jit(solution)/shard_map/all_to_all | solution.py:411
  47.1 3.5 %fusion.58.query_ref = f32[256,1024]{1,0:T(8,128)S(1)} fusion(bf16[256,2048]{1,0:T(8,128)(2,1)S(1)} %get-tuple-element.32.rows_ref, bf16[2048,1024]{1,0:T(8,128)(2,1)} %param.16), kind=kOutput, calls=%fused_computation.105 | convolution fusion | flops 1073741824 | bytes 6291456 | tf_op jit(solution)/shard_map/dot_general | solution.py:403
  50.6 14.4 %shard_map.129 = bf16[256,1024]{1,0:T(8,128)(2,1)S(1)} custom-call(s32[9]{0:T(128)S(1)} %convert_element_type.68.flag_ref, f32[8]{0:T(128)S(1)} %copy-done.12, f32[256,1024]{1,0:T(8,128)S(1)} %fusion.58.query_ref, bf16[1,256,512]{2,1,0:T(8,128)(2,1)S(1)} %bitcast.71, bf16[1,256,512]{2,1,0:T(8,128)(2,1)S(1)} %bitcast.72, bf16[1,256,512]{2,1,0:T(8,128)(2,1)S(1)} %bitcast.75, ...), custom_call_target="tpu_custom_call" | custom-call | flops 3623878656 | bytes 3932160 | tf_op jit(solution)/shard_map/pallas_call | solution.py:289
  66.4 8.5 %all-to-all-done = bf16[16,64,1024]{2,1,0:T(8,128)(2,1)} async-done(((bf16[16,64,1024]{2,1,0:T(8,128)(2,1)}), bf16[16,64,1024]{2,1,0:T(8,128)(2,1)}, u32[]{:S(2)}, u32[]{:S(2)}) %all-to-all-start) | async-done | bytes 2097184 | tf_op jit(solution)/shard_map/all_to_all | solution.py:411
  74.9 6.0 %all-to-all-start.1 = ((bf16[32,16,1024]{2,1,0:T(8,128)(2,1)}), bf16[32,16,1024]{2,1,0:T(8,128)(2,1)S(1)}, u32[]{:S(2)}, u32[]{:S(2)}) async-start(bf16[32,16,1024]{2,1,0:T(8,128)(2,1)} %bitcast.27), calls=%async_computation.1 | async-start | bytes 2097152 | tf_op jit(solution)/shard_map/all_to_all | solution.py:369
  82.4 1.7 slice_bitcast_fusion
  84.3 2.0 copy-done.19
  86.3 3.7 %convolution_convert_fusion = bf16[512,2048]{1,0:T(8,128)(2,1)} fusion(bf16[512,1024]{1,0:T(8,128)(2,1)S(1)} %bitcast.85, bf16[1024,2048]{1,0:T(8,128)(2,1)S(1)} %copy-done.19), kind=kOutput, calls=%fused_computation.5 | convolution fusion | flops 2148532224 | bytes 7340032 | tf_op jit(solution)/shard_map/dot_general | solution.py:389
  90.0 3.7 %convolution_convert_fusion.1 = bf16[512,2048]{1,0:T(8,128)(2,1)} fusion(bf16[512,1024]{1,0:T(8,128)(2,1)S(1)} %bitcast.86, bf16[1024,2048]{1,0:T(8,128)(2,1)S(1)} %copy-done.19), kind=kOutput, calls=%fused_computation.6 | convolution fusion | flops 2148532224 | bytes 7340032 | tf_op jit(solution)/shard_map/dot_general | solution.py:389
  93.7 13.3 %all-to-all-done.1 = bf16[32,16,1024]{2,1,0:T(8,128)(2,1)S(1)} async-done(((bf16[32,16,1024]{2,1,0:T(8,128)(2,1)}), bf16[32,16,1024]{2,1,0:T(8,128)(2,1)S(1)}, u32[]{:S(2)}, u32[]{:S(2)}) %all-to-all-start.1) | async-done | bytes 1048608 | tf_op jit(solution)/shard_map/all_to_all | solution.py:369
  107.0 3.6 %all-to-all-start.3 = ((bf16[32,16,1024]{2,1,0:T(8,128)(2,1)}), bf16[32,16,1024]{2,1,0:T(8,128)(2,1)S(1)}, u32[]{:S(2)}, u32[]{:S(2)}) async-start(bf16[32,16,1024]{2,1,0:T(8,128)(2,1)} %bitcast.32), calls=%async_computation.3 | async-start | bytes 2097152 | tf_op jit(solution)/shard_map/all_to_all | solution.py:369
  110.6 5.2 %add_convert_fusion.1.mid_ref = bf16[512,2048]{1,0:T(8,128)(2,1)S(1)} fusion(bf16[512,2048]{1,0:T(8,128)(2,1)} %convolution_convert_fusion.1, bf16[512,1024]{1,0:T(8,128)(2,1)S(1)} %bitcast.83, bf16[1024,2048]{1,0:T(8,128)(2,1)} %param.18), kind=kOutput, calls=%fused_computation.1 | convolution fusion | flops 2150629376 | bytes 9437184 | tf_op jit(solution)/shard_map/dot_general | solution.py:436
  115.8 18.5 %shard_map.131 = bf16[512,2048]{1,0:T(8,128)(2,1)S(1)} custom-call(bf16[512,2048]{1,0:T(8,128)(2,1)S(1)} %add_convert_fusion.1.mid_ref, f32[1,2048]{1,0:T(1,128)S(1)} %bitcast.80, bf16[2,2816,2048]{2,1,0:T(8,128)(2,1)} %w_in_ref.3, bf16[2816,2048]{1,0:T(8,128)(2,1)} %w_out_ref.3), custom_call_target="tpu_custom_call" | custom-call | flops 8858370048 | bytes 21495808 | tf_op jit(solution)/shard_map/pallas_call | solution.py:71
  137.8 4.9 %all-to-all-start.2 = ((bf16[32,16,2048]{2,1,0:T(8,128)(2,1)}), bf16[32,16,2048]{2,1,0:T(8,128)(2,1)S(1)}, u32[]{:S(2)}, u32[]{:S(2)}) async-start(bf16[32,16,2048]{2,1,0:T(8,128)(2,1)} %bitcast.70), calls=%async_computation.2 | async-start | bytes 4194304 | tf_op jit(solution)/shard_map/all_to_all | solution.py:369
  142.7 5.5 %add_convert_fusion.mid_ref = bf16[512,2048]{1,0:T(8,128)(2,1)S(1)} fusion(bf16[512,2048]{1,0:T(8,128)(2,1)} %convolution_convert_fusion, bf16[512,1024]{1,0:T(8,128)(2,1)} %bitcast.84, bf16[1024,2048]{1,0:T(8,128)(2,1)} %param.18), kind=kOutput, calls=%fused_computation | convolution fusion | flops 2150629376 | bytes 9437184 | tf_op jit(solution)/shard_map/dot_general | solution.py:436
  148.3 18.5 %shard_map.133 = bf16[512,2048]{1,0:T(8,128)(2,1)S(1)} custom-call(bf16[512,2048]{1,0:T(8,128)(2,1)S(1)} %add_convert_fusion.mid_ref, f32[1,2048]{1,0:T(1,128)S(1)} %bitcast.81, bf16[2,2816,2048]{2,1,0:T(8,128)(2,1)} %w_in_ref.3, bf16[2816,2048]{1,0:T(8,128)(2,1)} %w_out_ref.3), custom_call_target="tpu_custom_call" | custom-call | flops 8858370048 | bytes 21495808 | tf_op jit(solution)/shard_map/pallas_call | solution.py:71
  168.2 23.3 %all-to-all-done.2 = bf16[32,16,2048]{2,1,0:T(8,128)(2,1)S(1)} async-done(((bf16[32,16,2048]{2,1,0:T(8,128)(2,1)}), bf16[32,16,2048]{2,1,0:T(8,128)(2,1)S(1)}, u32[]{:S(2)}, u32[]{:S(2)}) %all-to-all-start.2) | async-done | bytes 2097184 | tf_op jit(solution)/shard_map/all_to_all | solution.py:369
  192.8 3.9 %all-to-all-start.4 = ((bf16[32,16,2048]{2,1,0:T(8,128)(2,1)}), bf16[32,16,2048]{2,1,0:T(8,128)(2,1)S(1)}, u32[]{:S(2)}, u32[]{:S(2)}) async-start(bf16[32,16,2048]{2,1,0:T(8,128)(2,1)} %bitcast.69), calls=%async_computation.4 | async-start | bytes 4194304 | tf_op jit(solution)/shard_map/all_to_all | solution.py:369
  197.0 3.9 %multiply_reduce_fusion = (f32[256]{0:T(256)S(1)}, f32[256,2048]{1,0:T(8,128)S(1)}) fusion(bf16[256,1024]{1,0:T(8,128)(2,1)S(1)} %shard_map.129, bf16[1024,2048]{1,0:T(8,128)(2,1)} %param.18, bf16[256,2048]{1,0:T(8,128)(2,1)} %copy-done.14), kind=kOutput, calls=%fused_computation.20 | convolution fusion | flops 1076887296 | bytes 7865344 | tf_op jit(solution)/shard_map/dot_general | solution.py:444
  203.1 1.6 copy-done.4
  204.7 1.6 copy-done.6
  206.3 2.4 shard_map.132.base_ref
  210.0 35.6 %all-to-all-done.4 = bf16[32,16,2048]{2,1,0:T(8,128)(2,1)S(1)} async-done(((bf16[32,16,2048]{2,1,0:T(8,128)(2,1)}), bf16[32,16,2048]{2,1,0:T(8,128)(2,1)S(1)}, u32[]{:S(2)}, u32[]{:S(2)}) %all-to-all-start.4) | async-done | bytes 2097184 | tf_op jit(solution)/shard_map/all_to_all | solution.py:369
  245.7 1.6 copy-done.2
  247.2 3.1 %shard_map.134 = bf16[256,2048]{1,0:T(8,128)(2,1)} custom-call(f32[256,2048]{1,0:T(8,128)S(1)} %copy-done.2, f32[256,2]{1,0:T(8,128)S(1)} %broadcast_divide_fusion.weight_ref, s32[256,2]{1,0:T(8,128)S(1)} %copy.56.key_ref, s32[1,512]{1,0:T(1,128)S(1)} %multiply_add_fusion.row_ref, bf16[512,2048]{1,0:T(8,128)(2,1)S(1)} %bitcast.67), custom_call_target="tpu_custom_call" | custom-call | flops 1073741824 | bytes 6291456 | tf_op jit(solution)/shard_map/pallas_call | solution.py:179
  (80 shorter events, 26.4 us)
Async XLA Ops:
  0.0 200.9 %copy-start = (bf16[2048,64]{0,1:T(8,128)(2,1)S(1)}, bf16[2048,64]{0,1:T(8,128)(2,1)}, u32[]{:S(2)}) copy-start(bf16[2048,64]{0,1:T(8,128)(2,1)} %param.21) | copy-start | bytes 786436
  0.7 3.2 %collective-permute-start = (bf16[1,512]{1,0:T(2,128)(2,1)S(1)}, bf16[1,512]{1,0:T(2,128)(2,1)S(1)}, u32[]{:S(2)}, u32[]{:S(2)}) collective-permute-start(bf16[1,512]{1,0:T(2,128)(2,1)S(1)} %slice.30), channel_id=1, source_target_pairs={{0,1},{1,2},{2,3},{3,4},{4,5},{5,6},{6,7},{7,8},{8,9},{9,10},{10,1... | collective-permute-start | bytes 3080 | tf_op jit(solution)/shard_map/ppermute | solution.py:22
  5.6 12.8 %collective-permute-start.1 = (bf16[272,512]{1,0:T(8,128)(2,1)}, bf16[272,512]{1,0:T(8,128)(2,1)S(1)}, u32[]{:S(2)}, u32[]{:S(2)}) collective-permute-start(bf16[272,512]{1,0:T(8,128)(2,1)} %fusion.35), channel_id=1, source_target_pairs={{0,8},{1,9},{2,10},{3,11},{4,12},{5,13},{6,14},{7,15},{8,16},{9,17... | collective-permute-start | bytes 835592 | tf_op jit(solution)/shard_map/ppermute | solution.py:22
  14.1 4.4 %copy-start.18 = (bf16[1024,2048]{1,0:T(8,128)(2,1)S(1)}, bf16[1024,2048]{1,0:T(8,128)(2,1)}, u32[]{:S(2)}) copy-start(bf16[1024,2048]{1,0:T(8,128)(2,1)} %param.14) | copy-start | bytes 12582916
  17.9 1.9 copy-start.14
  18.5 1.4 copy-start.16
  19.9 1.6 copy-start.7
  22.3 13.8 %copy-start.10 = (bf16[256,512]{1,0:T(8,128)(2,1)S(1)}, bf16[256,512]{1,0:T(8,128)(2,1)}, u32[]{:S(2)}) copy-start(bf16[256,512]{1,0:T(8,128)(2,1)} %signal_ref.1) | copy-start | bytes 786436
  23.1 13.0 %collective-permute-start.6 = (bf16[272,512]{1,0:T(8,128)(2,1)}, bf16[272,512]{1,0:T(8,128)(2,1)S(1)}, u32[]{:S(2)}, u32[]{:S(2)}) collective-permute-start(bf16[272,512]{1,0:T(8,128)(2,1)} %fusion.35), channel_id=1, source_target_pairs={{0,16},{1,17},{2,18},{3,19},{4,20},{5,21},{6,22},{7,23},{8,24},{9,... | collective-permute-start | bytes 835592 | tf_op jit(solution)/shard_map/ppermute | solution.py:383
  27.5 12.4 %collective-permute-start.2 = (bf16[256,512]{1,0:T(8,128)(2,1)}, bf16[256,512]{1,0:T(8,128)(2,1)S(1)}, u32[]{:S(2)}, u32[]{:S(2)}) collective-permute-start(bf16[256,512]{1,0:T(8,128)(2,1)} %get-tuple-element.30), channel_id=1, source_target_pairs={{0,2},{1,3},{2,0},{3,1},{4,6},{5,7},{6,4},{7,5},{8,10},{9,11},{10,... | collective-permute-start | bytes 786440 | tf_op jit(solution)/shard_map/ppermute | solution.py:319
  28.7 12.0 %collective-permute-start.3 = (bf16[256,512]{1,0:T(8,128)(2,1)}, bf16[256,512]{1,0:T(8,128)(2,1)S(1)}, u32[]{:S(2)}, u32[]{:S(2)}) collective-permute-start(bf16[256,512]{1,0:T(8,128)(2,1)} %get-tuple-element.29), channel_id=1, source_target_pairs={{0,4},{1,5},{2,6},{3,7},{4,0},{5,1},{6,2},{7,3},{8,12},{9,13},{10,... | collective-permute-start | bytes 786440 | tf_op jit(solution)/shard_map/ppermute | solution.py:319
  30.2 10.5 %collective-permute-start.4 = (bf16[256,512]{1,0:T(8,128)(2,1)}, bf16[256,512]{1,0:T(8,128)(2,1)S(1)}, u32[]{:S(2)}, u32[]{:S(2)}) collective-permute-start(bf16[256,512]{1,0:T(8,128)(2,1)} %get-tuple-element.28), channel_id=1, source_target_pairs={{0,6},{1,7},{2,4},{3,5},{4,2},{5,3},{6,0},{7,1},{8,14},{9,15},{10,... | collective-permute-start | bytes 786440 | tf_op jit(solution)/shard_map/ppermute | solution.py:319
  40.7 34.2 %all-to-all-start = ((bf16[16,64,1024]{2,1,0:T(8,128)(2,1)}), bf16[16,64,1024]{2,1,0:T(8,128)(2,1)}, u32[]{:S(2)}, u32[]{:S(2)}) async-start(bf16[16,64,1024]{2,1,0:T(8,128)(2,1)} %bitcast.19), calls=%async_computation | async-start | bytes 4194304 | tf_op jit(solution)/shard_map/all_to_all | solution.py:411
  46.6 4.0 %collective-permute-start.5 = (bf16[4,256,512]{2,1,0:T(8,128)(2,1)}, bf16[4,256,512]{2,1,0:T(8,128)(2,1)}, u32[]{:S(2)}, u32[]{:S(2)}) collective-permute-start(bf16[4,256,512]{2,1,0:T(8,128)(2,1)} %pad_maximum_fusion), channel_id=1, source_target_pairs={{0,1},{1,0},{2,3},{3,2},{4,5},{5,4},{6,7},{7,6},{8,9},{9,8},{10,11... | collective-permute-start | bytes 3145736 | tf_op jit(solution)/shard_map/ppermute | solution.py:323
  47.1 3.5 %copy-start.12 = (f32[8]{0:T(128)S(1)}, f32[8]{0:T(128)}, u32[]{:S(2)}) copy-start(f32[8]{0:T(128)} %scale_ref.1) | copy-start | bytes 100
  74.9 32.1 %all-to-all-start.1 = ((bf16[32,16,1024]{2,1,0:T(8,128)(2,1)}), bf16[32,16,1024]{2,1,0:T(8,128)(2,1)S(1)}, u32[]{:S(2)}, u32[]{:S(2)}) async-start(bf16[32,16,1024]{2,1,0:T(8,128)(2,1)} %bitcast.27), calls=%async_computation.1 | async-start | bytes 2097152 | tf_op jit(solution)/shard_map/all_to_all | solution.py:369
  84.1 2.2 copy-start.19
  107.0 29.9 %all-to-all-start.3 = ((bf16[32,16,1024]{2,1,0:T(8,128)(2,1)}), bf16[32,16,1024]{2,1,0:T(8,128)(2,1)S(1)}, u32[]{:S(2)}, u32[]{:S(2)}) async-start(bf16[32,16,1024]{2,1,0:T(8,128)(2,1)} %bitcast.32), calls=%async_computation.3 | async-start | bytes 2097152 | tf_op jit(solution)/shard_map/all_to_all | solution.py:369
  110.6 5.2 %copy-start.11 = (f32[2048]{0:T(1024)S(1)}, f32[2048]{0:T(1024)}, u32[]{:S(2)}) copy-start(f32[2048]{0:T(1024)} %param.20) | copy-start | bytes 24580
  134.4 1.3 copy-start.9
  136.8 1.0 copy-start.13
  137.8 53.7 %all-to-all-start.2 = ((bf16[32,16,2048]{2,1,0:T(8,128)(2,1)}), bf16[32,16,2048]{2,1,0:T(8,128)(2,1)S(1)}, u32[]{:S(2)}, u32[]{:S(2)}) async-start(bf16[32,16,2048]{2,1,0:T(8,128)(2,1)} %bitcast.70), calls=%async_computation.2 | async-start | bytes 4194304 | tf_op jit(solution)/shard_map/all_to_all | solution.py:369
  166.8 1.4 copy-start.8
  191.5 1.3 copy-start.3
  192.8 4.0 %copy-start.15 = (s32[256,2]{0,1:T(2,128)S(1)}, s32[256,2]{0,1:T(2,128)}, u32[]{:S(2)}) copy-start(s32[256,2]{0,1:T(2,128)} %param.24) | copy-start | bytes 6148
  192.8 4.0 %copy-start.17 = (s32[256,2]{0,1:T(2,128)S(1)}, s32[256,2]{0,1:T(2,128)}, u32[]{:S(2)}) copy-start(s32[256,2]{0,1:T(2,128)} %param.25) | copy-start | bytes 6148
  192.8 52.8 %all-to-all-start.4 = ((bf16[32,16,2048]{2,1,0:T(8,128)(2,1)}), bf16[32,16,2048]{2,1,0:T(8,128)(2,1)S(1)}, u32[]{:S(2)}, u32[]{:S(2)}) async-start(bf16[32,16,2048]{2,1,0:T(8,128)(2,1)} %bitcast.69), calls=%async_computation.4 | async-start | bytes 4194304 | tf_op jit(solution)/shard_map/all_to_all | solution.py:369
  201.4 1.4 copy-start.5
  203.1 1.6 copy-start.4
  204.7 1.6 copy-start.6
  208.7 1.3 copy-start.1
  245.6 1.6 copy-start.2

commit v5 on v4

--- a/solution.py
+++ b/solution.py
@@ -162,11 +162,16 @@
     )(info, signal, before, keys, far)
 
 
-def combine_body(base_ref, weight_ref, key_ref, row_ref, rows_ref, out_ref):
+def combine_body(base_ref, weight_ref, key_ref, row_ref, rows_ref, out_ref, hot_ref):
+    @pl.when(pl.program_id(0) == 0)
+    def _():
+        for route in range(2):
+            hot = key_ref[:, route : route + 1] == row_ref[...]
+            hot_ref[route] = hot.astype(jnp.bfloat16)
+
     total = base_ref[...]
     for route in range(2):
-        hot = (key_ref[:, route : route + 1] == row_ref[...]).astype(jnp.bfloat16)
-        rows = jnp.dot(hot, rows_ref[...], preferred_element_type=jnp.float32)
+        rows = jnp.dot(hot_ref[route], rows_ref[...], preferred_element_type=jnp.float32)
         rows = rows.astype(jnp.bfloat16).astype(jnp.float32)
         total = total + weight_ref[:, route : route + 1] * rows
     out_ref[...] = total.astype(out_ref.dtype)
@@ -188,13 +193,14 @@
         ],
         out_specs=pl.BlockSpec((row_count, width), lambda i: (0, i)),
         out_shape=jax.ShapeDtypeStruct((row_count, feat_dim), kind),
+        scratch_shapes=[pltpu.VMEM((2, row_count, slots), jnp.bfloat16)],
         compiler_params=pltpu.CompilerParams(vmem_limit_bytes=24 << 20),
         cost_estimate=pl.CostEstimate(
             flops=4 * row_count * slots * feat_dim,
             bytes_accessed=2 * slots * feat_dim + 8 * row_count * feat_dim,
             transcendentals=0,
         ),
-    )(base, weight, key, row_key.reshape(1, -1), rows)
+    )(base, weight, key, row_key.reshape(1, -1), pltpu.with_memory_space_constraint(rows, pltpu.HBM))
 
 
 def kv_body(rows_ref, weight_ref, out_ref):
@@ -371,15 +377,14 @@
     reach_blocks = WINDOW // row_count
     group = reach_blocks
     before = from_behind(signal[row_count - 1 :], "tm", 1)
+    prior = from_behind(signal, "tm", group)
+    prior_before = from_behind(signal[row_count - 1 :], "tm", group + 1)
     half = devices // 2
     routes = [
         table.astype(jnp.bfloat16).T.reshape(-1, signal.shape[1]) for table in (expert_ids, slot_ids)
     ]
     ahead = jnp.concatenate([signal, before] + routes, axis=0)
-    used = ahead.shape[0]
-    ahead = jnp.pad(ahead, ((0, -used % 16), (0, 0)))
-    prior = from_behind(ahead, "tm", group)
-    ahead, prior = lax.optimization_barrier((ahead, prior))
+    ahead = jnp.pad(ahead, ((0, -ahead.shape[0] % 16), (0, 0)))
     far = lax.ppermute(ahead, "tm", [(dev, (dev + half) % devices) for dev in range(devices)])
 
     def pairs_of(block, first):
@@ -397,7 +402,7 @@
     normed = norm_rows(embedded)
     kv_heads = w_keyval.shape[1] // 2 // HEAD_DIM
     own_kv = project_kv(normed, w_keyval)
-    prior_pairs = pairs_of(prior[:row_count], prior[row_count : row_count + 1])
+    prior_pairs = pairs_of(prior, prior_before)
     prior_kv = project_kv(norm_rows(embed(prior_pairs)), w_keyval)
     kv_parts, flags, sent = window_parts(own_kv, prior_kv, group)
     queries = jnp.dot(normed, w_query, preferred_element_type=jnp.float32)
@@ -429,15 +434,6 @@
             outgoing, placed = lax.optimization_barrier((outgoing, placed))
         context_in.append(exchange(outgoing.reshape(devices, CAP, -1)).reshape(slots, -1))
 
-    returned = []
-    for local in range(local_count):
-        mid = (
-            placed[local].astype(jnp.float32)
-            + jnp.dot(context_in[local], w_out, preferred_element_type=jnp.float32)
-        ).astype(jnp.bfloat16)
-        result = run_expert(mid, ffn_gain, expert_in, expert_out, local, local_count)
-        returned.append(exchange(result.reshape(devices, CAP, feat_dim)).reshape(slots, feat_dim))
-
     expert_ids, slot_ids, _ = lax.optimization_barrier((expert_ids, slot_ids, context))
     route_key = expert_ids * CAP + slot_ids
     stream_mid = (
@@ -449,6 +445,19 @@
     picked = jnp.sum(jnp.where(chosen_hot, affinity[:, None, :], 0.0), axis=-1)
     route_weight = picked / jnp.sum(picked, axis=1, keepdims=True)
 
+    returned = []
+    for local in range(local_count):
+        mid = (
+            placed[local].astype(jnp.float32)
+            + jnp.dot(context_in[local], w_out, preferred_element_type=jnp.float32)
+        ).astype(jnp.bfloat16)
+        result = run_expert(mid, ffn_gain, expert_in, expert_out, local, local_count)
+        if local == local_count - 1:
+            result, stream_mid, route_weight = lax.optimization_barrier(
+                (result, stream_mid, route_weight)
+            )
+        returned.append(exchange(result.reshape(devices, CAP, feat_dim)).reshape(slots, feat_dim))
+
     mixed = stream_mid.astype(jnp.float32)
     for local in range(local_count):
         kind = jnp.bfloat16 if local == local_count - 1 else jnp.float32

time: 251 us -> 247 us (0.984)
  local copies, waits for them, and re-layouts: 18.5 us -> 6.21 us
  Pallas kernels: 62.4 us -> 68 us
  waiting for transfers between devices: 88 us -> 91.5 us
    unnamed x42 -> x24, local copies, waits for them, and re-layouts: 15.5 us -> 3.18 us
    all_to_all x4, waiting for transfers between devices: 73.3 us -> 77.7 us  [exchange(): return lax.all_to_all(rows, 'tm', split_axis=0, concat_axis=0, tiled=True)]
    pallas_call x2, Pallas kernels: 5.59 us -> 8.52 us  [combine(): pl.pallas_call(combine_body, grid=(feat_dim // width,), in_specs=[pl.Bloc...]
    pallas_call x2, Pallas kernels: 37 us -> 39.7 us  [run_expert(): pl.pallas_call(functools.partial(expert_body, steps), grid=(row_total //...]
    ppermute x2 -> x3, starting transfers between devices: 10.8 us -> 11.4 us  [from_behind(): return lax.ppermute(block, axis, route)]
  transfers between devices with their start and end apart: 12 -> 13, of which waited for: 8 -> 7; matrix products, arithmetic and copies ran while one was open for 15% -> 17% of each run, Pallas kernels for 23% -> 26%
where the time goes in v5:
time: 247 us; the launch traced here: 246 us
  waiting for transfers between devices  91.5 us (37%)
  Pallas kernels  68 us (28%)
  starting transfers between devices  41.3 us (17%)
  matrix products  33.8 us (14%)
  local copies, waits for them, and re-layouts  6.21 us (3%)
  other arithmetic  4.71 us (2%)
    all_to_all x4, waiting for transfers between devices, exchange(): return lax.all_to_all(rows, 'tm', split_axis=0, concat_axis=0, tiled=True)  77.7 us
    pallas_call x2, Pallas kernels, run_expert(): pl.pallas_call(functools.partial(expert_body, steps), grid=(row_total //...  39.7 us
    all_to_all x4, starting transfers between devices, exchange(): return lax.all_to_all(rows, 'tm', split_axis=0, concat_axis=0, tiled=True)  17.8 us
    pallas_call x1, Pallas kernels, attend(): pl.pallas_call(functools.partial(attend_body, kv_heads), out_shape=jax.Sh...  14.4 us
    dot_general x4, matrix products, embed(): rows = jnp.dot(pairs, conv_weight, preferred_element_type=jnp.float32)  12.6 us
    ppermute x3, starting transfers between devices, from_behind(): return lax.ppermute(block, axis, route)  11.4 us
    dot_general x2, matrix products, shards(): jnp.dot(context_in[local], w_out, preferred_element_type=jnp.float32)  10.4 us
    pallas_call x2, Pallas kernels, combine(): pl.pallas_call(combine_body, grid=(feat_dim // width,), in_specs=[pl.Bloc...  8.52 us
  transfers between devices with their start and end apart: 13, of which 7 were waited for; matrix products, arithmetic and copies ran while one was open for 17% of the time, Pallas kernels for 26%

profile of v5, /device:TPU:0, one launch (start us, length us, event | category | flops | bytes accessed | tf_op | source)
XLA Modules:
  0.0 246.0 jit_solution(3342238144906451907)
XLA Ops:
  0.0 5.1 %collective-permute-start.2 = (bf16[256,512]{1,0:T(8,128)(2,1)}, bf16[256,512]{1,0:T(8,128)(2,1)S(1)}, u32[]{:S(2)}, u32[]{:S(2)}) collective-permute-start(bf16[256,512]{1,0:T(8,128)(2,1)} %signal_ref.1), channel_id=1, source_target_pairs={{0,8},{1,9},{2,10},{3,11},{4,12},{5,13},{6,14},{7,15},{8,16},{9,17... | collective-permute-start | bytes 786440 | tf_op jit(solution)/shard_map/ppermute | solution.py:22
  5.8 2.6 %collective-permute-start.1 = (bf16[1,512]{1,0:T(2,128)(2,1)S(1)}, bf16[1,512]{1,0:T(2,128)(2,1)S(1)}, u32[]{:S(2)}, u32[]{:S(2)}) collective-permute-start(bf16[1,512]{1,0:T(2,128)(2,1)S(1)} %slice.26), channel_id=1, source_target_pairs={{0,9},{1,10},{2,11},{3,12},{4,13},{5,14},{6,15},{7,16},{8,17},{9,1... | collective-permute-start | bytes 3080 | tf_op jit(solution)/shard_map/ppermute | solution.py:22
  8.4 3.8 %collective-permute-start = (bf16[1,512]{1,0:T(2,128)(2,1)S(1)}, bf16[1,512]{1,0:T(2,128)(2,1)S(1)}, u32[]{:S(2)}, u32[]{:S(2)}) collective-permute-start(bf16[1,512]{1,0:T(2,128)(2,1)S(1)} %slice.26), channel_id=1, source_target_pairs={{0,1},{1,2},{2,3},{3,4},{4,5},{5,6},{6,7},{7,8},{8,9},{9,10},{10,1... | collective-permute-start | bytes 3080 | tf_op jit(solution)/shard_map/ppermute | solution.py:22
  13.1 3.8 %fusion.7 = (f32[256]{0:T(256)S(1)}, bf16[256,2048]{1,0:T(8,128)(2,1)S(1)}) fusion(bf16[1024,2048]{1,0:T(8,128)(2,1)} %param.14, bf16[256,512]{1,0:T(8,128)(2,1)} %signal_ref.1, bf16[255,512]{1,0:T(8,128)(2,1)} %bitcast.70, bf16[1,512]{1,0:T(2,128)(2,1)S(1)} %collective-permute-done.before_ref), kind=kOutput, calls=%fused_computation.20 | convolution fusion | flops 1077411584 | bytes 5768192 | tf_op jit(solution)/shard_map/dot_general | solution.py:394
  17.7 3.9 %collective-permute-start.7 = (bf16[272,512]{1,0:T(8,128)(2,1)}, bf16[272,512]{1,0:T(8,128)(2,1)S(1)}, u32[]{:S(2)}, u32[]{:S(2)}) collective-permute-start(bf16[272,512]{1,0:T(8,128)(2,1)} %fusion.38), channel_id=1, source_target_pairs={{0,16},{1,17},{2,18},{3,19},{4,20},{5,21},{6,22},{7,23},{8,24},{9,... | collective-permute-start | bytes 835592 | tf_op jit(solution)/shard_map/ppermute | solution.py:388
  28.5 2.3 collective-permute-start.5
  30.8 2.8 %collective-permute-done.7.far_ref = bf16[272,512]{1,0:T(8,128)(2,1)S(1)} collective-permute-done((bf16[272,512]{1,0:T(8,128)(2,1)}, bf16[272,512]{1,0:T(8,128)(2,1)S(1)}, u32[]{:S(2)}, u32[]{:S(2)}) %collective-permute-start.7) | collective-permute-done | bytes 278560 | tf_op jit(solution)/shard_map/ppermute | solution.py:388
  33.7 3.8 %shard_map.130 = bf16[1024,1024]{1,0:T(8,128)(2,1)} custom-call(s32[2]{0:T(128)S(1)} %pad_add_fusion.info_ref, bf16[256,512]{1,0:T(8,128)(2,1)S(1)} %copy-done.2, bf16[1,512]{1,0:T(2,128)(2,1)S(1)} %collective-permute-done.before_ref, s32[2,256]{1,0:T(2,128)S(1)} %bitcast.79, bf16[272,512]{1,0:T(8,128)(2,1)S(1)} %collective-permute-done.7.far_ref), custom_call_target="tpu_custom_call" | custom-call | flops 1073741824 | bytes 2621440 | tf_op jit(solution)/shard_map/pallas_call | solution.py:144
  37.5 2.4 collective-permute-done.4
  39.9 4.4 %all-to-all-start = ((bf16[16,64,1024]{2,1,0:T(8,128)(2,1)}), bf16[16,64,1024]{2,1,0:T(8,128)(2,1)}, u32[]{:S(2)}, u32[]{:S(2)}) async-start(bf16[16,64,1024]{2,1,0:T(8,128)(2,1)} %bitcast.19), calls=%async_computation | async-start | bytes 4194304 | tf_op jit(solution)/shard_map/all_to_all | solution.py:416
  45.8 3.5 %fusion.61.query_ref = f32[256,1024]{1,0:T(8,128)S(1)} fusion(bf16[256,2048]{1,0:T(8,128)(2,1)S(1)} %get-tuple-element.34.rows_ref, bf16[2048,1024]{1,0:T(8,128)(2,1)} %param.16), kind=kOutput, calls=%fused_computation.107 | convolution fusion | flops 1073741824 | bytes 6291456 | tf_op jit(solution)/shard_map/dot_general | solution.py:408
  49.3 14.4 %shard_map.129 = bf16[256,1024]{1,0:T(8,128)(2,1)S(1)} custom-call(s32[9]{0:T(128)S(1)} %convert_element_type.68.flag_ref, f32[8]{0:T(128)S(1)} %copy-done.4, f32[256,1024]{1,0:T(8,128)S(1)} %fusion.61.query_ref, bf16[1,256,512]{2,1,0:T(8,128)(2,1)S(1)} %bitcast.68, bf16[1,256,512]{2,1,0:T(8,128)(2,1)S(1)} %bitcast.69, bf16[1,256,512]{2,1,0:T(8,128)(2,1)S(1)} %bitcast.72, ...), custom_call_target="tpu_custom_call" | custom-call | flops 3623878656 | bytes 3932160 | tf_op jit(solution)/shard_map/pallas_call | solution.py:295
  63.7 1.4 convolution_convert_fusion.4
  65.1 8.5 %all-to-all-done = bf16[16,64,1024]{2,1,0:T(8,128)(2,1)} async-done(((bf16[16,64,1024]{2,1,0:T(8,128)(2,1)}), bf16[16,64,1024]{2,1,0:T(8,128)(2,1)}, u32[]{:S(2)}, u32[]{:S(2)}) %all-to-all-start) | async-done | bytes 2097184 | tf_op jit(solution)/shard_map/all_to_all | solution.py:416
  73.6 5.1 %all-to-all-start.2 = ((bf16[32,16,1024]{2,1,0:T(8,128)(2,1)}), bf16[32,16,1024]{2,1,0:T(8,128)(2,1)S(1)}, u32[]{:S(2)}, u32[]{:S(2)}) async-start(bf16[32,16,1024]{2,1,0:T(8,128)(2,1)} %bitcast.30), calls=%async_computation.2 | async-start | bytes 2097152 | tf_op jit(solution)/shard_map/all_to_all | solution.py:375
  80.2 1.7 slice_bitcast_fusion
  82.1 2.0 copy-done.10
  84.1 3.7 %convolution_convert_fusion.1 = bf16[512,2048]{1,0:T(8,128)(2,1)} fusion(bf16[512,1024]{1,0:T(8,128)(2,1)S(1)} %bitcast.82, bf16[1024,2048]{1,0:T(8,128)(2,1)S(1)} %copy-done.10), kind=kOutput, calls=%fused_computation.6 | convolution fusion | flops 2148532224 | bytes 7340032 | tf_op jit(solution)/shard_map/dot_general | solution.py:394
  87.7 3.7 %convolution_convert_fusion = bf16[512,2048]{1,0:T(8,128)(2,1)} fusion(bf16[512,1024]{1,0:T(8,128)(2,1)S(1)} %bitcast.83, bf16[1024,2048]{1,0:T(8,128)(2,1)S(1)} %copy-done.10), kind=kOutput, calls=%fused_computation.5 | convolution fusion | flops 2148532224 | bytes 7340032 | tf_op jit(solution)/shard_map/dot_general | solution.py:394
  91.4 13.3 %all-to-all-done.2 = bf16[32,16,1024]{2,1,0:T(8,128)(2,1)S(1)} async-done(((bf16[32,16,1024]{2,1,0:T(8,128)(2,1)}), bf16[32,16,1024]{2,1,0:T(8,128)(2,1)S(1)}, u32[]{:S(2)}, u32[]{:S(2)}) %all-to-all-start.2) | async-done | bytes 1048608 | tf_op jit(solution)/shard_map/all_to_all | solution.py:375
  104.8 3.6 %all-to-all-start.1 = ((bf16[32,16,1024]{2,1,0:T(8,128)(2,1)}), bf16[32,16,1024]{2,1,0:T(8,128)(2,1)S(1)}, u32[]{:S(2)}, u32[]{:S(2)}) async-start(bf16[32,16,1024]{2,1,0:T(8,128)(2,1)} %bitcast.27), calls=%async_computation.1 | async-start | bytes 2097152 | tf_op jit(solution)/shard_map/all_to_all | solution.py:375
  108.4 5.2 %add_convert_fusion.mid_ref = bf16[512,2048]{1,0:T(8,128)(2,1)S(1)} fusion(bf16[512,2048]{1,0:T(8,128)(2,1)} %convolution_convert_fusion.1, bf16[512,1024]{1,0:T(8,128)(2,1)S(1)} %bitcast.81, bf16[1024,2048]{1,0:T(8,128)(2,1)} %param.18), kind=kOutput, calls=%fused_computation | convolution fusion | flops 2150629376 | bytes 9437184 | tf_op jit(solution)/shard_map/dot_general | solution.py:452
  113.6 19.9 %shard_map.132 = bf16[512,2048]{1,0:T(8,128)(2,1)} custom-call(bf16[512,2048]{1,0:T(8,128)(2,1)S(1)} %add_convert_fusion.mid_ref, f32[1,2048]{1,0:T(1,128)S(1)} %bitcast.77, bf16[2,2816,2048]{2,1,0:T(8,128)(2,1)} %w_in_ref.3, bf16[2816,2048]{1,0:T(8,128)(2,1)} %w_out_ref.3), custom_call_target="tpu_custom_call" | custom-call | flops 8858370048 | bytes 21495808 | tf_op jit(solution)/shard_map/pallas_call | solution.py:71
  134.6 5.1 %all-to-all-start.3 = ((bf16[32,16,2048]{2,1,0:T(8,128)(2,1)}), bf16[32,16,2048]{2,1,0:T(8,128)(2,1)}, u32[]{:S(2)}, u32[]{:S(2)}) async-start(bf16[32,16,2048]{2,1,0:T(8,128)(2,1)} %bitcast.32), calls=%async_computation.3 | async-start | bytes 4194304 | tf_op jit(solution)/shard_map/all_to_all | solution.py:375
  139.7 3.9 %fusion.4 = (f32[256]{0:T(256)S(1)}, bf16[256,2048]{1,0:T(8,128)(2,1)S(1)}) fusion(bf16[256,1024]{1,0:T(8,128)(2,1)S(1)} %shard_map.129, bf16[1024,2048]{1,0:T(8,128)(2,1)} %param.18, bf16[256,2048]{1,0:T(8,128)(2,1)} %copy-done.5), kind=kOutput, calls=%fused_computation.17 | convolution fusion | flops 1076887296 | bytes 6816768 | tf_op jit(solution)/shard_map/dot_general | solution.py:440
  144.6 5.2 %add_convert_fusion.1.mid_ref = bf16[512,2048]{1,0:T(8,128)(2,1)S(1)} fusion(bf16[512,2048]{1,0:T(8,128)(2,1)} %convolution_convert_fusion, bf16[512,1024]{1,0:T(8,128)(2,1)S(1)} %bitcast.80, bf16[1024,2048]{1,0:T(8,128)(2,1)} %param.18), kind=kOutput, calls=%fused_computation.1 | convolution fusion | flops 2150629376 | bytes 9437184 | tf_op jit(solution)/shard_map/dot_general | solution.py:452
  149.8 19.9 %shard_map.131 = bf16[512,2048]{1,0:T(8,128)(2,1)} custom-call(bf16[512,2048]{1,0:T(8,128)(2,1)S(1)} %add_convert_fusion.1.mid_ref, f32[1,2048]{1,0:T(1,128)S(1)} %bitcast.78, bf16[2,2816,2048]{2,1,0:T(8,128)(2,1)} %w_in_ref.3, bf16[2816,2048]{1,0:T(8,128)(2,1)} %w_out_ref.3), custom_call_target="tpu_custom_call" | custom-call | flops 8858370048 | bytes 21495808 | tf_op jit(solution)/shard_map/pallas_call | solution.py:71
  169.7 18.8 %all-to-all-done.3 = bf16[32,16,2048]{2,1,0:T(8,128)(2,1)} async-done(((bf16[32,16,2048]{2,1,0:T(8,128)(2,1)}), bf16[32,16,2048]{2,1,0:T(8,128)(2,1)}, u32[]{:S(2)}, u32[]{:S(2)}) %all-to-all-start.3) | async-done | bytes 2097184 | tf_op jit(solution)/shard_map/all_to_all | solution.py:375
  188.4 4.1 %all-to-all-start.4 = ((bf16[32,16,2048]{2,1,0:T(8,128)(2,1)}), bf16[32,16,2048]{2,1,0:T(8,128)(2,1)}, u32[]{:S(2)}, u32[]{:S(2)}) async-start(bf16[32,16,2048]{2,1,0:T(8,128)(2,1)} %bitcast.34), calls=%async_computation.4 | async-start | bytes 4194304 | tf_op jit(solution)/shard_map/all_to_all | solution.py:375
  192.9 3.9 %shard_map.133.base_ref = f32[256,2048]{1,0:T(8,128)S(1)} custom-call(f32[256,2048]{1,0:T(8,128)S(1)} %convert_element_type.85.base_ref, f32[256,2]{1,0:T(8,128)S(1)} %broadcast_divide_fusion.weight_ref, s32[256,2]{1,0:T(8,128)S(1)} %copy.56.key_ref, s32[1,512]{1,0:T(1,128)S(1)} %multiply_add_fusion.1.row_ref, bf16[512,2048]{1,0:T(8,128)(2,1)} %bitcast.33.rows_ref), custom_call_target="tpu_custom_call" | custom-call | flops 1073741824 | bytes 6291456 | tf_op jit(solution)/shard_map/pallas_call | solution.py:184
  196.8 44.6 %all-to-all-done.4 = bf16[32,16,2048]{2,1,0:T(8,128)(2,1)} async-done(((bf16[32,16,2048]{2,1,0:T(8,128)(2,1)}), bf16[32,16,2048]{2,1,0:T(8,128)(2,1)}, u32[]{:S(2)}, u32[]{:S(2)}) %all-to-all-start.4) | async-done | bytes 2097184 | tf_op jit(solution)/shard_map/all_to_all | solution.py:375
  241.4 4.6 %shard_map.134 = bf16[256,2048]{1,0:T(8,128)(2,1)} custom-call(f32[256,2048]{1,0:T(8,128)S(1)} %shard_map.133.base_ref, f32[256,2]{1,0:T(8,128)S(1)} %broadcast_divide_fusion.weight_ref, s32[256,2]{1,0:T(8,128)S(1)} %copy.56.key_ref, s32[1,512]{1,0:T(1,128)S(1)} %multiply_add_fusion.row_ref, bf16[512,2048]{1,0:T(8,128)(2,1)} %bitcast.35.rows_ref), custom_call_target="tpu_custom_call" | custom-call | flops 1073741824 | bytes 6291456 | tf_op jit(solution)/shard_map/pallas_call | solution.py:184
  (63 shorter events, 14.7 us)
Async XLA Ops:
  0.0 143.6 %copy-start = (bf16[2048,64]{0,1:T(8,128)(2,1)S(1)}, bf16[2048,64]{0,1:T(8,128)(2,1)}, u32[]{:S(2)}) copy-start(bf16[2048,64]{0,1:T(8,128)(2,1)} %param.21) | copy-start | bytes 786436
  0.0 21.7 %collective-permute-start.2 = (bf16[256,512]{1,0:T(8,128)(2,1)}, bf16[256,512]{1,0:T(8,128)(2,1)S(1)}, u32[]{:S(2)}, u32[]{:S(2)}) collective-permute-start(bf16[256,512]{1,0:T(8,128)(2,1)} %signal_ref.1), channel_id=1, source_target_pairs={{0,8},{1,9},{2,10},{3,11},{4,12},{5,13},{6,14},{7,15},{8,16},{9,17... | collective-permute-start | bytes 786440 | tf_op jit(solution)/shard_map/ppermute | solution.py:22
  5.8 15.8 %collective-permute-start.1 = (bf16[1,512]{1,0:T(2,128)(2,1)S(1)}, bf16[1,512]{1,0:T(2,128)(2,1)S(1)}, u32[]{:S(2)}, u32[]{:S(2)}) collective-permute-start(bf16[1,512]{1,0:T(2,128)(2,1)S(1)} %slice.26), channel_id=1, source_target_pairs={{0,9},{1,10},{2,11},{3,12},{4,13},{5,14},{6,15},{7,16},{8,17},{9,1... | collective-permute-start | bytes 3080 | tf_op jit(solution)/shard_map/ppermute | solution.py:22
  8.4 4.6 %collective-permute-start = (bf16[1,512]{1,0:T(2,128)(2,1)S(1)}, bf16[1,512]{1,0:T(2,128)(2,1)S(1)}, u32[]{:S(2)}, u32[]{:S(2)}) collective-permute-start(bf16[1,512]{1,0:T(2,128)(2,1)S(1)} %slice.26), channel_id=1, source_target_pairs={{0,1},{1,2},{2,3},{3,4},{4,5},{5,6},{6,7},{7,8},{8,9},{9,10},{10,1... | collective-permute-start | bytes 3080 | tf_op jit(solution)/shard_map/ppermute | solution.py:22
  13.0 3.9 %copy-start.2 = (bf16[256,512]{1,0:T(8,128)(2,1)S(1)}, bf16[256,512]{1,0:T(8,128)(2,1)}, u32[]{:S(2)}) copy-start(bf16[256,512]{1,0:T(8,128)(2,1)} %signal_ref.1) | copy-start | bytes 786436
  13.1 8.6 %copy-start.9 = (bf16[1024,2048]{1,0:T(8,128)(2,1)S(1)}, bf16[1024,2048]{1,0:T(8,128)(2,1)}, u32[]{:S(2)}) copy-start(bf16[1024,2048]{1,0:T(8,128)(2,1)} %param.14) | copy-start | bytes 12582916
  16.9 6.2 %copy-start.5 = (bf16[256,2048]{1,0:T(8,128)(2,1)}, bf16[256,2048]{1,0:T(8,128)(2,1)S(1)}, u32[]{:S(2)}) copy-start(bf16[256,2048]{1,0:T(8,128)(2,1)S(1)} %get-tuple-element.43) | copy-start | bytes 3145732
  17.7 15.9 %collective-permute-start.7 = (bf16[272,512]{1,0:T(8,128)(2,1)}, bf16[272,512]{1,0:T(8,128)(2,1)S(1)}, u32[]{:S(2)}, u32[]{:S(2)}) collective-permute-start(bf16[272,512]{1,0:T(8,128)(2,1)} %fusion.38), channel_id=1, source_target_pairs={{0,16},{1,17},{2,18},{3,19},{4,20},{5,21},{6,22},{7,23},{8,24},{9,... | collective-permute-start | bytes 835592 | tf_op jit(solution)/shard_map/ppermute | solution.py:388
  21.7 1.4 copy-start.7
  23.1 1.6 copy-start.1
  27.3 10.3 %collective-permute-start.3 = (bf16[256,512]{1,0:T(8,128)(2,1)}, bf16[256,512]{1,0:T(8,128)(2,1)S(1)}, u32[]{:S(2)}, u32[]{:S(2)}) collective-permute-start(bf16[256,512]{1,0:T(8,128)(2,1)} %get-tuple-element.32), channel_id=1, source_target_pairs={{0,2},{1,3},{2,0},{3,1},{4,6},{5,7},{6,4},{7,5},{8,10},{9,11},{10,... | collective-permute-start | bytes 786440 | tf_op jit(solution)/shard_map/ppermute | solution.py:325
  27.3 12.6 %collective-permute-start.4 = (bf16[256,512]{1,0:T(8,128)(2,1)}, bf16[256,512]{1,0:T(8,128)(2,1)S(1)}, u32[]{:S(2)}, u32[]{:S(2)}) collective-permute-start(bf16[256,512]{1,0:T(8,128)(2,1)} %get-tuple-element.31), channel_id=1, source_target_pairs={{0,4},{1,5},{2,6},{3,7},{4,0},{5,1},{6,2},{7,3},{8,12},{9,13},{10,... | collective-permute-start | bytes 786440 | tf_op jit(solution)/shard_map/ppermute | solution.py:325
  28.5 11.4 %collective-permute-start.5 = (bf16[256,512]{1,0:T(8,128)(2,1)}, bf16[256,512]{1,0:T(8,128)(2,1)S(1)}, u32[]{:S(2)}, u32[]{:S(2)}) collective-permute-start(bf16[256,512]{1,0:T(8,128)(2,1)} %get-tuple-element.30), channel_id=1, source_target_pairs={{0,6},{1,7},{2,4},{3,5},{4,2},{5,3},{6,0},{7,1},{8,14},{9,15},{10,... | collective-permute-start | bytes 786440 | tf_op jit(solution)/shard_map/ppermute | solution.py:325
  39.9 33.7 %all-to-all-start = ((bf16[16,64,1024]{2,1,0:T(8,128)(2,1)}), bf16[16,64,1024]{2,1,0:T(8,128)(2,1)}, u32[]{:S(2)}, u32[]{:S(2)}) async-start(bf16[16,64,1024]{2,1,0:T(8,128)(2,1)} %bitcast.19), calls=%async_computation | async-start | bytes 4194304 | tf_op jit(solution)/shard_map/all_to_all | solution.py:416
  45.4 3.8 %collective-permute-start.6 = (bf16[4,256,512]{2,1,0:T(8,128)(2,1)}, bf16[4,256,512]{2,1,0:T(8,128)(2,1)}, u32[]{:S(2)}, u32[]{:S(2)}) collective-permute-start(bf16[4,256,512]{2,1,0:T(8,128)(2,1)} %pad_maximum_fusion), channel_id=1, source_target_pairs={{0,1},{1,0},{2,3},{3,2},{4,5},{5,4},{6,7},{7,6},{8,9},{9,8},{10,11... | collective-permute-start | bytes 3145736 | tf_op jit(solution)/shard_map/ppermute | solution.py:329
  45.8 3.5 %copy-start.4 = (f32[8]{0:T(128)S(1)}, f32[8]{0:T(128)}, u32[]{:S(2)}) copy-start(f32[8]{0:T(128)} %scale_ref.1) | copy-start | bytes 100
  73.6 31.1 %all-to-all-start.2 = ((bf16[32,16,1024]{2,1,0:T(8,128)(2,1)}), bf16[32,16,1024]{2,1,0:T(8,128)(2,1)S(1)}, u32[]{:S(2)}, u32[]{:S(2)}) async-start(bf16[32,16,1024]{2,1,0:T(8,128)(2,1)} %bitcast.30), calls=%async_computation.2 | async-start | bytes 2097152 | tf_op jit(solution)/shard_map/all_to_all | solution.py:375
  81.9 2.2 copy-start.10
  104.8 29.9 %all-to-all-start.1 = ((bf16[32,16,1024]{2,1,0:T(8,128)(2,1)}), bf16[32,16,1024]{2,1,0:T(8,128)(2,1)S(1)}, u32[]{:S(2)}, u32[]{:S(2)}) async-start(bf16[32,16,1024]{2,1,0:T(8,128)(2,1)} %bitcast.27), calls=%async_computation.1 | async-start | bytes 2097152 | tf_op jit(solution)/shard_map/all_to_all | solution.py:375
  108.4 5.2 %copy-start.3 = (f32[2048]{0:T(1024)S(1)}, f32[2048]{0:T(1024)}, u32[]{:S(2)}) copy-start(f32[2048]{0:T(1024)} %param.20) | copy-start | bytes 24580
  134.6 53.8 %all-to-all-start.3 = ((bf16[32,16,2048]{2,1,0:T(8,128)(2,1)}), bf16[32,16,2048]{2,1,0:T(8,128)(2,1)}, u32[]{:S(2)}, u32[]{:S(2)}) async-start(bf16[32,16,2048]{2,1,0:T(8,128)(2,1)} %bitcast.32), calls=%async_computation.3 | async-start | bytes 4194304 | tf_op jit(solution)/shard_map/all_to_all | solution.py:375
  143.6 0.7 copy-start.6
  188.4 4.1 %copy-start.8 = (s32[256,2]{0,1:T(2,128)S(1)}, s32[256,2]{0,1:T(2,128)}, u32[]{:S(2)}) copy-start(s32[256,2]{0,1:T(2,128)} %param.25) | copy-start | bytes 6148
  188.4 52.9 %all-to-all-start.4 = ((bf16[32,16,2048]{2,1,0:T(8,128)(2,1)}), bf16[32,16,2048]{2,1,0:T(8,128)(2,1)}, u32[]{:S(2)}, u32[]{:S(2)}) async-start(bf16[32,16,2048]{2,1,0:T(8,128)(2,1)} %bitcast.34), calls=%async_computation.4 | async-start | bytes 4194304 | tf_op jit(solution)/shard_map/all_to_all | solution.py:375

commit v6 on v5

--- a/solution.py
+++ b/solution.py
@@ -63,7 +63,7 @@
 def run_expert(mid, gain, expert_in, expert_out, local, local_count):
     row_total, feat_dim = mid.shape
     units = expert_out.shape[0] // local_count
-    width = 352
+    width = 704
     steps = units // width
     first = local * steps
     tile = math.gcd(row_total, 512)
@@ -83,7 +83,7 @@
             pltpu.VMEM((tile, feat_dim), jnp.bfloat16),
             pltpu.VMEM((tile, feat_dim), jnp.float32),
         ],
-        compiler_params=pltpu.CompilerParams(vmem_limit_bytes=40 << 20),
+        compiler_params=pltpu.CompilerParams(vmem_limit_bytes=48 << 20),
         cost_estimate=pl.CostEstimate(
             flops=flops,
             bytes_accessed=6 * units * feat_dim + 4 * row_total * feat_dim,
@@ -180,7 +180,7 @@
 def combine(base, weight, key, row_key, rows, kind):
     row_count, feat_dim = base.shape
     slots = rows.shape[0]
-    width = math.gcd(feat_dim, 512)
+    width = math.gcd(feat_dim, 1024)
     return pl.pallas_call(
         combine_body,
         grid=(feat_dim // width,),

time: 247 us -> 245 us (level)
  Pallas kernels: 68 us -> 60.1 us
  waiting for transfers between devices: 91.5 us -> 98.5 us
    all_to_all x4, waiting for transfers between devices: 77.7 us -> 84.8 us  [exchange(): return lax.all_to_all(rows, 'tm', split_axis=0, concat_axis=0, tiled=True)]
    pallas_call x2, Pallas kernels: 39.7 us -> 33.5 us  [run_expert(): pl.pallas_call(functools.partial(expert_body, steps), grid=(row_total //...]
  transfers between devices with their start and end apart: 13 -> 13, of which waited for: 7 -> 7; matrix products, arithmetic and copies ran while one was open for 17% -> 17% of each run, Pallas kernels for 26% -> 23%
where the time goes in v6:
time: 245 us; the launch traced here: 244 us
  waiting for transfers between devices  98.5 us (40%)
  Pallas kernels  60.1 us (25%)
  starting transfers between devices  40.2 us (16%)
  matrix products  33.8 us (14%)
  local copies, waits for them, and re-layouts  6.21 us (3%)
  other arithmetic  4.71 us (2%)
    all_to_all x4, waiting for transfers between devices, exchange(): return lax.all_to_all(rows, 'tm', split_axis=0, concat_axis=0, tiled=True)  84.8 us
    pallas_call x2, Pallas kernels, run_expert(): pl.pallas_call(functools.partial(expert_body, steps), grid=(row_total //...  33.5 us
    all_to_all x4, starting transfers between devices, exchange(): return lax.all_to_all(rows, 'tm', split_axis=0, concat_axis=0, tiled=True)  16.7 us
    pallas_call x1, Pallas kernels, attend(): pl.pallas_call(functools.partial(attend_body, kv_heads), out_shape=jax.Sh...  14.4 us
    dot_general x4, matrix products, embed(): rows = jnp.dot(pairs, conv_weight, preferred_element_type=jnp.float32)  12.6 us
    ppermute x3, starting transfers between devices, from_behind(): return lax.ppermute(block, axis, route)  11.4 us
    dot_general x2, matrix products, shards(): jnp.dot(context_in[local], w_out, preferred_element_type=jnp.float32)  10.4 us
    all_to_all x1, waiting for transfers between devices, shards(): lax.all_to_all(pairs_out.reshape(half, 2 * local_count * CAP, -1), 'tm',...  8.5 us
  transfers between devices with their start and end apart: 13, of which 7 were waited for; matrix products, arithmetic and copies ran while one was open for 17% of the time, Pallas kernels for 23%

profile of v6, /device:TPU:0, one launch (start us, length us, event | category | flops | bytes accessed | tf_op | source)
XLA Modules:
  0.0 244.0 jit_solution(17678517388753281749)
XLA Ops:
  0.0 5.1 %collective-permute-start.2 = (bf16[256,512]{1,0:T(8,128)(2,1)}, bf16[256,512]{1,0:T(8,128)(2,1)S(1)}, u32[]{:S(2)}, u32[]{:S(2)}) collective-permute-start(bf16[256,512]{1,0:T(8,128)(2,1)} %signal_ref.1), channel_id=1, source_target_pairs={{0,8},{1,9},{2,10},{3,11},{4,12},{5,13},{6,14},{7,15},{8,16},{9,17... | collective-permute-start | bytes 786440 | tf_op jit(solution)/shard_map/ppermute | solution.py:22
  5.8 2.6 %collective-permute-start.1 = (bf16[1,512]{1,0:T(2,128)(2,1)S(1)}, bf16[1,512]{1,0:T(2,128)(2,1)S(1)}, u32[]{:S(2)}, u32[]{:S(2)}) collective-permute-start(bf16[1,512]{1,0:T(2,128)(2,1)S(1)} %slice.26), channel_id=1, source_target_pairs={{0,9},{1,10},{2,11},{3,12},{4,13},{5,14},{6,15},{7,16},{8,17},{9,1... | collective-permute-start | bytes 3080 | tf_op jit(solution)/shard_map/ppermute | solution.py:22
  8.4 3.8 %collective-permute-start = (bf16[1,512]{1,0:T(2,128)(2,1)S(1)}, bf16[1,512]{1,0:T(2,128)(2,1)S(1)}, u32[]{:S(2)}, u32[]{:S(2)}) collective-permute-start(bf16[1,512]{1,0:T(2,128)(2,1)S(1)} %slice.26), channel_id=1, source_target_pairs={{0,1},{1,2},{2,3},{3,4},{4,5},{5,6},{6,7},{7,8},{8,9},{9,10},{10,1... | collective-permute-start | bytes 3080 | tf_op jit(solution)/shard_map/ppermute | solution.py:22
  13.1 3.8 %fusion.7 = (f32[256]{0:T(256)S(1)}, bf16[256,2048]{1,0:T(8,128)(2,1)S(1)}) fusion(bf16[1024,2048]{1,0:T(8,128)(2,1)} %param.14, bf16[256,512]{1,0:T(8,128)(2,1)} %signal_ref.1, bf16[255,512]{1,0:T(8,128)(2,1)} %bitcast.70, bf16[1,512]{1,0:T(2,128)(2,1)S(1)} %collective-permute-done.before_ref), kind=kOutput, calls=%fused_computation.20 | convolution fusion | flops 1077411584 | bytes 5768192 | tf_op jit(solution)/shard_map/dot_general | solution.py:394
  17.7 3.9 %collective-permute-start.7 = (bf16[272,512]{1,0:T(8,128)(2,1)}, bf16[272,512]{1,0:T(8,128)(2,1)S(1)}, u32[]{:S(2)}, u32[]{:S(2)}) collective-permute-start(bf16[272,512]{1,0:T(8,128)(2,1)} %fusion.38), channel_id=1, source_target_pairs={{0,16},{1,17},{2,18},{3,19},{4,20},{5,21},{6,22},{7,23},{8,24},{9,... | collective-permute-start | bytes 835592 | tf_op jit(solution)/shard_map/ppermute | solution.py:388
  28.5 2.3 collective-permute-start.5
  30.8 2.8 %collective-permute-done.7.far_ref = bf16[272,512]{1,0:T(8,128)(2,1)S(1)} collective-permute-done((bf16[272,512]{1,0:T(8,128)(2,1)}, bf16[272,512]{1,0:T(8,128)(2,1)S(1)}, u32[]{:S(2)}, u32[]{:S(2)}) %collective-permute-start.7) | collective-permute-done | bytes 278560 | tf_op jit(solution)/shard_map/ppermute | solution.py:388
  33.7 3.8 %shard_map.130 = bf16[1024,1024]{1,0:T(8,128)(2,1)} custom-call(s32[2]{0:T(128)S(1)} %pad_add_fusion.info_ref, bf16[256,512]{1,0:T(8,128)(2,1)S(1)} %copy-done.2, bf16[1,512]{1,0:T(2,128)(2,1)S(1)} %collective-permute-done.before_ref, s32[2,256]{1,0:T(2,128)S(1)} %bitcast.79, bf16[272,512]{1,0:T(8,128)(2,1)S(1)} %collective-permute-done.7.far_ref), custom_call_target="tpu_custom_call" | custom-call | flops 1073741824 | bytes 2621440 | tf_op jit(solution)/shard_map/pallas_call | solution.py:144
  37.5 2.4 collective-permute-done.4
  39.9 4.4 %all-to-all-start = ((bf16[16,64,1024]{2,1,0:T(8,128)(2,1)}), bf16[16,64,1024]{2,1,0:T(8,128)(2,1)}, u32[]{:S(2)}, u32[]{:S(2)}) async-start(bf16[16,64,1024]{2,1,0:T(8,128)(2,1)} %bitcast.19), calls=%async_computation | async-start | bytes 4194304 | tf_op jit(solution)/shard_map/all_to_all | solution.py:416
  45.8 3.5 %fusion.61.query_ref = f32[256,1024]{1,0:T(8,128)S(1)} fusion(bf16[256,2048]{1,0:T(8,128)(2,1)S(1)} %get-tuple-element.34.rows_ref, bf16[2048,1024]{1,0:T(8,128)(2,1)} %param.16), kind=kOutput, calls=%fused_computation.107 | convolution fusion | flops 1073741824 | bytes 6291456 | tf_op jit(solution)/shard_map/dot_general | solution.py:408
  49.3 14.4 %shard_map.129 = bf16[256,1024]{1,0:T(8,128)(2,1)S(1)} custom-call(s32[9]{0:T(128)S(1)} %convert_element_type.68.flag_ref, f32[8]{0:T(128)S(1)} %copy-done.4, f32[256,1024]{1,0:T(8,128)S(1)} %fusion.61.query_ref, bf16[1,256,512]{2,1,0:T(8,128)(2,1)S(1)} %bitcast.68, bf16[1,256,512]{2,1,0:T(8,128)(2,1)S(1)} %bitcast.69, bf16[1,256,512]{2,1,0:T(8,128)(2,1)S(1)} %bitcast.72, ...), custom_call_target="tpu_custom_call" | custom-call | flops 3623878656 | bytes 3932160 | tf_op jit(solution)/shard_map/pallas_call | solution.py:295
  65.1 8.5 %all-to-all-done = bf16[16,64,1024]{2,1,0:T(8,128)(2,1)} async-done(((bf16[16,64,1024]{2,1,0:T(8,128)(2,1)}), bf16[16,64,1024]{2,1,0:T(8,128)(2,1)}, u32[]{:S(2)}, u32[]{:S(2)}) %all-to-all-start) | async-done | bytes 2097184 | tf_op jit(solution)/shard_map/all_to_all | solution.py:416
  73.6 5.1 %all-to-all-start.2 = ((bf16[32,16,1024]{2,1,0:T(8,128)(2,1)}), bf16[32,16,1024]{2,1,0:T(8,128)(2,1)S(1)}, u32[]{:S(2)}, u32[]{:S(2)}) async-start(bf16[32,16,1024]{2,1,0:T(8,128)(2,1)} %bitcast.30), calls=%async_computation.2 | async-start | bytes 2097152 | tf_op jit(solution)/shard_map/all_to_all | solution.py:375
  80.2 1.7 slice_bitcast_fusion
  82.1 2.0 copy-done.10
  84.1 3.7 %convolution_convert_fusion.1 = bf16[512,2048]{1,0:T(8,128)(2,1)} fusion(bf16[512,1024]{1,0:T(8,128)(2,1)S(1)} %bitcast.82, bf16[1024,2048]{1,0:T(8,128)(2,1)S(1)} %copy-done.10), kind=kOutput, calls=%fused_computation.6 | convolution fusion | flops 2148532224 | bytes 7340032 | tf_op jit(solution)/shard_map/dot_general | solution.py:394
  87.7 3.7 %convolution_convert_fusion = bf16[512,2048]{1,0:T(8,128)(2,1)} fusion(bf16[512,1024]{1,0:T(8,128)(2,1)S(1)} %bitcast.83, bf16[1024,2048]{1,0:T(8,128)(2,1)S(1)} %copy-done.10), kind=kOutput, calls=%fused_computation.5 | convolution fusion | flops 2148532224 | bytes 7340032 | tf_op jit(solution)/shard_map/dot_general | solution.py:394
  91.4 13.3 %all-to-all-done.2 = bf16[32,16,1024]{2,1,0:T(8,128)(2,1)S(1)} async-done(((bf16[32,16,1024]{2,1,0:T(8,128)(2,1)}), bf16[32,16,1024]{2,1,0:T(8,128)(2,1)S(1)}, u32[]{:S(2)}, u32[]{:S(2)}) %all-to-all-start.2) | async-done | bytes 1048608 | tf_op jit(solution)/shard_map/all_to_all | solution.py:375
  104.8 3.6 %all-to-all-start.1 = ((bf16[32,16,1024]{2,1,0:T(8,128)(2,1)}), bf16[32,16,1024]{2,1,0:T(8,128)(2,1)S(1)}, u32[]{:S(2)}, u32[]{:S(2)}) async-start(bf16[32,16,1024]{2,1,0:T(8,128)(2,1)} %bitcast.27), calls=%async_computation.1 | async-start | bytes 2097152 | tf_op jit(solution)/shard_map/all_to_all | solution.py:375
  108.4 5.2 %add_convert_fusion.mid_ref = bf16[512,2048]{1,0:T(8,128)(2,1)S(1)} fusion(bf16[512,2048]{1,0:T(8,128)(2,1)} %convolution_convert_fusion.1, bf16[512,1024]{1,0:T(8,128)(2,1)S(1)} %bitcast.81, bf16[1024,2048]{1,0:T(8,128)(2,1)} %param.18), kind=kOutput, calls=%fused_computation | convolution fusion | flops 2150629376 | bytes 9437184 | tf_op jit(solution)/shard_map/dot_general | solution.py:452
  113.6 16.8 %shard_map.132 = bf16[512,2048]{1,0:T(8,128)(2,1)} custom-call(bf16[512,2048]{1,0:T(8,128)(2,1)S(1)} %add_convert_fusion.mid_ref, f32[1,2048]{1,0:T(1,128)S(1)} %bitcast.77, bf16[2,2816,2048]{2,1,0:T(8,128)(2,1)} %w_in_ref.3, bf16[2816,2048]{1,0:T(8,128)(2,1)} %w_out_ref.3), custom_call_target="tpu_custom_call" | custom-call | flops 8858370048 | bytes 21495808 | tf_op jit(solution)/shard_map/pallas_call | solution.py:71
  130.4 4.2 %all-to-all-done.1 = bf16[32,16,1024]{2,1,0:T(8,128)(2,1)S(1)} async-done(((bf16[32,16,1024]{2,1,0:T(8,128)(2,1)}), bf16[32,16,1024]{2,1,0:T(8,128)(2,1)S(1)}, u32[]{:S(2)}, u32[]{:S(2)}) %all-to-all-start.1) | async-done | bytes 1048608 | tf_op jit(solution)/shard_map/all_to_all | solution.py:375
  134.6 4.0 %all-to-all-start.3 = ((bf16[32,16,2048]{2,1,0:T(8,128)(2,1)}), bf16[32,16,2048]{2,1,0:T(8,128)(2,1)}, u32[]{:S(2)}, u32[]{:S(2)}) async-start(bf16[32,16,2048]{2,1,0:T(8,128)(2,1)} %bitcast.32), calls=%async_computation.3 | async-start | bytes 4194304 | tf_op jit(solution)/shard_map/all_to_all | solution.py:375
  138.6 3.9 %fusion.4 = (f32[256]{0:T(256)S(1)}, bf16[256,2048]{1,0:T(8,128)(2,1)S(1)}) fusion(bf16[256,1024]{1,0:T(8,128)(2,1)S(1)} %shard_map.129, bf16[1024,2048]{1,0:T(8,128)(2,1)} %param.18, bf16[256,2048]{1,0:T(8,128)(2,1)} %copy-done.5), kind=kOutput, calls=%fused_computation.17 | convolution fusion | flops 1076887296 | bytes 6816768 | tf_op jit(solution)/shard_map/dot_general | solution.py:440
  143.5 5.2 %add_convert_fusion.1.mid_ref = bf16[512,2048]{1,0:T(8,128)(2,1)S(1)} fusion(bf16[512,2048]{1,0:T(8,128)(2,1)} %convolution_convert_fusion, bf16[512,1024]{1,0:T(8,128)(2,1)S(1)} %bitcast.80, bf16[1024,2048]{1,0:T(8,128)(2,1)} %param.18), kind=kOutput, calls=%fused_computation.1 | convolution fusion | flops 2150629376 | bytes 9437184 | tf_op jit(solution)/shard_map/dot_general | solution.py:452
  148.7 16.7 %shard_map.131 = bf16[512,2048]{1,0:T(8,128)(2,1)} custom-call(bf16[512,2048]{1,0:T(8,128)(2,1)S(1)} %add_convert_fusion.1.mid_ref, f32[1,2048]{1,0:T(1,128)S(1)} %bitcast.78, bf16[2,2816,2048]{2,1,0:T(8,128)(2,1)} %w_in_ref.3, bf16[2816,2048]{1,0:T(8,128)(2,1)} %w_out_ref.3), custom_call_target="tpu_custom_call" | custom-call | flops 8858370048 | bytes 21495808 | tf_op jit(solution)/shard_map/pallas_call | solution.py:71
  165.5 21.9 %all-to-all-done.3 = bf16[32,16,2048]{2,1,0:T(8,128)(2,1)} async-done(((bf16[32,16,2048]{2,1,0:T(8,128)(2,1)}), bf16[32,16,2048]{2,1,0:T(8,128)(2,1)}, u32[]{:S(2)}, u32[]{:S(2)}) %all-to-all-start.3) | async-done | bytes 2097184 | tf_op jit(solution)/shard_map/all_to_all | solution.py:375
  187.3 4.1 %all-to-all-start.4 = ((bf16[32,16,2048]{2,1,0:T(8,128)(2,1)}), bf16[32,16,2048]{2,1,0:T(8,128)(2,1)}, u32[]{:S(2)}, u32[]{:S(2)}) async-start(bf16[32,16,2048]{2,1,0:T(8,128)(2,1)} %bitcast.34), calls=%async_computation.4 | async-start | bytes 4194304 | tf_op jit(solution)/shard_map/all_to_all | solution.py:375
  191.8 3.1 %shard_map.133.base_ref = f32[256,2048]{1,0:T(8,128)S(1)} custom-call(f32[256,2048]{1,0:T(8,128)S(1)} %convert_element_type.85.base_ref, f32[256,2]{1,0:T(8,128)S(1)} %broadcast_divide_fusion.weight_ref, s32[256,2]{1,0:T(8,128)S(1)} %copy.56.key_ref, s32[1,512]{1,0:T(1,128)S(1)} %multiply_add_fusion.1.row_ref, bf16[512,2048]{1,0:T(8,128)(2,1)} %bitcast.33.rows_ref), custom_call_target="tpu_custom_call" | custom-call | flops 1073741824 | bytes 6291456 | tf_op jit(solution)/shard_map/pallas_call | solution.py:184
  194.9 45.3 %all-to-all-done.4 = bf16[32,16,2048]{2,1,0:T(8,128)(2,1)} async-done(((bf16[32,16,2048]{2,1,0:T(8,128)(2,1)}), bf16[32,16,2048]{2,1,0:T(8,128)(2,1)}, u32[]{:S(2)}, u32[]{:S(2)}) %all-to-all-start.4) | async-done | bytes 2097184 | tf_op jit(solution)/shard_map/all_to_all | solution.py:375
  240.3 3.7 %shard_map.134 = bf16[256,2048]{1,0:T(8,128)(2,1)} custom-call(f32[256,2048]{1,0:T(8,128)S(1)} %shard_map.133.base_ref, f32[256,2]{1,0:T(8,128)S(1)} %broadcast_divide_fusion.weight_ref, s32[256,2]{1,0:T(8,128)S(1)} %copy.56.key_ref, s32[1,512]{1,0:T(1,128)S(1)} %multiply_add_fusion.row_ref, bf16[512,2048]{1,0:T(8,128)(2,1)} %bitcast.35.rows_ref), custom_call_target="tpu_custom_call" | custom-call | flops 1073741824 | bytes 6291456 | tf_op jit(solution)/shard_map/pallas_call | solution.py:184
  (63 shorter events, 15.1 us)
Async XLA Ops:
  0.0 142.5 %copy-start = (bf16[2048,64]{0,1:T(8,128)(2,1)S(1)}, bf16[2048,64]{0,1:T(8,128)(2,1)}, u32[]{:S(2)}) copy-start(bf16[2048,64]{0,1:T(8,128)(2,1)} %param.21) | copy-start | bytes 786436
  0.0 21.7 %collective-permute-start.2 = (bf16[256,512]{1,0:T(8,128)(2,1)}, bf16[256,512]{1,0:T(8,128)(2,1)S(1)}, u32[]{:S(2)}, u32[]{:S(2)}) collective-permute-start(bf16[256,512]{1,0:T(8,128)(2,1)} %signal_ref.1), channel_id=1, source_target_pairs={{0,8},{1,9},{2,10},{3,11},{4,12},{5,13},{6,14},{7,15},{8,16},{9,17... | collective-permute-start | bytes 786440 | tf_op jit(solution)/shard_map/ppermute | solution.py:22
  5.8 15.8 %collective-permute-start.1 = (bf16[1,512]{1,0:T(2,128)(2,1)S(1)}, bf16[1,512]{1,0:T(2,128)(2,1)S(1)}, u32[]{:S(2)}, u32[]{:S(2)}) collective-permute-start(bf16[1,512]{1,0:T(2,128)(2,1)S(1)} %slice.26), channel_id=1, source_target_pairs={{0,9},{1,10},{2,11},{3,12},{4,13},{5,14},{6,15},{7,16},{8,17},{9,1... | collective-permute-start | bytes 3080 | tf_op jit(solution)/shard_map/ppermute | solution.py:22
  8.4 4.6 %collective-permute-start = (bf16[1,512]{1,0:T(2,128)(2,1)S(1)}, bf16[1,512]{1,0:T(2,128)(2,1)S(1)}, u32[]{:S(2)}, u32[]{:S(2)}) collective-permute-start(bf16[1,512]{1,0:T(2,128)(2,1)S(1)} %slice.26), channel_id=1, source_target_pairs={{0,1},{1,2},{2,3},{3,4},{4,5},{5,6},{6,7},{7,8},{8,9},{9,10},{10,1... | collective-permute-start | bytes 3080 | tf_op jit(solution)/shard_map/ppermute | solution.py:22
  13.0 3.9 %copy-start.2 = (bf16[256,512]{1,0:T(8,128)(2,1)S(1)}, bf16[256,512]{1,0:T(8,128)(2,1)}, u32[]{:S(2)}) copy-start(bf16[256,512]{1,0:T(8,128)(2,1)} %signal_ref.1) | copy-start | bytes 786436
  13.1 8.6 %copy-start.9 = (bf16[1024,2048]{1,0:T(8,128)(2,1)S(1)}, bf16[1024,2048]{1,0:T(8,128)(2,1)}, u32[]{:S(2)}) copy-start(bf16[1024,2048]{1,0:T(8,128)(2,1)} %param.14) | copy-start | bytes 12582916
  16.9 6.2 %copy-start.5 = (bf16[256,2048]{1,0:T(8,128)(2,1)}, bf16[256,2048]{1,0:T(8,128)(2,1)S(1)}, u32[]{:S(2)}) copy-start(bf16[256,2048]{1,0:T(8,128)(2,1)S(1)} %get-tuple-element.43) | copy-start | bytes 3145732
  17.7 15.9 %collective-permute-start.7 = (bf16[272,512]{1,0:T(8,128)(2,1)}, bf16[272,512]{1,0:T(8,128)(2,1)S(1)}, u32[]{:S(2)}, u32[]{:S(2)}) collective-permute-start(bf16[272,512]{1,0:T(8,128)(2,1)} %fusion.38), channel_id=1, source_target_pairs={{0,16},{1,17},{2,18},{3,19},{4,20},{5,21},{6,22},{7,23},{8,24},{9,... | collective-permute-start | bytes 835592 | tf_op jit(solution)/shard_map/ppermute | solution.py:388
  21.7 1.4 copy-start.7
  23.1 1.6 copy-start.1
  27.3 10.3 %collective-permute-start.3 = (bf16[256,512]{1,0:T(8,128)(2,1)}, bf16[256,512]{1,0:T(8,128)(2,1)S(1)}, u32[]{:S(2)}, u32[]{:S(2)}) collective-permute-start(bf16[256,512]{1,0:T(8,128)(2,1)} %get-tuple-element.32), channel_id=1, source_target_pairs={{0,2},{1,3},{2,0},{3,1},{4,6},{5,7},{6,4},{7,5},{8,10},{9,11},{10,... | collective-permute-start | bytes 786440 | tf_op jit(solution)/shard_map/ppermute | solution.py:325
  27.3 12.6 %collective-permute-start.4 = (bf16[256,512]{1,0:T(8,128)(2,1)}, bf16[256,512]{1,0:T(8,128)(2,1)S(1)}, u32[]{:S(2)}, u32[]{:S(2)}) collective-permute-start(bf16[256,512]{1,0:T(8,128)(2,1)} %get-tuple-element.31), channel_id=1, source_target_pairs={{0,4},{1,5},{2,6},{3,7},{4,0},{5,1},{6,2},{7,3},{8,12},{9,13},{10,... | collective-permute-start | bytes 786440 | tf_op jit(solution)/shard_map/ppermute | solution.py:325
  28.5 11.4 %collective-permute-start.5 = (bf16[256,512]{1,0:T(8,128)(2,1)}, bf16[256,512]{1,0:T(8,128)(2,1)S(1)}, u32[]{:S(2)}, u32[]{:S(2)}) collective-permute-start(bf16[256,512]{1,0:T(8,128)(2,1)} %get-tuple-element.30), channel_id=1, source_target_pairs={{0,6},{1,7},{2,4},{3,5},{4,2},{5,3},{6,0},{7,1},{8,14},{9,15},{10,... | collective-permute-start | bytes 786440 | tf_op jit(solution)/shard_map/ppermute | solution.py:325
  39.9 33.7 %all-to-all-start = ((bf16[16,64,1024]{2,1,0:T(8,128)(2,1)}), bf16[16,64,1024]{2,1,0:T(8,128)(2,1)}, u32[]{:S(2)}, u32[]{:S(2)}) async-start(bf16[16,64,1024]{2,1,0:T(8,128)(2,1)} %bitcast.19), calls=%async_computation | async-start | bytes 4194304 | tf_op jit(solution)/shard_map/all_to_all | solution.py:416
  45.4 3.8 %collective-permute-start.6 = (bf16[4,256,512]{2,1,0:T(8,128)(2,1)}, bf16[4,256,512]{2,1,0:T(8,128)(2,1)}, u32[]{:S(2)}, u32[]{:S(2)}) collective-permute-start(bf16[4,256,512]{2,1,0:T(8,128)(2,1)} %pad_maximum_fusion), channel_id=1, source_target_pairs={{0,1},{1,0},{2,3},{3,2},{4,5},{5,4},{6,7},{7,6},{8,9},{9,8},{10,11... | collective-permute-start | bytes 3145736 | tf_op jit(solution)/shard_map/ppermute | solution.py:329
  45.8 3.5 %copy-start.4 = (f32[8]{0:T(128)S(1)}, f32[8]{0:T(128)}, u32[]{:S(2)}) copy-start(f32[8]{0:T(128)} %scale_ref.1) | copy-start | bytes 100
  73.6 31.1 %all-to-all-start.2 = ((bf16[32,16,1024]{2,1,0:T(8,128)(2,1)}), bf16[32,16,1024]{2,1,0:T(8,128)(2,1)S(1)}, u32[]{:S(2)}, u32[]{:S(2)}) async-start(bf16[32,16,1024]{2,1,0:T(8,128)(2,1)} %bitcast.30), calls=%async_computation.2 | async-start | bytes 2097152 | tf_op jit(solution)/shard_map/all_to_all | solution.py:375
  81.9 2.2 copy-start.10
  104.8 29.9 %all-to-all-start.1 = ((bf16[32,16,1024]{2,1,0:T(8,128)(2,1)}), bf16[32,16,1024]{2,1,0:T(8,128)(2,1)S(1)}, u32[]{:S(2)}, u32[]{:S(2)}) async-start(bf16[32,16,1024]{2,1,0:T(8,128)(2,1)} %bitcast.27), calls=%async_computation.1 | async-start | bytes 2097152 | tf_op jit(solution)/shard_map/all_to_all | solution.py:375
  108.4 5.2 %copy-start.3 = (f32[2048]{0:T(1024)S(1)}, f32[2048]{0:T(1024)}, u32[]{:S(2)}) copy-start(f32[2048]{0:T(1024)} %param.20) | copy-start | bytes 24580
  134.6 52.7 %all-to-all-start.3 = ((bf16[32,16,2048]{2,1,0:T(8,128)(2,1)}), bf16[32,16,2048]{2,1,0:T(8,128)(2,1)}, u32[]{:S(2)}, u32[]{:S(2)}) async-start(bf16[32,16,2048]{2,1,0:T(8,128)(2,1)} %bitcast.32), calls=%async_computation.3 | async-start | bytes 4194304 | tf_op jit(solution)/shard_map/all_to_all | solution.py:375
  142.5 0.7 copy-start.6
  187.3 4.1 %copy-start.8 = (s32[256,2]{0,1:T(2,128)S(1)}, s32[256,2]{0,1:T(2,128)}, u32[]{:S(2)}) copy-start(s32[256,2]{0,1:T(2,128)} %param.25) | copy-start | bytes 6148
  187.3 52.9 %all-to-all-start.4 = ((bf16[32,16,2048]{2,1,0:T(8,128)(2,1)}), bf16[32,16,2048]{2,1,0:T(8,128)(2,1)}, u32[]{:S(2)}, u32[]{:S(2)}) async-start(bf16[32,16,2048]{2,1,0:T(8,128)(2,1)} %bitcast.34), calls=%async_computation.4 | async-start | bytes 4194304 | tf_op jit(solution)/shard_map/all_to_all | solution.py:375

commit v7 on v6

--- a/solution.py
+++ b/solution.py
@@ -412,7 +412,7 @@
     in_first = dev_index < half
     info = jnp.stack([jnp.where(in_first, 0, half), jnp.where(in_first, 0, 1)]).astype(jnp.int32)
     pairs_out = spread_pairs(info, signal, before, route_key.T, far, half, copies, local_count)
-    pairs_out, _ = lax.optimization_barrier((pairs_out, kv_parts[2:-1]))
+    pairs_out, _, _ = lax.optimization_barrier((pairs_out, kv_parts[2:-1], queries))
     pairs_in = lax.all_to_all(
         pairs_out.reshape(half, 2 * local_count * CAP, -1),
         "tm",

time: 245 us -> 243 us (level)
    ppermute x1, waiting for transfers between devices: 0.01 us -> 2.52 us  [window_parts(): lax.ppermute(shared, 'tm', [(dev, dev ^ 1) for dev in range(devices)])]
  transfers between devices with their start and end apart: 13 -> 13, of which waited for: 7 -> 8; matrix products, arithmetic and copies ran while one was open for 17% -> 16% of each run, Pallas kernels for 23% -> 23%
where the time goes in v7:
time: 243 us; the launch traced here: 242 us
  waiting for transfers between devices  99.1 us (41%)
  Pallas kernels  59.3 us (24%)
  starting transfers between devices  40.2 us (17%)
  matrix products  32.7 us (13%)
  local copies, waits for them, and re-layouts  7.44 us (3%)
  other arithmetic  3.08 us (1%)
    all_to_all x4, waiting for transfers between devices, exchange(): return lax.all_to_all(rows, 'tm', split_axis=0, concat_axis=0, tiled=True)  84.7 us
    pallas_call x2, Pallas kernels, run_expert(): pl.pallas_call(functools.partial(expert_body, steps), grid=(row_total //...  33.4 us
    all_to_all x4, starting transfers between devices, exchange(): return lax.all_to_all(rows, 'tm', split_axis=0, concat_axis=0, tiled=True)  16.7 us
    pallas_call x1, Pallas kernels, attend(): pl.pallas_call(functools.partial(attend_body, kv_heads), out_shape=jax.Sh...  13.7 us
    dot_general x4, matrix products, embed(): rows = jnp.dot(pairs, conv_weight, preferred_element_type=jnp.float32)  12.6 us
    ppermute x3, starting transfers between devices, from_behind(): return lax.ppermute(block, axis, route)  11.4 us
    dot_general x2, matrix products, shards(): jnp.dot(context_in[local], w_out, preferred_element_type=jnp.float32)  10.4 us
    all_to_all x1, waiting for transfers between devices, shards(): lax.all_to_all(pairs_out.reshape(half, 2 * local_count * CAP, -1), 'tm',...  8.9 us
  transfers between devices with their start and end apart: 13, of which 8 were waited for; matrix products, arithmetic and copies ran while one was open for 16% of the time, Pallas kernels for 23%

profile of v7, /device:TPU:0, one launch (start us, length us, event | category | flops | bytes accessed | tf_op | source)
XLA Modules:
  0.0 242.3 jit_solution(1284787004304274977)
XLA Ops:
  0.0 5.1 %collective-permute-start.2 = (bf16[256,512]{1,0:T(8,128)(2,1)}, bf16[256,512]{1,0:T(8,128)(2,1)S(1)}, u32[]{:S(2)}, u32[]{:S(2)}) collective-permute-start(bf16[256,512]{1,0:T(8,128)(2,1)} %signal_ref.1), channel_id=1, source_target_pairs={{0,8},{1,9},{2,10},{3,11},{4,12},{5,13},{6,14},{7,15},{8,16},{9,17... | collective-permute-start | bytes 786440 | tf_op jit(solution)/shard_map/ppermute | solution.py:22
  5.8 2.6 %collective-permute-start.1 = (bf16[1,512]{1,0:T(2,128)(2,1)S(1)}, bf16[1,512]{1,0:T(2,128)(2,1)S(1)}, u32[]{:S(2)}, u32[]{:S(2)}) collective-permute-start(bf16[1,512]{1,0:T(2,128)(2,1)S(1)} %slice.26), channel_id=1, source_target_pairs={{0,9},{1,10},{2,11},{3,12},{4,13},{5,14},{6,15},{7,16},{8,17},{9,1... | collective-permute-start | bytes 3080 | tf_op jit(solution)/shard_map/ppermute | solution.py:22
  8.4 3.8 %collective-permute-start = (bf16[1,512]{1,0:T(2,128)(2,1)S(1)}, bf16[1,512]{1,0:T(2,128)(2,1)S(1)}, u32[]{:S(2)}, u32[]{:S(2)}) collective-permute-start(bf16[1,512]{1,0:T(2,128)(2,1)S(1)} %slice.26), channel_id=1, source_target_pairs={{0,1},{1,2},{2,3},{3,4},{4,5},{5,6},{6,7},{7,8},{8,9},{9,10},{10,1... | collective-permute-start | bytes 3080 | tf_op jit(solution)/shard_map/ppermute | solution.py:22
  13.1 3.8 %fusion.7 = (f32[256]{0:T(256)S(1)}, bf16[256,2048]{1,0:T(8,128)(2,1)S(1)}) fusion(bf16[1024,2048]{1,0:T(8,128)(2,1)} %param.14, bf16[256,512]{1,0:T(8,128)(2,1)} %signal_ref.1, bf16[255,512]{1,0:T(8,128)(2,1)} %bitcast.70, bf16[1,512]{1,0:T(2,128)(2,1)S(1)} %collective-permute-done.before_ref), kind=kOutput, calls=%fused_computation.20 | convolution fusion | flops 1077411584 | bytes 5768192 | tf_op jit(solution)/shard_map/dot_general | solution.py:394
  17.0 3.9 %collective-permute-start.7 = (bf16[272,512]{1,0:T(8,128)(2,1)S(1)}, bf16[272,512]{1,0:T(8,128)(2,1)S(1)}, u32[]{:S(2)}, u32[]{:S(2)}) collective-permute-start(bf16[272,512]{1,0:T(8,128)(2,1)S(1)} %fusion.38), channel_id=1, source_target_pairs={{0,16},{1,17},{2,18},{3,19},{4,20},{5,21},{6,22},{7,23},{8,24},{9,... | collective-permute-start | bytes 835592 | tf_op jit(solution)/shard_map/ppermute | solution.py:388
  27.0 2.3 collective-permute-start.5
  29.2 2.2 fusion.61.query_ref
  32.7 3.8 %shard_map.130 = bf16[1024,1024]{1,0:T(8,128)(2,1)} custom-call(s32[2]{0:T(128)S(1)} %pad_add_fusion.info_ref, bf16[256,512]{1,0:T(8,128)(2,1)S(1)} %copy-done.2, bf16[1,512]{1,0:T(2,128)(2,1)S(1)} %collective-permute-done.before_ref, s32[2,256]{1,0:T(2,128)S(1)} %bitcast.79, bf16[272,512]{1,0:T(8,128)(2,1)S(1)} %collective-permute-done.7.far_ref), custom_call_target="tpu_custom_call" | custom-call | flops 1073741824 | bytes 2621440 | tf_op jit(solution)/shard_map/pallas_call | solution.py:144
  36.6 1.7 collective-permute-done.4
  38.2 4.4 %all-to-all-start = ((bf16[16,64,1024]{2,1,0:T(8,128)(2,1)}), bf16[16,64,1024]{2,1,0:T(8,128)(2,1)}, u32[]{:S(2)}, u32[]{:S(2)}) async-start(bf16[16,64,1024]{2,1,0:T(8,128)(2,1)} %bitcast.19), calls=%async_computation | async-start | bytes 4194304 | tf_op jit(solution)/shard_map/all_to_all | solution.py:416
  44.2 2.5 %collective-permute-done.6.refs_5_ = bf16[4,256,512]{2,1,0:T(8,128)(2,1)S(1)} collective-permute-done((bf16[4,256,512]{2,1,0:T(8,128)(2,1)}, bf16[4,256,512]{2,1,0:T(8,128)(2,1)S(1)}, u32[]{:S(2)}, u32[]{:S(2)}) %collective-permute-start.6) | collective-permute-done | bytes 1048608 | tf_op jit(solution)/shard_map/ppermute | solution.py:329
  47.9 13.7 %shard_map.129 = bf16[256,1024]{1,0:T(8,128)(2,1)S(1)} custom-call(s32[9]{0:T(128)S(1)} %convert_element_type.68.flag_ref, f32[8]{0:T(128)S(1)} %copy-done.4, f32[256,1024]{1,0:T(8,128)S(1)} %copy-done.5, bf16[1,256,512]{2,1,0:T(8,128)(2,1)S(1)} %bitcast.68, bf16[1,256,512]{2,1,0:T(8,128)(2,1)S(1)} %bitcast.69, bf16[1,256,512]{2,1,0:T(8,128)(2,1)S(1)} %bitcast.72, ...), custom_call_target="tpu_custom_call" | custom-call | flops 3623878656 | bytes 3932160 | tf_op jit(solution)/shard_map/pallas_call | solution.py:295
  63.1 8.9 %all-to-all-done = bf16[16,64,1024]{2,1,0:T(8,128)(2,1)} async-done(((bf16[16,64,1024]{2,1,0:T(8,128)(2,1)}), bf16[16,64,1024]{2,1,0:T(8,128)(2,1)}, u32[]{:S(2)}, u32[]{:S(2)}) %all-to-all-start) | async-done | bytes 2097184 | tf_op jit(solution)/shard_map/all_to_all | solution.py:416
  71.9 5.0 %all-to-all-start.2 = ((bf16[32,16,1024]{2,1,0:T(8,128)(2,1)}), bf16[32,16,1024]{2,1,0:T(8,128)(2,1)S(1)}, u32[]{:S(2)}, u32[]{:S(2)}) async-start(bf16[32,16,1024]{2,1,0:T(8,128)(2,1)} %bitcast.30), calls=%async_computation.2 | async-start | bytes 2097152 | tf_op jit(solution)/shard_map/all_to_all | solution.py:375
  78.5 1.7 slice_bitcast_fusion
  80.5 2.0 copy-done.12
  82.4 3.7 %convolution_convert_fusion.1 = bf16[512,2048]{1,0:T(8,128)(2,1)} fusion(bf16[512,1024]{1,0:T(8,128)(2,1)S(1)} %bitcast.82, bf16[1024,2048]{1,0:T(8,128)(2,1)S(1)} %copy-done.12), kind=kOutput, calls=%fused_computation.6 | convolution fusion | flops 2148532224 | bytes 7340032 | tf_op jit(solution)/shard_map/dot_general | solution.py:394
  86.1 3.7 %convolution_convert_fusion = bf16[512,2048]{1,0:T(8,128)(2,1)} fusion(bf16[512,1024]{1,0:T(8,128)(2,1)S(1)} %bitcast.83, bf16[1024,2048]{1,0:T(8,128)(2,1)S(1)} %copy-done.12), kind=kOutput, calls=%fused_computation.5 | convolution fusion | flops 2148532224 | bytes 7340032 | tf_op jit(solution)/shard_map/dot_general | solution.py:394
  89.8 13.2 %all-to-all-done.2 = bf16[32,16,1024]{2,1,0:T(8,128)(2,1)S(1)} async-done(((bf16[32,16,1024]{2,1,0:T(8,128)(2,1)}), bf16[32,16,1024]{2,1,0:T(8,128)(2,1)S(1)}, u32[]{:S(2)}, u32[]{:S(2)}) %all-to-all-start.2) | async-done | bytes 1048608 | tf_op jit(solution)/shard_map/all_to_all | solution.py:375
  103.0 3.6 %all-to-all-start.1 = ((bf16[32,16,1024]{2,1,0:T(8,128)(2,1)}), bf16[32,16,1024]{2,1,0:T(8,128)(2,1)S(1)}, u32[]{:S(2)}, u32[]{:S(2)}) async-start(bf16[32,16,1024]{2,1,0:T(8,128)(2,1)} %bitcast.27), calls=%async_computation.1 | async-start | bytes 2097152 | tf_op jit(solution)/shard_map/all_to_all | solution.py:375
  106.7 5.2 %add_convert_fusion.mid_ref = bf16[512,2048]{1,0:T(8,128)(2,1)S(1)} fusion(bf16[512,2048]{1,0:T(8,128)(2,1)} %convolution_convert_fusion.1, bf16[512,1024]{1,0:T(8,128)(2,1)S(1)} %bitcast.81, bf16[1024,2048]{1,0:T(8,128)(2,1)} %param.18), kind=kOutput, calls=%fused_computation | convolution fusion | flops 2150629376 | bytes 9437184 | tf_op jit(solution)/shard_map/dot_general | solution.py:452
  111.9 16.7 %shard_map.132 = bf16[512,2048]{1,0:T(8,128)(2,1)} custom-call(bf16[512,2048]{1,0:T(8,128)(2,1)S(1)} %add_convert_fusion.mid_ref, f32[1,2048]{1,0:T(1,128)S(1)} %bitcast.77, bf16[2,2816,2048]{2,1,0:T(8,128)(2,1)} %w_in_ref.3, bf16[2816,2048]{1,0:T(8,128)(2,1)} %w_out_ref.3), custom_call_target="tpu_custom_call" | custom-call | flops 8858370048 | bytes 21495808 | tf_op jit(solution)/shard_map/pallas_call | solution.py:71
  128.6 4.3 %all-to-all-done.1 = bf16[32,16,1024]{2,1,0:T(8,128)(2,1)S(1)} async-done(((bf16[32,16,1024]{2,1,0:T(8,128)(2,1)}), bf16[32,16,1024]{2,1,0:T(8,128)(2,1)S(1)}, u32[]{:S(2)}, u32[]{:S(2)}) %all-to-all-start.1) | async-done | bytes 1048608 | tf_op jit(solution)/shard_map/all_to_all | solution.py:375
  132.9 4.0 %all-to-all-start.3 = ((bf16[32,16,2048]{2,1,0:T(8,128)(2,1)}), bf16[32,16,2048]{2,1,0:T(8,128)(2,1)}, u32[]{:S(2)}, u32[]{:S(2)}) async-start(bf16[32,16,2048]{2,1,0:T(8,128)(2,1)} %bitcast.32), calls=%async_computation.3 | async-start | bytes 4194304 | tf_op jit(solution)/shard_map/all_to_all | solution.py:375
  136.9 3.9 %fusion.4 = (f32[256]{0:T(256)S(1)}, bf16[256,2048]{1,0:T(8,128)(2,1)S(1)}) fusion(bf16[256,1024]{1,0:T(8,128)(2,1)S(1)} %shard_map.129, bf16[1024,2048]{1,0:T(8,128)(2,1)} %param.18, bf16[256,2048]{1,0:T(8,128)(2,1)} %copy-done.6), kind=kOutput, calls=%fused_computation.17 | convolution fusion | flops 1076887296 | bytes 6816768 | tf_op jit(solution)/shard_map/dot_general | solution.py:440
  141.7 5.2 %add_convert_fusion.1.mid_ref = bf16[512,2048]{1,0:T(8,128)(2,1)S(1)} fusion(bf16[512,2048]{1,0:T(8,128)(2,1)} %convolution_convert_fusion, bf16[512,1024]{1,0:T(8,128)(2,1)S(1)} %bitcast.80, bf16[1024,2048]{1,0:T(8,128)(2,1)} %param.18), kind=kOutput, calls=%fused_computation.1 | convolution fusion | flops 2150629376 | bytes 9437184 | tf_op jit(solution)/shard_map/dot_general | solution.py:452
  147.0 16.7 %shard_map.131 = bf16[512,2048]{1,0:T(8,128)(2,1)} custom-call(bf16[512,2048]{1,0:T(8,128)(2,1)S(1)} %add_convert_fusion.1.mid_ref, f32[1,2048]{1,0:T(1,128)S(1)} %bitcast.78, bf16[2,2816,2048]{2,1,0:T(8,128)(2,1)} %w_in_ref.3, bf16[2816,2048]{1,0:T(8,128)(2,1)} %w_out_ref.3), custom_call_target="tpu_custom_call" | custom-call | flops 8858370048 | bytes 21495808 | tf_op jit(solution)/shard_map/pallas_call | solution.py:71
  163.7 21.9 %all-to-all-done.3 = bf16[32,16,2048]{2,1,0:T(8,128)(2,1)} async-done(((bf16[32,16,2048]{2,1,0:T(8,128)(2,1)}), bf16[32,16,2048]{2,1,0:T(8,128)(2,1)}, u32[]{:S(2)}, u32[]{:S(2)}) %all-to-all-start.3) | async-done | bytes 2097184 | tf_op jit(solution)/shard_map/all_to_all | solution.py:375
  185.6 4.1 %all-to-all-start.4 = ((bf16[32,16,2048]{2,1,0:T(8,128)(2,1)}), bf16[32,16,2048]{2,1,0:T(8,128)(2,1)}, u32[]{:S(2)}, u32[]{:S(2)}) async-start(bf16[32,16,2048]{2,1,0:T(8,128)(2,1)} %bitcast.34), calls=%async_computation.4 | async-start | bytes 4194304 | tf_op jit(solution)/shard_map/all_to_all | solution.py:375
  190.1 3.1 %shard_map.133.base_ref = f32[256,2048]{1,0:T(8,128)S(1)} custom-call(f32[256,2048]{1,0:T(8,128)S(1)} %convert_element_type.85.base_ref, f32[256,2]{1,0:T(8,128)S(1)} %broadcast_divide_fusion.weight_ref, s32[256,2]{1,0:T(8,128)S(1)} %copy.56.key_ref, s32[1,512]{1,0:T(1,128)S(1)} %multiply_add_fusion.1.row_ref, bf16[512,2048]{1,0:T(8,128)(2,1)} %bitcast.33.rows_ref), custom_call_target="tpu_custom_call" | custom-call | flops 1073741824 | bytes 6291456 | tf_op jit(solution)/shard_map/pallas_call | solution.py:184
  193.2 45.4 %all-to-all-done.4 = bf16[32,16,2048]{2,1,0:T(8,128)(2,1)} async-done(((bf16[32,16,2048]{2,1,0:T(8,128)(2,1)}), bf16[32,16,2048]{2,1,0:T(8,128)(2,1)}, u32[]{:S(2)}, u32[]{:S(2)}) %all-to-all-start.4) | async-done | bytes 2097184 | tf_op jit(solution)/shard_map/all_to_all | solution.py:375
  238.5 3.7 %shard_map.134 = bf16[256,2048]{1,0:T(8,128)(2,1)} custom-call(f32[256,2048]{1,0:T(8,128)S(1)} %shard_map.133.base_ref, f32[256,2]{1,0:T(8,128)S(1)} %broadcast_divide_fusion.weight_ref, s32[256,2]{1,0:T(8,128)S(1)} %copy.56.key_ref, s32[1,512]{1,0:T(1,128)S(1)} %multiply_add_fusion.row_ref, bf16[512,2048]{1,0:T(8,128)(2,1)} %bitcast.35.rows_ref), custom_call_target="tpu_custom_call" | custom-call | flops 1073741824 | bytes 6291456 | tf_op jit(solution)/shard_map/pallas_call | solution.py:184
  (67 shorter events, 16.1 us)
Async XLA Ops:
  0.0 140.8 %copy-start = (bf16[2048,64]{0,1:T(8,128)(2,1)S(1)}, bf16[2048,64]{0,1:T(8,128)(2,1)}, u32[]{:S(2)}) copy-start(bf16[2048,64]{0,1:T(8,128)(2,1)} %param.21) | copy-start | bytes 786436
  0.0 21.0 %collective-permute-start.2 = (bf16[256,512]{1,0:T(8,128)(2,1)}, bf16[256,512]{1,0:T(8,128)(2,1)S(1)}, u32[]{:S(2)}, u32[]{:S(2)}) collective-permute-start(bf16[256,512]{1,0:T(8,128)(2,1)} %signal_ref.1), channel_id=1, source_target_pairs={{0,8},{1,9},{2,10},{3,11},{4,12},{5,13},{6,14},{7,15},{8,16},{9,17... | collective-permute-start | bytes 786440 | tf_op jit(solution)/shard_map/ppermute | solution.py:22
  5.8 15.1 %collective-permute-start.1 = (bf16[1,512]{1,0:T(2,128)(2,1)S(1)}, bf16[1,512]{1,0:T(2,128)(2,1)S(1)}, u32[]{:S(2)}, u32[]{:S(2)}) collective-permute-start(bf16[1,512]{1,0:T(2,128)(2,1)S(1)} %slice.26), channel_id=1, source_target_pairs={{0,9},{1,10},{2,11},{3,12},{4,13},{5,14},{6,15},{7,16},{8,17},{9,1... | collective-permute-start | bytes 3080 | tf_op jit(solution)/shard_map/ppermute | solution.py:22
  8.4 4.7 %collective-permute-start = (bf16[1,512]{1,0:T(2,128)(2,1)S(1)}, bf16[1,512]{1,0:T(2,128)(2,1)S(1)}, u32[]{:S(2)}, u32[]{:S(2)}) collective-permute-start(bf16[1,512]{1,0:T(2,128)(2,1)S(1)} %slice.26), channel_id=1, source_target_pairs={{0,1},{1,2},{2,3},{3,4},{4,5},{5,6},{6,7},{7,8},{8,9},{9,10},{10,1... | collective-permute-start | bytes 3080 | tf_op jit(solution)/shard_map/ppermute | solution.py:22
  13.1 3.9 %copy-start.2 = (bf16[256,512]{1,0:T(8,128)(2,1)S(1)}, bf16[256,512]{1,0:T(8,128)(2,1)}, u32[]{:S(2)}) copy-start(bf16[256,512]{1,0:T(8,128)(2,1)} %signal_ref.1) | copy-start | bytes 786436
  13.1 7.8 %copy-start.11 = (bf16[1024,2048]{1,0:T(8,128)(2,1)S(1)}, bf16[1024,2048]{1,0:T(8,128)(2,1)}, u32[]{:S(2)}) copy-start(bf16[1024,2048]{1,0:T(8,128)(2,1)} %param.14) | copy-start | bytes 12582916
  17.0 6.0 %copy-start.6 = (bf16[256,2048]{1,0:T(8,128)(2,1)}, bf16[256,2048]{1,0:T(8,128)(2,1)S(1)}, u32[]{:S(2)}) copy-start(bf16[256,2048]{1,0:T(8,128)(2,1)S(1)} %get-tuple-element.43) | copy-start | bytes 3145732
  17.0 15.7 %collective-permute-start.7 = (bf16[272,512]{1,0:T(8,128)(2,1)S(1)}, bf16[272,512]{1,0:T(8,128)(2,1)S(1)}, u32[]{:S(2)}, u32[]{:S(2)}) collective-permute-start(bf16[272,512]{1,0:T(8,128)(2,1)S(1)} %fusion.38), channel_id=1, source_target_pairs={{0,16},{1,17},{2,18},{3,19},{4,20},{5,21},{6,22},{7,23},{8,24},{9,... | collective-permute-start | bytes 835592 | tf_op jit(solution)/shard_map/ppermute | solution.py:388
  21.0 1.4 copy-start.8
  22.4 1.6 copy-start.1
  24.8 4.5 %copy-start.10 = (bf16[2048,1024]{1,0:T(8,128)(2,1)S(1)}, bf16[2048,1024]{1,0:T(8,128)(2,1)}, u32[]{:S(2)}) copy-start(bf16[2048,1024]{1,0:T(8,128)(2,1)} %param.16) | copy-start | bytes 12582916
  25.7 10.9 %collective-permute-start.3 = (bf16[256,512]{1,0:T(8,128)(2,1)S(1)}, bf16[256,512]{1,0:T(8,128)(2,1)S(1)}, u32[]{:S(2)}, u32[]{:S(2)}) collective-permute-start(bf16[256,512]{1,0:T(8,128)(2,1)S(1)} %get-tuple-element.32), channel_id=1, source_target_pairs={{0,2},{1,3},{2,0},{3,1},{4,6},{5,7},{6,4},{7,5},{8,10},{9,11},{10,... | collective-permute-start | bytes 786440 | tf_op jit(solution)/shard_map/ppermute | solution.py:325
  25.7 12.5 %collective-permute-start.4 = (bf16[256,512]{1,0:T(8,128)(2,1)S(1)}, bf16[256,512]{1,0:T(8,128)(2,1)S(1)}, u32[]{:S(2)}, u32[]{:S(2)}) collective-permute-start(bf16[256,512]{1,0:T(8,128)(2,1)S(1)} %get-tuple-element.31), channel_id=1, source_target_pairs={{0,4},{1,5},{2,6},{3,7},{4,0},{5,1},{6,2},{7,3},{8,12},{9,13},{10,... | collective-permute-start | bytes 786440 | tf_op jit(solution)/shard_map/ppermute | solution.py:325
  27.0 11.3 %collective-permute-start.5 = (bf16[256,512]{1,0:T(8,128)(2,1)S(1)}, bf16[256,512]{1,0:T(8,128)(2,1)S(1)}, u32[]{:S(2)}, u32[]{:S(2)}) collective-permute-start(bf16[256,512]{1,0:T(8,128)(2,1)S(1)} %get-tuple-element.30), channel_id=1, source_target_pairs={{0,6},{1,7},{2,4},{3,5},{4,2},{5,3},{6,0},{7,1},{8,14},{9,15},{10,... | collective-permute-start | bytes 786440 | tf_op jit(solution)/shard_map/ppermute | solution.py:325
  38.2 33.7 %all-to-all-start = ((bf16[16,64,1024]{2,1,0:T(8,128)(2,1)}), bf16[16,64,1024]{2,1,0:T(8,128)(2,1)}, u32[]{:S(2)}, u32[]{:S(2)}) async-start(bf16[16,64,1024]{2,1,0:T(8,128)(2,1)} %bitcast.19), calls=%async_computation | async-start | bytes 4194304 | tf_op jit(solution)/shard_map/all_to_all | solution.py:416
  42.7 4.0 %copy-start.4 = (f32[8]{0:T(128)S(1)}, f32[8]{0:T(128)}, u32[]{:S(2)}) copy-start(f32[8]{0:T(128)} %scale_ref.1) | copy-start | bytes 100
  43.8 2.9 %collective-permute-start.6 = (bf16[4,256,512]{2,1,0:T(8,128)(2,1)}, bf16[4,256,512]{2,1,0:T(8,128)(2,1)S(1)}, u32[]{:S(2)}, u32[]{:S(2)}) collective-permute-start(bf16[4,256,512]{2,1,0:T(8,128)(2,1)} %pad_maximum_fusion), channel_id=1, source_target_pairs={{0,1},{1,0},{2,3},{3,2},{4,5},{5,4},{6,7},{7,6},{8,9},{9,8},{10,11... | collective-permute-start | bytes 3145736 | tf_op jit(solution)/shard_map/ppermute | solution.py:329
  46.7 1.2 copy-start.5
  71.9 31.1 %all-to-all-start.2 = ((bf16[32,16,1024]{2,1,0:T(8,128)(2,1)}), bf16[32,16,1024]{2,1,0:T(8,128)(2,1)S(1)}, u32[]{:S(2)}, u32[]{:S(2)}) async-start(bf16[32,16,1024]{2,1,0:T(8,128)(2,1)} %bitcast.30), calls=%async_computation.2 | async-start | bytes 2097152 | tf_op jit(solution)/shard_map/all_to_all | solution.py:375
  80.2 2.2 copy-start.12
  103.0 29.9 %all-to-all-start.1 = ((bf16[32,16,1024]{2,1,0:T(8,128)(2,1)}), bf16[32,16,1024]{2,1,0:T(8,128)(2,1)S(1)}, u32[]{:S(2)}, u32[]{:S(2)}) async-start(bf16[32,16,1024]{2,1,0:T(8,128)(2,1)} %bitcast.27), calls=%async_computation.1 | async-start | bytes 2097152 | tf_op jit(solution)/shard_map/all_to_all | solution.py:375
  106.7 5.2 %copy-start.3 = (f32[2048]{0:T(1024)S(1)}, f32[2048]{0:T(1024)}, u32[]{:S(2)}) copy-start(f32[2048]{0:T(1024)} %param.20) | copy-start | bytes 24580
  132.9 52.7 %all-to-all-start.3 = ((bf16[32,16,2048]{2,1,0:T(8,128)(2,1)}), bf16[32,16,2048]{2,1,0:T(8,128)(2,1)}, u32[]{:S(2)}, u32[]{:S(2)}) async-start(bf16[32,16,2048]{2,1,0:T(8,128)(2,1)} %bitcast.32), calls=%async_computation.3 | async-start | bytes 4194304 | tf_op jit(solution)/shard_map/all_to_all | solution.py:375
  140.8 0.7 copy-start.7
  185.6 4.1 %copy-start.9 = (s32[256,2]{0,1:T(2,128)S(1)}, s32[256,2]{0,1:T(2,128)}, u32[]{:S(2)}) copy-start(s32[256,2]{0,1:T(2,128)} %param.25) | copy-start | bytes 6148
  185.6 52.9 %all-to-all-start.4 = ((bf16[32,16,2048]{2,1,0:T(8,128)(2,1)}), bf16[32,16,2048]{2,1,0:T(8,128)(2,1)}, u32[]{:S(2)}, u32[]{:S(2)}) async-start(bf16[32,16,2048]{2,1,0:T(8,128)(2,1)} %bitcast.34), calls=%async_computation.4 | async-start | bytes 4194304 | tf_op jit(solution)/shard_map/all_to_all | solution.py:375

commit v8 on v7

--- a/solution.py
+++ b/solution.py
@@ -169,11 +169,14 @@
             hot = key_ref[:, route : route + 1] == row_ref[...]
             hot_ref[route] = hot.astype(jnp.bfloat16)
 
+    count, slots = hot_ref.shape[1:]
+    both = jnp.dot(
+        hot_ref[...].reshape(2 * count, slots), rows_ref[...], preferred_element_type=jnp.float32
+    )
     total = base_ref[...]
     for route in range(2):
-        rows = jnp.dot(hot_ref[route], rows_ref[...], preferred_element_type=jnp.float32)
-        rows = rows.astype(jnp.bfloat16).astype(jnp.float32)
-        total = total + weight_ref[:, route : route + 1] * rows
+        rows = both[route * count : (route + 1) * count].astype(jnp.bfloat16)
+        total = total + weight_ref[:, route : route + 1] * rows.astype(jnp.float32)
     out_ref[...] = total.astype(out_ref.dtype)
 
 

time: 243 us -> 243 us (level)
  no operation moved by 1% of the time
where the time goes in v8:
time: 243 us; the launch traced here: 242 us
  waiting for transfers between devices  99.1 us (41%)
  Pallas kernels  59.3 us (24%)
  starting transfers between devices  40.2 us (17%)
  matrix products  32.7 us (13%)
  local copies, waits for them, and re-layouts  7.44 us (3%)
  other arithmetic  3.08 us (1%)
    all_to_all x4, waiting for transfers between devices, exchange(): return lax.all_to_all(rows, 'tm', split_axis=0, concat_axis=0, tiled=True)  84.7 us
    pallas_call x2, Pallas kernels, run_expert(): pl.pallas_call(functools.partial(expert_body, steps), grid=(row_total //...  33.4 us
    all_to_all x4, starting transfers between devices, exchange(): return lax.all_to_all(rows, 'tm', split_axis=0, concat_axis=0, tiled=True)  16.7 us
    pallas_call x1, Pallas kernels, attend(): pl.pallas_call(functools.partial(attend_body, kv_heads), out_shape=jax.Sh...  13.7 us
    dot_general x4, matrix products, embed(): rows = jnp.dot(pairs, conv_weight, preferred_element_type=jnp.float32)  12.6 us
    ppermute x3, starting transfers between devices, from_behind(): return lax.ppermute(block, axis, route)  11.4 us
    dot_general x2, matrix products, shards(): jnp.dot(context_in[local], w_out, preferred_element_type=jnp.float32)  10.4 us
    all_to_all x1, waiting for transfers between devices, shards(): lax.all_to_all(pairs_out.reshape(half, 2 * local_count * CAP, -1), 'tm',...  8.9 us
  transfers between devices with their start and end apart: 13, of which 8 were waited for; matrix products, arithmetic and copies ran while one was open for 16% of the time, Pallas kernels for 23%

profile of v8, /device:TPU:0, one launch (start us, length us, event | category | flops | bytes accessed | tf_op | source)
XLA Modules:
  0.0 242.3 jit_solution(17846720352667318786)
XLA Ops:
  0.0 5.1 %collective-permute-start.2 = (bf16[256,512]{1,0:T(8,128)(2,1)}, bf16[256,512]{1,0:T(8,128)(2,1)S(1)}, u32[]{:S(2)}, u32[]{:S(2)}) collective-permute-start(bf16[256,512]{1,0:T(8,128)(2,1)} %signal_ref.1), channel_id=1, source_target_pairs={{0,8},{1,9},{2,10},{3,11},{4,12},{5,13},{6,14},{7,15},{8,16},{9,17... | collective-permute-start | bytes 786440 | tf_op jit(solution)/shard_map/ppermute | solution.py:22
  5.8 2.6 %collective-permute-start.1 = (bf16[1,512]{1,0:T(2,128)(2,1)S(1)}, bf16[1,512]{1,0:T(2,128)(2,1)S(1)}, u32[]{:S(2)}, u32[]{:S(2)}) collective-permute-start(bf16[1,512]{1,0:T(2,128)(2,1)S(1)} %slice.26), channel_id=1, source_target_pairs={{0,9},{1,10},{2,11},{3,12},{4,13},{5,14},{6,15},{7,16},{8,17},{9,1... | collective-permute-start | bytes 3080 | tf_op jit(solution)/shard_map/ppermute | solution.py:22
  8.4 3.8 %collective-permute-start = (bf16[1,512]{1,0:T(2,128)(2,1)S(1)}, bf16[1,512]{1,0:T(2,128)(2,1)S(1)}, u32[]{:S(2)}, u32[]{:S(2)}) collective-permute-start(bf16[1,512]{1,0:T(2,128)(2,1)S(1)} %slice.26), channel_id=1, source_target_pairs={{0,1},{1,2},{2,3},{3,4},{4,5},{5,6},{6,7},{7,8},{8,9},{9,10},{10,1... | collective-permute-start | bytes 3080 | tf_op jit(solution)/shard_map/ppermute | solution.py:22
  13.1 3.8 %fusion.7 = (f32[256]{0:T(256)S(1)}, bf16[256,2048]{1,0:T(8,128)(2,1)S(1)}) fusion(bf16[1024,2048]{1,0:T(8,128)(2,1)} %param.14, bf16[256,512]{1,0:T(8,128)(2,1)} %signal_ref.1, bf16[255,512]{1,0:T(8,128)(2,1)} %bitcast.70, bf16[1,512]{1,0:T(2,128)(2,1)S(1)} %collective-permute-done.before_ref), kind=kOutput, calls=%fused_computation.20 | convolution fusion | flops 1077411584 | bytes 5768192 | tf_op jit(solution)/shard_map/dot_general | solution.py:397
  17.0 3.9 %collective-permute-start.7 = (bf16[272,512]{1,0:T(8,128)(2,1)S(1)}, bf16[272,512]{1,0:T(8,128)(2,1)S(1)}, u32[]{:S(2)}, u32[]{:S(2)}) collective-permute-start(bf16[272,512]{1,0:T(8,128)(2,1)S(1)} %fusion.38), channel_id=1, source_target_pairs={{0,16},{1,17},{2,18},{3,19},{4,20},{5,21},{6,22},{7,23},{8,24},{9,... | collective-permute-start | bytes 835592 | tf_op jit(solution)/shard_map/ppermute | solution.py:391
  27.0 2.3 collective-permute-start.5
  29.2 2.2 fusion.61.query_ref
  32.7 3.8 %shard_map.130 = bf16[1024,1024]{1,0:T(8,128)(2,1)} custom-call(s32[2]{0:T(128)S(1)} %pad_add_fusion.info_ref, bf16[256,512]{1,0:T(8,128)(2,1)S(1)} %copy-done.2, bf16[1,512]{1,0:T(2,128)(2,1)S(1)} %collective-permute-done.before_ref, s32[2,256]{1,0:T(2,128)S(1)} %bitcast.79, bf16[272,512]{1,0:T(8,128)(2,1)S(1)} %collective-permute-done.7.far_ref), custom_call_target="tpu_custom_call" | custom-call | flops 1073741824 | bytes 2621440 | tf_op jit(solution)/shard_map/pallas_call | solution.py:144
  36.6 1.7 collective-permute-done.4
  38.2 4.4 %all-to-all-start = ((bf16[16,64,1024]{2,1,0:T(8,128)(2,1)}), bf16[16,64,1024]{2,1,0:T(8,128)(2,1)}, u32[]{:S(2)}, u32[]{:S(2)}) async-start(bf16[16,64,1024]{2,1,0:T(8,128)(2,1)} %bitcast.19), calls=%async_computation | async-start | bytes 4194304 | tf_op jit(solution)/shard_map/all_to_all | solution.py:419
  44.2 2.5 %collective-permute-done.6.refs_5_ = bf16[4,256,512]{2,1,0:T(8,128)(2,1)S(1)} collective-permute-done((bf16[4,256,512]{2,1,0:T(8,128)(2,1)}, bf16[4,256,512]{2,1,0:T(8,128)(2,1)S(1)}, u32[]{:S(2)}, u32[]{:S(2)}) %collective-permute-start.6) | collective-permute-done | bytes 1048608 | tf_op jit(solution)/shard_map/ppermute | solution.py:332
  47.9 13.7 %shard_map.129 = bf16[256,1024]{1,0:T(8,128)(2,1)S(1)} custom-call(s32[9]{0:T(128)S(1)} %convert_element_type.68.flag_ref, f32[8]{0:T(128)S(1)} %copy-done.4, f32[256,1024]{1,0:T(8,128)S(1)} %copy-done.5, bf16[1,256,512]{2,1,0:T(8,128)(2,1)S(1)} %bitcast.68, bf16[1,256,512]{2,1,0:T(8,128)(2,1)S(1)} %bitcast.69, bf16[1,256,512]{2,1,0:T(8,128)(2,1)S(1)} %bitcast.72, ...), custom_call_target="tpu_custom_call" | custom-call | flops 3623878656 | bytes 3932160 | tf_op jit(solution)/shard_map/pallas_call | solution.py:298
  63.1 8.9 %all-to-all-done = bf16[16,64,1024]{2,1,0:T(8,128)(2,1)} async-done(((bf16[16,64,1024]{2,1,0:T(8,128)(2,1)}), bf16[16,64,1024]{2,1,0:T(8,128)(2,1)}, u32[]{:S(2)}, u32[]{:S(2)}) %all-to-all-start) | async-done | bytes 2097184 | tf_op jit(solution)/shard_map/all_to_all | solution.py:419
  71.9 5.0 %all-to-all-start.2 = ((bf16[32,16,1024]{2,1,0:T(8,128)(2,1)}), bf16[32,16,1024]{2,1,0:T(8,128)(2,1)S(1)}, u32[]{:S(2)}, u32[]{:S(2)}) async-start(bf16[32,16,1024]{2,1,0:T(8,128)(2,1)} %bitcast.30), calls=%async_computation.2 | async-start | bytes 2097152 | tf_op jit(solution)/shard_map/all_to_all | solution.py:378
  78.5 1.7 slice_bitcast_fusion
  80.5 2.0 copy-done.12
  82.4 3.7 %convolution_convert_fusion.1 = bf16[512,2048]{1,0:T(8,128)(2,1)} fusion(bf16[512,1024]{1,0:T(8,128)(2,1)S(1)} %bitcast.82, bf16[1024,2048]{1,0:T(8,128)(2,1)S(1)} %copy-done.12), kind=kOutput, calls=%fused_computation.6 | convolution fusion | flops 2148532224 | bytes 7340032 | tf_op jit(solution)/shard_map/dot_general | solution.py:397
  86.1 3.7 %convolution_convert_fusion = bf16[512,2048]{1,0:T(8,128)(2,1)} fusion(bf16[512,1024]{1,0:T(8,128)(2,1)S(1)} %bitcast.83, bf16[1024,2048]{1,0:T(8,128)(2,1)S(1)} %copy-done.12), kind=kOutput, calls=%fused_computation.5 | convolution fusion | flops 2148532224 | bytes 7340032 | tf_op jit(solution)/shard_map/dot_general | solution.py:397
  89.8 13.2 %all-to-all-done.2 = bf16[32,16,1024]{2,1,0:T(8,128)(2,1)S(1)} async-done(((bf16[32,16,1024]{2,1,0:T(8,128)(2,1)}), bf16[32,16,1024]{2,1,0:T(8,128)(2,1)S(1)}, u32[]{:S(2)}, u32[]{:S(2)}) %all-to-all-start.2) | async-done | bytes 1048608 | tf_op jit(solution)/shard_map/all_to_all | solution.py:378
  103.0 3.6 %all-to-all-start.1 = ((bf16[32,16,1024]{2,1,0:T(8,128)(2,1)}), bf16[32,16,1024]{2,1,0:T(8,128)(2,1)S(1)}, u32[]{:S(2)}, u32[]{:S(2)}) async-start(bf16[32,16,1024]{2,1,0:T(8,128)(2,1)} %bitcast.27), calls=%async_computation.1 | async-start | bytes 2097152 | tf_op jit(solution)/shard_map/all_to_all | solution.py:378
  106.7 5.2 %add_convert_fusion.mid_ref = bf16[512,2048]{1,0:T(8,128)(2,1)S(1)} fusion(bf16[512,2048]{1,0:T(8,128)(2,1)} %convolution_convert_fusion.1, bf16[512,1024]{1,0:T(8,128)(2,1)S(1)} %bitcast.81, bf16[1024,2048]{1,0:T(8,128)(2,1)} %param.18), kind=kOutput, calls=%fused_computation | convolution fusion | flops 2150629376 | bytes 9437184 | tf_op jit(solution)/shard_map/dot_general | solution.py:455
  111.9 16.7 %shard_map.132 = bf16[512,2048]{1,0:T(8,128)(2,1)} custom-call(bf16[512,2048]{1,0:T(8,128)(2,1)S(1)} %add_convert_fusion.mid_ref, f32[1,2048]{1,0:T(1,128)S(1)} %bitcast.77, bf16[2,2816,2048]{2,1,0:T(8,128)(2,1)} %w_in_ref.3, bf16[2816,2048]{1,0:T(8,128)(2,1)} %w_out_ref.3), custom_call_target="tpu_custom_call" | custom-call | flops 8858370048 | bytes 21495808 | tf_op jit(solution)/shard_map/pallas_call | solution.py:71
  128.6 4.3 %all-to-all-done.1 = bf16[32,16,1024]{2,1,0:T(8,128)(2,1)S(1)} async-done(((bf16[32,16,1024]{2,1,0:T(8,128)(2,1)}), bf16[32,16,1024]{2,1,0:T(8,128)(2,1)S(1)}, u32[]{:S(2)}, u32[]{:S(2)}) %all-to-all-start.1) | async-done | bytes 1048608 | tf_op jit(solution)/shard_map/all_to_all | solution.py:378
  132.9 4.0 %all-to-all-start.3 = ((bf16[32,16,2048]{2,1,0:T(8,128)(2,1)}), bf16[32,16,2048]{2,1,0:T(8,128)(2,1)}, u32[]{:S(2)}, u32[]{:S(2)}) async-start(bf16[32,16,2048]{2,1,0:T(8,128)(2,1)} %bitcast.32), calls=%async_computation.3 | async-start | bytes 4194304 | tf_op jit(solution)/shard_map/all_to_all | solution.py:378
  136.9 3.9 %fusion.4 = (f32[256]{0:T(256)S(1)}, bf16[256,2048]{1,0:T(8,128)(2,1)S(1)}) fusion(bf16[256,1024]{1,0:T(8,128)(2,1)S(1)} %shard_map.129, bf16[1024,2048]{1,0:T(8,128)(2,1)} %param.18, bf16[256,2048]{1,0:T(8,128)(2,1)} %copy-done.6), kind=kOutput, calls=%fused_computation.17 | convolution fusion | flops 1076887296 | bytes 6816768 | tf_op jit(solution)/shard_map/dot_general | solution.py:443
  141.7 5.2 %add_convert_fusion.1.mid_ref = bf16[512,2048]{1,0:T(8,128)(2,1)S(1)} fusion(bf16[512,2048]{1,0:T(8,128)(2,1)} %convolution_convert_fusion, bf16[512,1024]{1,0:T(8,128)(2,1)S(1)} %bitcast.80, bf16[1024,2048]{1,0:T(8,128)(2,1)} %param.18), kind=kOutput, calls=%fused_computation.1 | convolution fusion | flops 2150629376 | bytes 9437184 | tf_op jit(solution)/shard_map/dot_general | solution.py:455
  147.0 16.7 %shard_map.131 = bf16[512,2048]{1,0:T(8,128)(2,1)} custom-call(bf16[512,2048]{1,0:T(8,128)(2,1)S(1)} %add_convert_fusion.1.mid_ref, f32[1,2048]{1,0:T(1,128)S(1)} %bitcast.78, bf16[2,2816,2048]{2,1,0:T(8,128)(2,1)} %w_in_ref.3, bf16[2816,2048]{1,0:T(8,128)(2,1)} %w_out_ref.3), custom_call_target="tpu_custom_call" | custom-call | flops 8858370048 | bytes 21495808 | tf_op jit(solution)/shard_map/pallas_call | solution.py:71
  163.7 21.9 %all-to-all-done.3 = bf16[32,16,2048]{2,1,0:T(8,128)(2,1)} async-done(((bf16[32,16,2048]{2,1,0:T(8,128)(2,1)}), bf16[32,16,2048]{2,1,0:T(8,128)(2,1)}, u32[]{:S(2)}, u32[]{:S(2)}) %all-to-all-start.3) | async-done | bytes 2097184 | tf_op jit(solution)/shard_map/all_to_all | solution.py:378
  185.6 4.1 %all-to-all-start.4 = ((bf16[32,16,2048]{2,1,0:T(8,128)(2,1)}), bf16[32,16,2048]{2,1,0:T(8,128)(2,1)}, u32[]{:S(2)}, u32[]{:S(2)}) async-start(bf16[32,16,2048]{2,1,0:T(8,128)(2,1)} %bitcast.34), calls=%async_computation.4 | async-start | bytes 4194304 | tf_op jit(solution)/shard_map/all_to_all | solution.py:378
  190.1 3.1 %shard_map.133.base_ref = f32[256,2048]{1,0:T(8,128)S(1)} custom-call(f32[256,2048]{1,0:T(8,128)S(1)} %convert_element_type.85.base_ref, f32[256,2]{1,0:T(8,128)S(1)} %broadcast_divide_fusion.weight_ref, s32[256,2]{1,0:T(8,128)S(1)} %copy.56.key_ref, s32[1,512]{1,0:T(1,128)S(1)} %multiply_add_fusion.1.row_ref, bf16[512,2048]{1,0:T(8,128)(2,1)} %bitcast.33.rows_ref), custom_call_target="tpu_custom_call" | custom-call | flops 1073741824 | bytes 6291456 | tf_op jit(solution)/shard_map/pallas_call | solution.py:187
  193.2 45.3 %all-to-all-done.4 = bf16[32,16,2048]{2,1,0:T(8,128)(2,1)} async-done(((bf16[32,16,2048]{2,1,0:T(8,128)(2,1)}), bf16[32,16,2048]{2,1,0:T(8,128)(2,1)}, u32[]{:S(2)}, u32[]{:S(2)}) %all-to-all-start.4) | async-done | bytes 2097184 | tf_op jit(solution)/shard_map/all_to_all | solution.py:378
  238.5 3.7 %shard_map.134 = bf16[256,2048]{1,0:T(8,128)(2,1)} custom-call(f32[256,2048]{1,0:T(8,128)S(1)} %shard_map.133.base_ref, f32[256,2]{1,0:T(8,128)S(1)} %broadcast_divide_fusion.weight_ref, s32[256,2]{1,0:T(8,128)S(1)} %copy.56.key_ref, s32[1,512]{1,0:T(1,128)S(1)} %multiply_add_fusion.row_ref, bf16[512,2048]{1,0:T(8,128)(2,1)} %bitcast.35.rows_ref), custom_call_target="tpu_custom_call" | custom-call | flops 1073741824 | bytes 6291456 | tf_op jit(solution)/shard_map/pallas_call | solution.py:187
  (67 shorter events, 16.1 us)
Async XLA Ops:
  0.0 140.8 %copy-start = (bf16[2048,64]{0,1:T(8,128)(2,1)S(1)}, bf16[2048,64]{0,1:T(8,128)(2,1)}, u32[]{:S(2)}) copy-start(bf16[2048,64]{0,1:T(8,128)(2,1)} %param.21) | copy-start | bytes 786436
  0.0 21.0 %collective-permute-start.2 = (bf16[256,512]{1,0:T(8,128)(2,1)}, bf16[256,512]{1,0:T(8,128)(2,1)S(1)}, u32[]{:S(2)}, u32[]{:S(2)}) collective-permute-start(bf16[256,512]{1,0:T(8,128)(2,1)} %signal_ref.1), channel_id=1, source_target_pairs={{0,8},{1,9},{2,10},{3,11},{4,12},{5,13},{6,14},{7,15},{8,16},{9,17... | collective-permute-start | bytes 786440 | tf_op jit(solution)/shard_map/ppermute | solution.py:22
  5.8 15.1 %collective-permute-start.1 = (bf16[1,512]{1,0:T(2,128)(2,1)S(1)}, bf16[1,512]{1,0:T(2,128)(2,1)S(1)}, u32[]{:S(2)}, u32[]{:S(2)}) collective-permute-start(bf16[1,512]{1,0:T(2,128)(2,1)S(1)} %slice.26), channel_id=1, source_target_pairs={{0,9},{1,10},{2,11},{3,12},{4,13},{5,14},{6,15},{7,16},{8,17},{9,1... | collective-permute-start | bytes 3080 | tf_op jit(solution)/shard_map/ppermute | solution.py:22
  8.4 4.7 %collective-permute-start = (bf16[1,512]{1,0:T(2,128)(2,1)S(1)}, bf16[1,512]{1,0:T(2,128)(2,1)S(1)}, u32[]{:S(2)}, u32[]{:S(2)}) collective-permute-start(bf16[1,512]{1,0:T(2,128)(2,1)S(1)} %slice.26), channel_id=1, source_target_pairs={{0,1},{1,2},{2,3},{3,4},{4,5},{5,6},{6,7},{7,8},{8,9},{9,10},{10,1... | collective-permute-start | bytes 3080 | tf_op jit(solution)/shard_map/ppermute | solution.py:22
  13.1 3.9 %copy-start.2 = (bf16[256,512]{1,0:T(8,128)(2,1)S(1)}, bf16[256,512]{1,0:T(8,128)(2,1)}, u32[]{:S(2)}) copy-start(bf16[256,512]{1,0:T(8,128)(2,1)} %signal_ref.1) | copy-start | bytes 786436
  13.1 7.8 %copy-start.11 = (bf16[1024,2048]{1,0:T(8,128)(2,1)S(1)}, bf16[1024,2048]{1,0:T(8,128)(2,1)}, u32[]{:S(2)}) copy-start(bf16[1024,2048]{1,0:T(8,128)(2,1)} %param.14) | copy-start | bytes 12582916
  17.0 6.0 %copy-start.6 = (bf16[256,2048]{1,0:T(8,128)(2,1)}, bf16[256,2048]{1,0:T(8,128)(2,1)S(1)}, u32[]{:S(2)}) copy-start(bf16[256,2048]{1,0:T(8,128)(2,1)S(1)} %get-tuple-element.43) | copy-start | bytes 3145732
  17.0 15.7 %collective-permute-start.7 = (bf16[272,512]{1,0:T(8,128)(2,1)S(1)}, bf16[272,512]{1,0:T(8,128)(2,1)S(1)}, u32[]{:S(2)}, u32[]{:S(2)}) collective-permute-start(bf16[272,512]{1,0:T(8,128)(2,1)S(1)} %fusion.38), channel_id=1, source_target_pairs={{0,16},{1,17},{2,18},{3,19},{4,20},{5,21},{6,22},{7,23},{8,24},{9,... | collective-permute-start | bytes 835592 | tf_op jit(solution)/shard_map/ppermute | solution.py:391
  21.0 1.4 copy-start.8
  22.4 1.6 copy-start.1
  24.8 4.5 %copy-start.10 = (bf16[2048,1024]{1,0:T(8,128)(2,1)S(1)}, bf16[2048,1024]{1,0:T(8,128)(2,1)}, u32[]{:S(2)}) copy-start(bf16[2048,1024]{1,0:T(8,128)(2,1)} %param.16) | copy-start | bytes 12582916
  25.7 10.9 %collective-permute-start.3 = (bf16[256,512]{1,0:T(8,128)(2,1)S(1)}, bf16[256,512]{1,0:T(8,128)(2,1)S(1)}, u32[]{:S(2)}, u32[]{:S(2)}) collective-permute-start(bf16[256,512]{1,0:T(8,128)(2,1)S(1)} %get-tuple-element.32), channel_id=1, source_target_pairs={{0,2},{1,3},{2,0},{3,1},{4,6},{5,7},{6,4},{7,5},{8,10},{9,11},{10,... | collective-permute-start | bytes 786440 | tf_op jit(solution)/shard_map/ppermute | solution.py:328
  25.7 12.5 %collective-permute-start.4 = (bf16[256,512]{1,0:T(8,128)(2,1)S(1)}, bf16[256,512]{1,0:T(8,128)(2,1)S(1)}, u32[]{:S(2)}, u32[]{:S(2)}) collective-permute-start(bf16[256,512]{1,0:T(8,128)(2,1)S(1)} %get-tuple-element.31), channel_id=1, source_target_pairs={{0,4},{1,5},{2,6},{3,7},{4,0},{5,1},{6,2},{7,3},{8,12},{9,13},{10,... | collective-permute-start | bytes 786440 | tf_op jit(solution)/shard_map/ppermute | solution.py:328
  27.0 11.3 %collective-permute-start.5 = (bf16[256,512]{1,0:T(8,128)(2,1)S(1)}, bf16[256,512]{1,0:T(8,128)(2,1)S(1)}, u32[]{:S(2)}, u32[]{:S(2)}) collective-permute-start(bf16[256,512]{1,0:T(8,128)(2,1)S(1)} %get-tuple-element.30), channel_id=1, source_target_pairs={{0,6},{1,7},{2,4},{3,5},{4,2},{5,3},{6,0},{7,1},{8,14},{9,15},{10,... | collective-permute-start | bytes 786440 | tf_op jit(solution)/shard_map/ppermute | solution.py:328
  38.2 33.7 %all-to-all-start = ((bf16[16,64,1024]{2,1,0:T(8,128)(2,1)}), bf16[16,64,1024]{2,1,0:T(8,128)(2,1)}, u32[]{:S(2)}, u32[]{:S(2)}) async-start(bf16[16,64,1024]{2,1,0:T(8,128)(2,1)} %bitcast.19), calls=%async_computation | async-start | bytes 4194304 | tf_op jit(solution)/shard_map/all_to_all | solution.py:419
  42.7 4.0 %copy-start.4 = (f32[8]{0:T(128)S(1)}, f32[8]{0:T(128)}, u32[]{:S(2)}) copy-start(f32[8]{0:T(128)} %scale_ref.1) | copy-start | bytes 100
  43.8 2.9 %collective-permute-start.6 = (bf16[4,256,512]{2,1,0:T(8,128)(2,1)}, bf16[4,256,512]{2,1,0:T(8,128)(2,1)S(1)}, u32[]{:S(2)}, u32[]{:S(2)}) collective-permute-start(bf16[4,256,512]{2,1,0:T(8,128)(2,1)} %pad_maximum_fusion), channel_id=1, source_target_pairs={{0,1},{1,0},{2,3},{3,2},{4,5},{5,4},{6,7},{7,6},{8,9},{9,8},{10,11... | collective-permute-start | bytes 3145736 | tf_op jit(solution)/shard_map/ppermute | solution.py:332
  46.7 1.2 copy-start.5
  71.9 31.1 %all-to-all-start.2 = ((bf16[32,16,1024]{2,1,0:T(8,128)(2,1)}), bf16[32,16,1024]{2,1,0:T(8,128)(2,1)S(1)}, u32[]{:S(2)}, u32[]{:S(2)}) async-start(bf16[32,16,1024]{2,1,0:T(8,128)(2,1)} %bitcast.30), calls=%async_computation.2 | async-start | bytes 2097152 | tf_op jit(solution)/shard_map/all_to_all | solution.py:378
  80.2 2.2 copy-start.12
  103.0 29.9 %all-to-all-start.1 = ((bf16[32,16,1024]{2,1,0:T(8,128)(2,1)}), bf16[32,16,1024]{2,1,0:T(8,128)(2,1)S(1)}, u32[]{:S(2)}, u32[]{:S(2)}) async-start(bf16[32,16,1024]{2,1,0:T(8,128)(2,1)} %bitcast.27), calls=%async_computation.1 | async-start | bytes 2097152 | tf_op jit(solution)/shard_map/all_to_all | solution.py:378
  106.7 5.2 %copy-start.3 = (f32[2048]{0:T(1024)S(1)}, f32[2048]{0:T(1024)}, u32[]{:S(2)}) copy-start(f32[2048]{0:T(1024)} %param.20) | copy-start | bytes 24580
  132.9 52.7 %all-to-all-start.3 = ((bf16[32,16,2048]{2,1,0:T(8,128)(2,1)}), bf16[32,16,2048]{2,1,0:T(8,128)(2,1)}, u32[]{:S(2)}, u32[]{:S(2)}) async-start(bf16[32,16,2048]{2,1,0:T(8,128)(2,1)} %bitcast.32), calls=%async_computation.3 | async-start | bytes 4194304 | tf_op jit(solution)/shard_map/all_to_all | solution.py:378
  140.8 0.7 copy-start.7
  185.6 4.1 %copy-start.9 = (s32[256,2]{0,1:T(2,128)S(1)}, s32[256,2]{0,1:T(2,128)}, u32[]{:S(2)}) copy-start(s32[256,2]{0,1:T(2,128)} %param.25) | copy-start | bytes 6148
  185.6 52.9 %all-to-all-start.4 = ((bf16[32,16,2048]{2,1,0:T(8,128)(2,1)}), bf16[32,16,2048]{2,1,0:T(8,128)(2,1)}, u32[]{:S(2)}, u32[]{:S(2)}) async-start(bf16[32,16,2048]{2,1,0:T(8,128)(2,1)} %bitcast.34), calls=%async_computation.4 | async-start | bytes 4194304 | tf_op jit(solution)/shard_map/all_to_all | solution.py:378
